TPU v7x, 128 devices: a whole 4x4x4 slice. The times are simulated.
128 devices in a mesh: section: 8 (over y, core), row: 16 (over x, z).
Axes of the slice: x: 4, y: 4, z: 4, core: 2. Of those that a mesh axis runs over, the one named last changes fastest.
Arguments:
- coupling: bfloat16 [2048, 128, 128], P(('section', 'row')), may hold values from -4 to 4
- diag_inverse: float32 [2048, 128, 128], P(('section', 'row')), may hold values from -0.046875 to 0.046875
- pivot_inverse: bfloat16 [512, 128, 128], P(('section', 'row')), may hold values from -0.5 to 0.5
- cross_left: bfloat16 [16384, 128, 128], P(('section', 'row')), may hold values from -0.5 to 0.5
- cross_right: bfloat16 [16384, 128, 128], P(('section', 'row')), may hold values from -4 to 4
- cross_pivot: int32 [16384], P(('section', 'row')), may hold values from 0 to 3
- cross_owner: int32 [16384, 1], P(('section', 'row')), may hold values from 0 to 15; in each aligned block of 128 rows (0 to 127, 128 to 255, ...) at most 16 rows name the same one
- foreign_target_row: int32 [16384], P(('section', 'row')), may hold values from 0 to 15
- cross_count: int32 [128], P(('section', 'row')), may hold values from 1 to 128, 12288 in all
- local_left: bfloat16 [16384, 128, 128], P(('section', 'row')), may hold values from -0.5 to 0.5
- local_right: bfloat16 [16384, 128, 128], P(('section', 'row')), may hold values from -4 to 4
- local_pivot: int32 [16384], P(('section', 'row')), may hold values from 0 to 3
- local_target: int32 [16384], P(('section', 'row')), may hold values from 0 to 15
- adjoint_seed: float32 [2048, 128, 128], P(('section', 'row')), may hold values from -48 to 48
Outputs:
- coupling_new: float32 [2048, 128, 128], P(('section', 'row'))
- adjoint: float32 [2048, 128, 128], P(('section', 'row'))
Inputs may be any that keep to these rules, and one draw needn't show every extreme that they name: `cross_owner`: among the 128 cross slots of one device, live or not, at most 16 name the same owner, a bound that some block reaches of them. `cross_count`: some device has all its cross slots live.
All inputs are finite; a program needn't handle non-finite values.
Results may differ from a plain program's by a relative error of at most 0.0089.
Values may be sent and summed in bfloat16 or wider, within the bound.
No kernel may reach another device: no remote copies, remote signals or barrier semaphores. Data moves between devices by JAX's collectives and lax.ppermute only.
A program may use at most 192 MiB of HBM per device.

v0:
```python
import jax
import jax.numpy as jnp
from jax import lax
from jax.sharding import PartitionSpec as P

CAP = 16


precise = lax.Precision.HIGHEST


def shifted(x, axis, by):
    size = lax.axis_size(axis)
    pairs = [(i, i + by) for i in range(size) if 0 <= i + by < size]
    return lax.ppermute(x, axis, pairs)


def pivot_products(lower_factor_blocks, pivots, pivot_inverse):
    selected_entry = jnp.take(pivot_inverse, pivots, axis=0)
    return jnp.einsum(
        "zmq,zqy->zmy", lower_factor_blocks, selected_entry, preferred_element_type=jnp.float32
    ).astype(jnp.bfloat16)


def finish_products(rescaled_blocks, upper_factor_blocks):
    return jnp.einsum(
        "zmq,zqy->zmy", rescaled_blocks, upper_factor_blocks, preferred_element_type=jnp.float32
    ).astype(jnp.bfloat16)


def add_into_rows(blocks, targets, row_count):
    picks = (targets[None, :] == jnp.arange(row_count, dtype=jnp.float32)[:, None]).astype(
        jnp.bfloat16
    )
    return jnp.einsum("ks,sab->kab", picks, blocks, preferred_element_type=jnp.float32)


def apply_map(matrix, vector):
    return jnp.einsum("kab,knb->kna", matrix, vector, precision=precise)


def per_device(
    coupling,
    diag_inverse,
    pivot_inverse,
    cross_left,
    cross_right,
    cross_pivot,
    cross_owner,
    foreign_target_row,
    cross_count,
    local_left,
    local_right,
    local_pivot,
    local_target,
    adjoint_seed,
):
    row_count = coupling.shape[0]
    width = coupling.shape[1]
    groups = lax.axis_size("row")
    slots = cross_left.shape[0]
    capacity = CAP
    slot_index = jnp.arange(slots, dtype=jnp.int32)
    local_scaled = pivot_products(local_left, local_pivot, pivot_inverse)
    local_blocks = finish_products(local_scaled, local_right)
    local_sum = add_into_rows(local_blocks, local_target.astype(jnp.float32), row_count)
    owner = cross_owner[:, 0]
    earlier = (owner[None, :] == owner[:, None]) & (slot_index[None, :] < slot_index[:, None])
    position = owner * capacity + jnp.sum(earlier.astype(jnp.int32), axis=1)
    buffer_index = jnp.arange(groups * capacity, dtype=jnp.int32)
    matches = position[None, :] == buffer_index[:, None]
    filled = jnp.any(matches, axis=1)
    source = jnp.sum(jnp.where(matches, slot_index[None, :], 0), axis=1)
    live_target = jnp.where(slot_index < cross_count[0], foreign_target_row, -1)
    sent_target = (
        jnp.where(filled, jnp.take(live_target, source), -1)
        .astype(jnp.bfloat16)
        .reshape(groups, capacity)
    )
    cross_scaled = pivot_products(cross_left, cross_pivot, pivot_inverse)
    cross_blocks = finish_products(cross_scaled, cross_right)
    sent_blocks = jnp.take(cross_blocks, source, axis=0).reshape(groups, capacity, width, width)
    arrived, arrived_target = (
        lax.all_to_all(sent_blocks, "row", split_axis=0, concat_axis=0, tiled=True),
        lax.all_to_all(sent_target, "row", split_axis=0, concat_axis=0, tiled=True),
    )
    remote_sum = add_into_rows(
        arrived.reshape(groups * capacity, width, width),
        arrived_target.reshape(groups * capacity).astype(jnp.float32),
        row_count,
    )
    updated = coupling.astype(jnp.float32) - local_sum - remote_sum
    step_matrix = -jnp.einsum("kab,kbc->kac", diag_inverse, updated, precision=precise)
    step_offset = jnp.einsum("kab,knb->kna", diag_inverse, adjoint_seed, precision=precise)

    def advance(counter, current):
        after = shifted(current, "section", -1)
        return step_offset + apply_map(step_matrix, after)

    adjoint = lax.fori_loop(0, lax.axis_size("section") - 1, advance, step_offset)
    return (updated, adjoint)


def solution(mesh):
    return jax.shard_map(
        per_device,
        mesh=mesh,
        in_specs=(
            P(("section", "row"), None, None),
            P(("section", "row"), None, None),
            P(("section", "row"), None, None),
            P(("section", "row"), None, None),
            P(("section", "row"), None, None),
            P(("section", "row")),
            P(("section", "row"), None),
            P(("section", "row")),
            P(("section", "row")),
            P(("section", "row"), None, None),
            P(("section", "row"), None, None),
            P(("section", "row")),
            P(("section", "row")),
            P(("section", "row"), None, None),
        ),
        out_specs=(P(("section", "row"), None, None), P(("section", "row"), None, None)),
        check_vma=False,
    )
```

profile of v0, /device:TPU:1, one launch (start us, length us, event | category | flops | bytes accessed | tf_op | source)
XLA Modules:
  0.0 365.9 jit_solution(14801473776317432012)
XLA Ops:
  0.6 0.9 convert_reduce_fusion
  1.6 0.7 multiply_add_fusion
  2.4 0.1 fusion.38
  3.2 0.7 compare_select_fusion.5
  3.9 1.9 gather_fusion
  6.0 0.6 copy.41
  6.6 8.4 %all-to-all-start = ((bf16[16,1,16]{2,1,0:T(2,128)(2,1)}), bf16[16,1,16]{2,1,0:T(2,128)(2,1)S(1)}, u32[]{:S(2)}, u32[]{:S(2)}) async-start(bf16[16,1,16]{2,1,0:T(2,128)(2,1)} %copy.41), calls=%async_computation | async-start | bytes 16384 | tf_op jit(solution)/shard_map/all_to_all | solution.py:85
  15.0 0.7 compare_select_fusion.3
  15.7 0.7 compare_and_fusion.1
  16.4 3.9 %gather_fusion.3 = bf16[128,128,128]{2,1,0:T(8,128)(2,1)} fusion(bf16[4,128,128]{2,1,0:T(8,128)(2,1)} %param.20, s32[1024]{0:T(1024)S(1)} %pad_clamp_fusion), kind=kCustom, calls=%fused_computation.1.clone | custom fusion | bytes 8389120 | tf_op jit(solution)/shard_map/jit(_take)/gather | solution.py:19
  20.3 10.8 %fusion.25 = bf16[128,128,128]{2,1,0:T(8,128)(2,1)} fusion(bf16[128,128,128]{2,1,0:T(8,128)(2,1)} %param.22, bf16[128,128,128]{2,1,0:T(8,128)(2,1)} %param.21, bf16[128,128,128]{2,1,0:T(8,128)(2,1)} %gather_fusion.3, pred[128]{0:T(512)(128)(4,1)S(1)} %compare_and_fusion.1), kind=kOutput, calls=%fused_computation.19 | convolution fusion | flops 1080033280 | bytes 16777344 | tf_op jit(solution)/shard_map/zmq,zqy->zmy/dot_general | solution.py:26
  31.1 10.7 %gather_fusion.1 = bf16[256,128,128]{2,1,0:T(8,128)(2,1)} fusion(bf16[128,128,128]{2,1,0:T(8,128)(2,1)} %fusion.25, s32[1024]{0:T(1024)S(1)} %pad_clamp_fusion.1), kind=kCustom, calls=%fused_computation.3 | custom fusion | bytes 16778240 | tf_op jit(solution)/shard_map/jit(_take)/gather | solution.py:82
  41.8 7.4 %broadcast_select_fusion = bf16[16,16,128,128]{3,2,1,0:T(8,128)(2,1)} fusion(bf16[16,16,128,128]{3,2,1,0:T(8,128)(2,1)} %bitcast.31, pred[16,16]{1,0:T(8,128)(4,1)S(1)} %compare_and_fusion), kind=kLoop, calls=%fused_computation.5 | loop fusion | flops 4194304 | bytes 16777472 | tf_op jit(solution)/shard_map/jit(_take)/select_n | solution.py:82
  49.2 7.0 %all-to-all-start.1 = ((bf16[16,16,128,128]{3,2,1,0:T(8,128)(2,1)}), bf16[16,16,128,128]{3,2,1,0:T(8,128)(2,1)}, u32[]{:S(2)}, u32[]{:S(2)}) async-start(bf16[16,16,128,128]{3,2,1,0:T(8,128)(2,1)} %broadcast_select_fusion), calls=%async_computation.1 | async-start | bytes 16777216 | tf_op jit(solution)/shard_map/all_to_all | solution.py:84
  56.3 3.0 gather_fusion.2
  59.4 2.3 fusion.50
  61.6 1.0 copy.58
  62.6 10.8 %fusion.20 = bf16[128,128,128]{2,1,0:T(8,128)(2,1)} fusion(bf16[128,128,128]{2,1,0:T(8,128)(2,1)} %param.28, bf16[128,128,128]{2,1,0:T(8,128)(2,1)} %param.27, bf16[128,128,128]{2,1,0:T(8,128)(2,1)} %gather_fusion.2, pred[128]{0:T(512)(128)(4,1)S(1)} %compare_and_fusion.2), kind=kOutput, calls=%fused_computation.18 | convolution fusion | flops 1080033280 | bytes 16777344 | tf_op jit(solution)/shard_map/zmq,zqy->zmy/dot_general | solution.py:26
  73.4 4.8 %fusion.34 = f32[16,128,128]{2,0,1:T(8,128)S(1)} fusion(bf16[128,128,128]{2,1,0:T(8,128)(2,1)} %fusion.20, bf16[16,128,128]{2,1,0:T(8,128)(2,1)} %param.18, f32[128]{0:T(128)S(1)} %convert_element_type.47), kind=kOutput, calls=%fused_computation.23 | convolution fusion | flops 67635200 | bytes 5767680 | tf_op jit(solution)/shard_map/ks,sab->kab/dot_general | solution.py:35
  78.3 115.9 %all-to-all-done.1 = bf16[16,16,128,128]{3,2,1,0:T(8,128)(2,1)} async-done(((bf16[16,16,128,128]{3,2,1,0:T(8,128)(2,1)}), bf16[16,16,128,128]{3,2,1,0:T(8,128)(2,1)}, u32[]{:S(2)}, u32[]{:S(2)}) %all-to-all-start.1) | async-done | bytes 8388640 | tf_op jit(solution)/shard_map/all_to_all | solution.py:84
  194.2 12.2 %copy.44 = bf16[16,16,128,128]{3,1,0,2:T(8,128)(2,1)} copy(bf16[16,16,128,128]{3,2,1,0:T(8,128)(2,1)} %all-to-all-done.1) | data formatting | bytes 16777216 | tf_op jit(solution)/shard_map/all_to_all | solution.py:84
  206.4 4.6 %convolution_subtract_fusion = f32[16,128,128]{2,0,1:T(8,128)S(1)} fusion(f32[16,128,128]{2,0,1:T(8,128)S(1)} %fusion.34, bf16[256,128,128]{2,0,1:T(8,128)(2,1)} %bitcast.32, f32[256]{0:T(256)S(1)} %reshape.120), kind=kOutput, calls=%fused_computation.22 | convolution fusion | flops 134483968 | bytes 10486784 | tf_op jit(solution)/shard_map/ks,sab->kab/dot_general | solution.py:35
  211.0 0.3 copy.47
  211.3 1.0 copy-done.2
  212.3 2.8 fusion.37
  215.1 1.6 copy.46
  216.7 149.2 %while.10 = (s32[]{:T(128)}, f32[16,128,128]{2,1,0:T(8,128)}, f32[16,128,128]{2,1,0:T(8,128)S(1)}, f32[16,128,128]{2,1,0:T(8,128)S(1)}, s32[]{:T(128)}) while((s32[]{:T(128)}, f32[16,128,128]{2,1,0:T(8,128)}, f32[16,128,128]{2,1,0:T(8,128)S(1)}, f32[16,128,128]{2,1,0:T(8,128)S(1)}, s32[]{:T(128)}) %tuple.31), condition=%wide.region_4.6_spmd, body=%wide.region_3.5_spmd.sunk | while | flops 402915328 | bytes 8388709 | solution.py:100
  216.7 5.5 %collective-permute-start = (f32[16,128,128]{2,1,0:T(8,128)}, f32[16,128,128]{2,1,0:T(8,128)}, u32[]{:S(2)}, u32[]{:S(2)}) collective-permute-start(f32[16,128,128]{2,1,0:T(8,128)} %get-tuple-element.89), channel_id=1, source_target_pairs={{16,0},{32,16},{48,32},{64,48},{80,64},{96,80},{112,96},{17,1},{33... | collective-permute-start | bytes 3145736 | tf_op jit(solution)/shard_map/while/body/eval_jaxpr/ppermute | solution.py:15
  222.2 13.8 %collective-permute-done = f32[16,128,128]{2,1,0:T(8,128)} collective-permute-done((f32[16,128,128]{2,1,0:T(8,128)}, f32[16,128,128]{2,1,0:T(8,128)}, u32[]{:S(2)}, u32[]{:S(2)}) %collective-permute-start) | collective-permute-done | bytes 1048608 | tf_op jit(solution)/shard_map/while/body/eval_jaxpr/ppermute | solution.py:15
  236.0 4.5 %convolution_add_fusion.2 = f32[16,128,128]{2,1,0:T(8,128)} fusion(f32[16,128,128]{2,1,0:T(8,128)S(1)} %get-tuple-element.96, f32[16,128,128]{2,1,0:T(8,128)} %collective-permute-done, f32[16,128,128]{2,1,0:T(8,128)S(1)} %get-tuple-element.95), kind=kOutput, calls=%fused_computation.4.clone.1 | convolution fusion | flops 402915328 | bytes 4194304 | tf_op jit(solution)/shard_map/while/body/eval_jaxpr/kab,knb->kna/dot_general | solution.py:39
  240.5 1.9 collective-permute-start
  242.4 14.5 %collective-permute-done = f32[16,128,128]{2,1,0:T(8,128)} collective-permute-done((f32[16,128,128]{2,1,0:T(8,128)}, f32[16,128,128]{2,1,0:T(8,128)}, u32[]{:S(2)}, u32[]{:S(2)}) %collective-permute-start) | collective-permute-done | bytes 1048608 | tf_op jit(solution)/shard_map/while/body/eval_jaxpr/ppermute | solution.py:15
  256.9 4.5 %convolution_add_fusion.2 = f32[16,128,128]{2,1,0:T(8,128)} fusion(f32[16,128,128]{2,1,0:T(8,128)S(1)} %get-tuple-element.96, f32[16,128,128]{2,1,0:T(8,128)} %collective-permute-done, f32[16,128,128]{2,1,0:T(8,128)S(1)} %get-tuple-element.95), kind=kOutput, calls=%fused_computation.4.clone.1 | convolution fusion | flops 402915328 | bytes 4194304 | tf_op jit(solution)/shard_map/while/body/eval_jaxpr/kab,knb->kna/dot_general | solution.py:39
  261.4 1.9 collective-permute-start
  263.3 14.5 %collective-permute-done = f32[16,128,128]{2,1,0:T(8,128)} collective-permute-done((f32[16,128,128]{2,1,0:T(8,128)}, f32[16,128,128]{2,1,0:T(8,128)}, u32[]{:S(2)}, u32[]{:S(2)}) %collective-permute-start) | collective-permute-done | bytes 1048608 | tf_op jit(solution)/shard_map/while/body/eval_jaxpr/ppermute | solution.py:15
  277.8 4.5 %convolution_add_fusion.2 = f32[16,128,128]{2,1,0:T(8,128)} fusion(f32[16,128,128]{2,1,0:T(8,128)S(1)} %get-tuple-element.96, f32[16,128,128]{2,1,0:T(8,128)} %collective-permute-done, f32[16,128,128]{2,1,0:T(8,128)S(1)} %get-tuple-element.95), kind=kOutput, calls=%fused_computation.4.clone.1 | convolution fusion | flops 402915328 | bytes 4194304 | tf_op jit(solution)/shard_map/while/body/eval_jaxpr/kab,knb->kna/dot_general | solution.py:39
  282.3 1.9 collective-permute-start
  284.2 14.5 %collective-permute-done = f32[16,128,128]{2,1,0:T(8,128)} collective-permute-done((f32[16,128,128]{2,1,0:T(8,128)}, f32[16,128,128]{2,1,0:T(8,128)}, u32[]{:S(2)}, u32[]{:S(2)}) %collective-permute-start) | collective-permute-done | bytes 1048608 | tf_op jit(solution)/shard_map/while/body/eval_jaxpr/ppermute | solution.py:15
  298.7 4.5 %convolution_add_fusion.2 = f32[16,128,128]{2,1,0:T(8,128)} fusion(f32[16,128,128]{2,1,0:T(8,128)S(1)} %get-tuple-element.96, f32[16,128,128]{2,1,0:T(8,128)} %collective-permute-done, f32[16,128,128]{2,1,0:T(8,128)S(1)} %get-tuple-element.95), kind=kOutput, calls=%fused_computation.4.clone.1 | convolution fusion | flops 402915328 | bytes 4194304 | tf_op jit(solution)/shard_map/while/body/eval_jaxpr/kab,knb->kna/dot_general | solution.py:39
  303.2 1.9 collective-permute-start
  305.1 14.5 %collective-permute-done = f32[16,128,128]{2,1,0:T(8,128)} collective-permute-done((f32[16,128,128]{2,1,0:T(8,128)}, f32[16,128,128]{2,1,0:T(8,128)}, u32[]{:S(2)}, u32[]{:S(2)}) %collective-permute-start) | collective-permute-done | bytes 1048608 | tf_op jit(solution)/shard_map/while/body/eval_jaxpr/ppermute | solution.py:15
  319.6 4.5 %convolution_add_fusion.2 = f32[16,128,128]{2,1,0:T(8,128)} fusion(f32[16,128,128]{2,1,0:T(8,128)S(1)} %get-tuple-element.96, f32[16,128,128]{2,1,0:T(8,128)} %collective-permute-done, f32[16,128,128]{2,1,0:T(8,128)S(1)} %get-tuple-element.95), kind=kOutput, calls=%fused_computation.4.clone.1 | convolution fusion | flops 402915328 | bytes 4194304 | tf_op jit(solution)/shard_map/while/body/eval_jaxpr/kab,knb->kna/dot_general | solution.py:39
  324.1 1.9 collective-permute-start
  326.0 14.5 %collective-permute-done = f32[16,128,128]{2,1,0:T(8,128)} collective-permute-done((f32[16,128,128]{2,1,0:T(8,128)}, f32[16,128,128]{2,1,0:T(8,128)}, u32[]{:S(2)}, u32[]{:S(2)}) %collective-permute-start) | collective-permute-done | bytes 1048608 | tf_op jit(solution)/shard_map/while/body/eval_jaxpr/ppermute | solution.py:15
  340.5 4.5 %convolution_add_fusion.2 = f32[16,128,128]{2,1,0:T(8,128)} fusion(f32[16,128,128]{2,1,0:T(8,128)S(1)} %get-tuple-element.96, f32[16,128,128]{2,1,0:T(8,128)} %collective-permute-done, f32[16,128,128]{2,1,0:T(8,128)S(1)} %get-tuple-element.95), kind=kOutput, calls=%fused_computation.4.clone.1 | convolution fusion | flops 402915328 | bytes 4194304 | tf_op jit(solution)/shard_map/while/body/eval_jaxpr/kab,knb->kna/dot_general | solution.py:39
  345.0 1.9 collective-permute-start
  346.9 14.5 %collective-permute-done = f32[16,128,128]{2,1,0:T(8,128)} collective-permute-done((f32[16,128,128]{2,1,0:T(8,128)}, f32[16,128,128]{2,1,0:T(8,128)}, u32[]{:S(2)}, u32[]{:S(2)}) %collective-permute-start) | collective-permute-done | bytes 1048608 | tf_op jit(solution)/shard_map/while/body/eval_jaxpr/ppermute | solution.py:15
  361.4 4.5 %convolution_add_fusion.2 = f32[16,128,128]{2,1,0:T(8,128)} fusion(f32[16,128,128]{2,1,0:T(8,128)S(1)} %get-tuple-element.96, f32[16,128,128]{2,1,0:T(8,128)} %collective-permute-done, f32[16,128,128]{2,1,0:T(8,128)S(1)} %get-tuple-element.95), kind=kOutput, calls=%fused_computation.4.clone.1 | convolution fusion | flops 402915328 | bytes 4194304 | tf_op jit(solution)/shard_map/while/body/eval_jaxpr/kab,knb->kna/dot_general | solution.py:39
  (28 shorter events, 0.6 us)
Async XLA Ops:
  0.6 58.7 %copy-start = (f32[16,128,128]{2,1,0:T(8,128)S(1)}, f32[16,128,128]{2,1,0:T(8,128)}, u32[]{:S(2)}) copy-start(f32[16,128,128]{2,1,0:T(8,128)} %param.19) | copy-start | bytes 3145732
  6.6 42.7 %all-to-all-start = ((bf16[16,1,16]{2,1,0:T(2,128)(2,1)}), bf16[16,1,16]{2,1,0:T(2,128)(2,1)S(1)}, u32[]{:S(2)}, u32[]{:S(2)}) async-start(bf16[16,1,16]{2,1,0:T(2,128)(2,1)} %copy.41), calls=%async_computation | async-start | bytes 16384 | tf_op jit(solution)/shard_map/all_to_all | solution.py:85
  49.2 7.0 %copy-start.5 = (s32[128]{0:T(128)S(1)}, s32[128]{0:T(128)}, u32[]{:S(2)}) copy-start(s32[128]{0:T(128)} %param.29) | copy-start | bytes 1540
  49.2 7.1 %copy-start.1 = (bf16[4,128,128]{2,1,0:T(8,128)(2,1)S(1)}, bf16[4,128,128]{2,1,0:T(8,128)(2,1)}, u32[]{:S(2)}) copy-start(bf16[4,128,128]{2,1,0:T(8,128)(2,1)} %param.20) | copy-start | bytes 393220
  49.2 145.0 %all-to-all-start.1 = ((bf16[16,16,128,128]{3,2,1,0:T(8,128)(2,1)}), bf16[16,16,128,128]{3,2,1,0:T(8,128)(2,1)}, u32[]{:S(2)}, u32[]{:S(2)}) async-start(bf16[16,16,128,128]{3,2,1,0:T(8,128)(2,1)} %broadcast_select_fusion), calls=%async_computation.1 | async-start | bytes 16777216 | tf_op jit(solution)/shard_map/all_to_all | solution.py:84
  56.3 3.0 copy-start.4
  56.3 3.0 copy-start.3
  211.3 1.0 copy-start.2
  216.7 19.3 %collective-permute-start = (f32[16,128,128]{2,1,0:T(8,128)}, f32[16,128,128]{2,1,0:T(8,128)}, u32[]{:S(2)}, u32[]{:S(2)}) collective-permute-start(f32[16,128,128]{2,1,0:T(8,128)} %get-tuple-element.89), channel_id=1, source_target_pairs={{16,0},{32,16},{48,32},{64,48},{80,64},{96,80},{112,96},{17,1},{33... | collective-permute-start | bytes 3145736 | tf_op jit(solution)/shard_map/while/body/eval_jaxpr/ppermute | solution.py:15
  240.5 16.4 %collective-permute-start = (f32[16,128,128]{2,1,0:T(8,128)}, f32[16,128,128]{2,1,0:T(8,128)}, u32[]{:S(2)}, u32[]{:S(2)}) collective-permute-start(f32[16,128,128]{2,1,0:T(8,128)} %get-tuple-element.89), channel_id=1, source_target_pairs={{16,0},{32,16},{48,32},{64,48},{80,64},{96,80},{112,96},{17,1},{33... | collective-permute-start | bytes 3145736 | tf_op jit(solution)/shard_map/while/body/eval_jaxpr/ppermute | solution.py:15
  261.4 16.4 %collective-permute-start = (f32[16,128,128]{2,1,0:T(8,128)}, f32[16,128,128]{2,1,0:T(8,128)}, u32[]{:S(2)}, u32[]{:S(2)}) collective-permute-start(f32[16,128,128]{2,1,0:T(8,128)} %get-tuple-element.89), channel_id=1, source_target_pairs={{16,0},{32,16},{48,32},{64,48},{80,64},{96,80},{112,96},{17,1},{33... | collective-permute-start | bytes 3145736 | tf_op jit(solution)/shard_map/while/body/eval_jaxpr/ppermute | solution.py:15
  282.3 16.4 %collective-permute-start = (f32[16,128,128]{2,1,0:T(8,128)}, f32[16,128,128]{2,1,0:T(8,128)}, u32[]{:S(2)}, u32[]{:S(2)}) collective-permute-start(f32[16,128,128]{2,1,0:T(8,128)} %get-tuple-element.89), channel_id=1, source_target_pairs={{16,0},{32,16},{48,32},{64,48},{80,64},{96,80},{112,96},{17,1},{33... | collective-permute-start | bytes 3145736 | tf_op jit(solution)/shard_map/while/body/eval_jaxpr/ppermute | solution.py:15
  303.2 16.4 %collective-permute-start = (f32[16,128,128]{2,1,0:T(8,128)}, f32[16,128,128]{2,1,0:T(8,128)}, u32[]{:S(2)}, u32[]{:S(2)}) collective-permute-start(f32[16,128,128]{2,1,0:T(8,128)} %get-tuple-element.89), channel_id=1, source_target_pairs={{16,0},{32,16},{48,32},{64,48},{80,64},{96,80},{112,96},{17,1},{33... | collective-permute-start | bytes 3145736 | tf_op jit(solution)/shard_map/while/body/eval_jaxpr/ppermute | solution.py:15
  324.1 16.4 %collective-permute-start = (f32[16,128,128]{2,1,0:T(8,128)}, f32[16,128,128]{2,1,0:T(8,128)}, u32[]{:S(2)}, u32[]{:S(2)}) collective-permute-start(f32[16,128,128]{2,1,0:T(8,128)} %get-tuple-element.89), channel_id=1, source_target_pairs={{16,0},{32,16},{48,32},{64,48},{80,64},{96,80},{112,96},{17,1},{33... | collective-permute-start | bytes 3145736 | tf_op jit(solution)/shard_map/while/body/eval_jaxpr/ppermute | solution.py:15
  345.0 16.4 %collective-permute-start = (f32[16,128,128]{2,1,0:T(8,128)}, f32[16,128,128]{2,1,0:T(8,128)}, u32[]{:S(2)}, u32[]{:S(2)}) collective-permute-start(f32[16,128,128]{2,1,0:T(8,128)} %get-tuple-element.89), channel_id=1, source_target_pairs={{16,0},{32,16},{48,32},{64,48},{80,64},{96,80},{112,96},{17,1},{33... | collective-permute-start | bytes 3145736 | tf_op jit(solution)/shard_map/while/body/eval_jaxpr/ppermute | solution.py:15
where the time goes:
time: 368 us; the launch traced here: 366 us
  waiting for transfers between devices  217 us (59%)
  matrix products  67.4 us (18%)
  local copies, waits for them, and re-layouts  36.6 us (10%)
  starting transfers between devices  32.4 us (9%)
  other arithmetic  11.3 us (3%)
    all_to_all x1, waiting for transfers between devices, per_device(): lax.all_to_all(sent_blocks, 'row', split_axis=0, concat_axis=0, tiled=True)  116 us
    ppermute x7, waiting for transfers between devices, shifted(): return lax.ppermute(x, axis, pairs)  101 us
    dot_general x7, matrix products, apply_map(): return jnp.einsum('kab,knb->kna', matrix, vector, precision=precise)  31.4 us
    dot_general x2, matrix products, finish_products(): jnp.einsum('zmq,zqy->zmy', rescaled_blocks, upper_factor_blocks, preferre...  21.5 us
    ppermute x7, starting transfers between devices, shifted(): return lax.ppermute(x, axis, pairs)  17 us
    all_to_all x1, local copies, waits for them, and re-layouts, per_device(): lax.all_to_all(sent_blocks, 'row', split_axis=0, concat_axis=0, tiled=True)  12.2 us
    gather x1, local copies, waits for them, and re-layouts, per_device(): jnp.take(cross_blocks, source, axis=0)  10.7 us
    dot_general x2, matrix products, add_into_rows(): jnp.einsum('ks,sab->kab', picks, blocks, preferred_element_type=jnp.float32)  9.41 us
  transfers between devices with their start and end apart: 9, of which 8 were waited for; matrix products, arithmetic and copies ran while one was open for 15% of the time, Pallas kernels for 0%

commit v1 on v0

v1 whole, which is shorter than its diff:
```python
import functools

import jax
import jax.numpy as jnp
from jax import lax
from jax.experimental import pallas as pl
from jax.experimental.pallas import tpu as pltpu
from jax.sharding import PartitionSpec as P

B = 128
SIDE = 4
UNROLL = 4
MIB = 1 << 20

HBM = pl.BlockSpec(memory_space=pl.ANY)
VMEM = pl.BlockSpec(memory_space=pltpu.VMEM)
SMEM = pl.BlockSpec(memory_space=pltpu.SMEM)

bf16 = jnp.bfloat16
f32 = jnp.float32
precise = lax.Precision.HIGHEST


def mm(a, b):
    return jnp.dot(a, b, preferred_element_type=f32)


def mm_nt(a, b):
    return lax.dot_general(a, b, (((1,), (1,)), ((), ())), preferred_element_type=f32)


def split(x):
    high = x.astype(bf16)
    return high, (x - high.astype(f32)).astype(bf16)


def cross_kernel(first, cells, sizes, cell_ref, pivot_ref, table_ref, left_ref, right_ref, *refs):
    outs = refs[: len(sizes)]
    slot_list, cell_list, left, right, total, lsem, rsem, osem = refs[len(sizes) :]
    slots = left_ref.shape[0]

    def note(i, n):
        c = cell_ref[i] - first
        slot_list[n] = i
        cell_list[n] = c
        return n + jnp.where((c >= 0) & (c < cells), 1, 0)

    count = lax.fori_loop(0, slots, note, 0, unroll=8)
    rounds = (count + UNROLL - 1) // UNROLL

    def pad(j, _):
        slot_list[j] = 0
        cell_list[j] = cells
        return 0

    lax.fori_loop(count, rounds * UNROLL, pad, 0)

    def fetch(j, _):
        s = slot_list[j]
        pltpu.make_async_copy(left_ref.at[s], left.at[j], lsem.at[j]).start()
        pltpu.make_async_copy(right_ref.at[s], right.at[j], rsem.at[j]).start()
        return 0

    lax.fori_loop(0, rounds * UNROLL, fetch, 0)

    def clear(c, _):
        total[c] = jnp.zeros((B, B), bf16)
        return 0

    lax.fori_loop(0, cells + 1, clear, 0, unroll=4)

    def work(r, _):
        js = [r * UNROLL + u for u in range(UNROLL)]
        for j in js:
            pltpu.make_async_copy(left_ref.at[0], left.at[j], lsem.at[j]).wait()
            pltpu.make_async_copy(right_ref.at[0], right.at[j], rsem.at[j]).wait()
        scaled = [mm(left[j], table_ref[pivot_ref[slot_list[j]]]).astype(bf16) for j in js]
        updates = [mm(s, right[j]) for s, j in zip(scaled, js)]
        for j, u in zip(js, updates):
            c = cell_list[j]
            total[c] = (total[c].astype(f32) + u).astype(bf16)
        return 0

    lax.fori_loop(0, rounds, work, 0)

    copies = []
    start = 0
    for k, size in enumerate(sizes):
        copies.append(pltpu.make_async_copy(total.at[pl.ds(start, size)], outs[k], osem.at[k]))
        start += size
    for c in copies:
        c.start()
    for c in copies:
        c.wait()


def cross_sums(first, sizes, cell, pivot, table, left, right, live):
    cells = sum(sizes)
    slots = left.shape[0]
    return pl.pallas_call(
        functools.partial(cross_kernel, first, cells, sizes),
        out_shape=[jax.ShapeDtypeStruct((n, B, B), bf16) for n in sizes],
        in_specs=[SMEM, SMEM, VMEM, HBM, HBM],
        out_specs=[HBM] * len(sizes),
        scratch_shapes=[
            pltpu.SMEM((slots + UNROLL,), jnp.int32),
            pltpu.SMEM((slots + UNROLL,), jnp.int32),
            pltpu.VMEM((slots, B, B), bf16),
            pltpu.VMEM((slots, B, B), bf16),
            pltpu.VMEM((cells + 1, B, B), bf16),
            pltpu.SemaphoreType.DMA((slots,)),
            pltpu.SemaphoreType.DMA((slots,)),
            pltpu.SemaphoreType.DMA((len(sizes),)),
        ],
        compiler_params=pltpu.CompilerParams(vmem_limit_bytes=30 * MIB),
        cost_estimate=pl.CostEstimate(
            flops=live * 4 * B**3, bytes_accessed=live * 4 * B * B + cells * 2 * B * B, transcendentals=0
        ),
        name="cross_sums",
    )(cell, pivot, table, left, right)


def local_kernel(per_step, pivot_ref, target_ref, table_ref, coupling_ref, left_ref, right_ref, order_ref, out_ref):
    step = pl.program_id(0)

    @pl.when(step == 0)
    def _():
        out_ref[...] = coupling_ref[...].astype(f32)

    for base in range(0, per_step, UNROLL):
        js = range(base, base + UNROLL)
        scaled = [mm(left_ref[j], table_ref[pivot_ref[step * per_step + j]]).astype(bf16) for j in js]
        updates = [mm(s, right_ref[j]).astype(bf16).astype(f32) for s, j in zip(scaled, js)]
        for j, u in zip(js, updates):
            t = target_ref[step * per_step + j]
            out_ref[t] = out_ref[t] - u


def local_sums(pivot, target, table, coupling, left, right, order):
    slots = left.shape[0]
    rows = coupling.shape[0]
    per_step = 8
    block = pl.BlockSpec((per_step, B, B), lambda i: (i, 0, 0))
    return pl.pallas_call(
        functools.partial(local_kernel, per_step),
        grid=(slots // per_step,),
        out_shape=jax.ShapeDtypeStruct((rows, B, B), f32),
        in_specs=[SMEM, SMEM, VMEM, VMEM, block, block, HBM],
        out_specs=pl.BlockSpec((rows, B, B), lambda i: (0, 0, 0)),
        compiler_params=pltpu.CompilerParams(vmem_limit_bytes=16 * MIB),
        cost_estimate=pl.CostEstimate(
            flops=slots * 4 * B**3, bytes_accessed=slots * 4 * B * B + rows * 6 * B * B, transcendentals=0
        ),
        name="local_sums",
    )(pivot, target, table, coupling, left, right, order)


def first_totals_kernel(own_x, own_z, *refs):
    arrivals = refs[:8]
    outs = refs[8:16]
    held, sem = refs[16:]
    b = pl.program_id(0)
    for s, own in enumerate((own_x, own_z)):
        for half in range(2):
            t = own[half, 0].astype(f32)
            for a in arrivals[s * 4 + half * 2 : s * 4 + half * 2 + 2]:
                t = t + a[0].astype(f32)
            held[b, s, half] = t.astype(bf16)
    for k in range(SIDE):

        @pl.when(b == k)
        def _():
            for s in range(2):
                pltpu.make_async_copy(held.at[k, s], outs[s * SIDE + k], sem.at[k, s]).start()

    @pl.when(b == SIDE - 1)
    def _():
        for k in range(SIDE):
            for s in range(2):
                pltpu.make_async_copy(held.at[k, s], outs[s * SIDE + k], sem.at[k, s]).wait()


def first_totals(own_x, own_z, arrivals):
    quarter = own_x.shape[0] // (2 * SIDE)
    own_spec = pl.BlockSpec((2, 1, quarter, B, B), lambda b: (0, b, 0, 0, 0))
    spec = pl.BlockSpec((1, quarter, B, B), lambda b: (b, 0, 0, 0))
    outs = pl.pallas_call(
        first_totals_kernel,
        grid=(SIDE,),
        out_shape=[jax.ShapeDtypeStruct((2, quarter, B, B), bf16)] * (2 * SIDE),
        in_specs=[own_spec, own_spec] + [spec] * 8,
        out_specs=[HBM] * (2 * SIDE),
        scratch_shapes=[
            pltpu.VMEM((SIDE, 2, 2, quarter, B, B), bf16),
            pltpu.SemaphoreType.DMA((SIDE, 2)),
        ],
        compiler_params=pltpu.CompilerParams(vmem_limit_bytes=16 * MIB),
        cost_estimate=pl.CostEstimate(flops=0, bytes_accessed=256 * 2 * B * B, transcendentals=0),
        name="first_totals",
    )(
        own_x.reshape(2, SIDE, quarter, B, B),
        own_z.reshape(2, SIDE, quarter, B, B),
        *[a.reshape(SIDE, quarter, B, B) for a in arrivals],
    )
    return outs[:SIDE], outs[SIDE:]


def coupling_kernel(base_ref, diag_ref, *refs):
    parts = refs[:8]
    new_ref, step_ref = refs[8:]
    i = pl.program_id(0)
    per = base_ref.shape[0]
    steps = pl.num_programs(0) // 2

    def finish(mine):
        for r in range(per):
            t = base_ref[r]
            for p in mine:
                t = t - p[r].astype(f32)
            new_ref[r] = t
            th, tl = split(t)
            dh, dl = split(diag_ref[r])
            step_ref[r] = -(mm(dh, th) + (mm(dh, tl) + mm(dl, th))).astype(bf16)

    @pl.when(i < steps)
    def _():
        finish(parts[:4])

    @pl.when(i >= steps)
    def _():
        finish(parts[4:])


def coupling_and_step(base, diag, parts_x, parts_z):
    rows = base.shape[0]
    per = 2
    steps = rows // per // 2
    block = pl.BlockSpec((per, B, B), lambda i: (i, 0, 0))
    x_block = pl.BlockSpec((per, B, B), lambda i: (jnp.minimum(i, steps - 1), 0, 0))
    z_block = pl.BlockSpec((per, B, B), lambda i: (jnp.maximum(i - steps, 0), 0, 0))
    return pl.pallas_call(
        coupling_kernel,
        grid=(rows // per,),
        out_shape=[jax.ShapeDtypeStruct((rows, B, B), f32), jax.ShapeDtypeStruct((rows, B, B), bf16)],
        in_specs=[block, block] + [x_block] * 4 + [z_block] * 4,
        out_specs=[block, block],
        compiler_params=pltpu.CompilerParams(vmem_limit_bytes=16 * MIB),
        cost_estimate=pl.CostEstimate(flops=rows * 6 * B**3, bytes_accessed=rows * 22 * B * B, transcendentals=0),
        name="coupling_and_step",
    )(base, diag, *parts_x, *parts_z)


def chain_kernel(sections, chains, step_ref, offset_ref, out_ref):
    current = []
    for j in range(chains):
        k = (sections - 1) * chains + j
        o = offset_ref[k]
        out_ref[k] = o
        current.append(o.astype(f32))
    for s in range(sections - 2, -1, -1):
        for j in range(chains):
            k = s * chains + j
            high, low = split(current[j])
            m = step_ref[k]
            new = offset_ref[k].astype(f32) + (mm_nt(high, m) + mm_nt(low, m))
            out_ref[k] = new.astype(bf16)
            current[j] = new


def run_chains(sections, steps, offsets):
    rows = steps.shape[0]
    return pl.pallas_call(
        functools.partial(chain_kernel, sections, rows // sections),
        out_shape=jax.ShapeDtypeStruct((rows, B, B), bf16),
        in_specs=[VMEM, VMEM],
        out_specs=VMEM,
        compiler_params=pltpu.CompilerParams(vmem_limit_bytes=16 * MIB),
        cost_estimate=pl.CostEstimate(flops=rows * 4 * B**3, bytes_accessed=rows * 6 * B * B, transcendentals=0),
        name="run_chains",
    )(steps, offsets)


def moved(x, along, by):
    pairs = []
    for a in range(SIDE):
        for c in range(SIDE):
            if along == 0:
                pairs.append((a * SIDE + c, (a + by) % SIDE * SIDE + c))
            else:
                pairs.append((a * SIDE + c, a * SIDE + (c + by) % SIDE))
    return lax.ppermute(x, "row", pairs)


def add(a, b):
    return (a.astype(f32) + b.astype(f32)).astype(bf16)


def per_device(
    coupling,
    diag_inverse,
    pivot_inverse,
    cross_left,
    cross_right,
    cross_pivot,
    cross_owner,
    foreign_target_row,
    cross_count,
    local_left,
    local_right,
    local_pivot,
    local_target,
    adjoint_seed,
):
    sections = lax.axis_size("section")
    rows = coupling.shape[0]
    slots = cross_left.shape[0]
    half = rows // 2
    quarter = rows // 4
    me = lax.axis_index("row")

    owner = cross_owner[:, 0]
    dx = (owner // SIDE - me // SIDE) % SIDE
    dz = (owner % SIDE - me % SIDE) % SIDE
    second = foreign_target_row // half
    row = foreign_target_row % half
    a = jnp.where(second == 0, dx, dz)
    b = jnp.where(second == 0, dz, dx)
    upper = row // quarter
    spot = b * quarter + row % quarter
    n = SIDE * quarter
    group = 4 * n
    minus = (a == 3).astype(jnp.int32)
    cell = jnp.where(
        a == 2,
        second * 2 * n + upper * n + spot,
        jnp.where(
            a == 0,
            3 * group + second * 2 * n + upper * n + spot,
            jnp.where(minus == upper, 2 * group, group) + second * 2 * n + minus * n + spot,
        ),
    )
    live = jnp.arange(slots, dtype=jnp.int32) < cross_count[0]
    cell = jnp.where(live, cell, -1)

    sums = functools.partial(
        cross_sums,
        cell=cell,
        pivot=cross_pivot,
        table=pivot_inverse,
        left=cross_left,
        right=cross_right,
    )
    far = sums(0, [n] * 4, live=slots // 4)
    ways = ((0, 1), (0, -1), (1, 1), (1, -1))
    far_in = [moved(x, *w) for x, w in zip(far, ways)]
    near = sums(group, [n] * 8 + [2 * n] * 2, live=slots * 3 // 4)
    free_in = [moved(x, *w) for x, w in zip(near[:4], ways)]
    joined = [add(x, y) for x, y in zip(near[4:8], far_in)]
    joined_in = [moved(x, *w) for x, w in zip(joined, ways)]

    step_offset = jnp.einsum("kab,knb->kna", diag_inverse, adjoint_seed, precision=precise).astype(bf16)
    offsets = lax.all_to_all(step_offset, "section", split_axis=0, concat_axis=0, tiled=True)
    base = local_sums(local_pivot, local_target, pivot_inverse, coupling, local_left, local_right, joined[0])

    arrivals = []
    for s in range(2):
        fp, fm = free_in[2 * s : 2 * s + 2]
        jp, jm = joined_in[2 * s : 2 * s + 2]
        arrivals += [jp, fm, fp, jm]
    tot_x, tot_z = first_totals(near[8], near[9], arrivals)
    flat = lambda x: x.reshape(half, B, B)
    parts_x = [flat(tot_x[0])] + [moved(flat(tot_x[k]), 1, k) for k in (2, 1, 3)]
    parts_z = [flat(tot_z[0])] + [moved(flat(tot_z[k]), 0, k) for k in (2, 1, 3)]
    updated, step_matrix = coupling_and_step(base, diag_inverse, parts_x, parts_z)
    steps = lax.all_to_all(step_matrix, "section", split_axis=0, concat_axis=0, tiled=True)
    solved = run_chains(sections, steps, offsets)
    adjoint = lax.all_to_all(solved, "section", split_axis=0, concat_axis=0, tiled=True).astype(f32)
    return (updated, adjoint)


def solution(mesh):
    spread = ("section", "row")
    block = P(spread, None, None)
    line = P(spread)
    return jax.shard_map(
        per_device,
        mesh=mesh,
        in_specs=(
            block,
            block,
            block,
            block,
            block,
            line,
            P(spread, None),
            line,
            line,
            block,
            block,
            line,
            line,
            block,
        ),
        out_specs=(block, block),
        check_vma=False,
    )
```

time: 368 us -> 152 us (0.41)
  waiting for transfers between devices: 217 us -> 17.7 us
  matrix products: 67.4 us -> 3.1 us
  Pallas kernels: 0 us -> 36.6 us
  blocking collectives: 0 us -> 28 us
  local copies, waits for them, and re-layouts: 36.6 us -> 15.6 us
  starting transfers between devices: 32.4 us -> 45.3 us
  other arithmetic: 11.3 us -> 2.34 us
    all_to_all x2 -> x1, waiting for transfers between devices: 116 us -> 0.01 us  [per_device(): lax.all_to_all(step_offset, 'section', split_axis=0, concat_axis=0, tiled...]
    ppermute x7 -> x18, waiting for transfers between devices: 101 us -> 17.7 us  [moved(): return lax.ppermute(x, 'row', pairs)]
    dot_general x12 -> x0, matrix products: 65.1 us -> none  [the longest x7 31.4 us: apply_map(): return jnp.einsum('kab,knb->kna', matrix, vector, precision=precise)]
    pallas_call x0 -> x6, Pallas kernels: none -> 36.6 us  [the longest x2 19.9 us: cross_sums(): pl.pallas_call(functools.partial(cross_kernel, first, cells, sizes), out_...]
    all_to_all x0 -> x2, blocking collectives: none -> 28 us  [the longest x1 15.2 us: per_device(): lax.all_to_all(step_matrix, 'section', split_axis=0, concat_axis=0, tiled...]
    ppermute x7 -> x18, starting transfers between devices: 17 us -> 38.1 us  [moved(): return lax.ppermute(x, 'row', pairs)]
    gather x5 -> x0, local copies, waits for them, and re-layouts: 19.6 us -> none  [the longest x1 10.7 us: per_device(): jnp.take(cross_blocks, source, axis=0)]
    unnamed x13 -> x38, local copies, waits for them, and re-layouts: 1.97 us -> 15.6 us
  transfers between devices with their start and end apart: 9 -> 19, of which waited for: 8 -> 5; matrix products, arithmetic and copies ran while one was open for 15% -> 2% of each run, Pallas kernels for 0% -> 17%
where the time goes in v1:
time: 152 us; the launch traced here: 150 us
  starting transfers between devices  45.3 us (30%)
  Pallas kernels  36.6 us (24%)
  blocking collectives  28 us (18%)
  waiting for transfers between devices  17.7 us (12%)
  local copies, waits for them, and re-layouts  15.6 us (10%)
  matrix products  3.1 us (2%)
  other arithmetic  2.34 us (2%)
  between operations  1.61 us (1%)
    ppermute x18, starting transfers between devices, moved(): return lax.ppermute(x, 'row', pairs)  38.1 us
    pallas_call x2, Pallas kernels, cross_sums(): pl.pallas_call(functools.partial(cross_kernel, first, cells, sizes), out_...  19.9 us
    ppermute x18, waiting for transfers between devices, moved(): return lax.ppermute(x, 'row', pairs)  17.7 us
    unnamed x38, local copies, waits for them, and re-layouts  15.6 us
    all_to_all x1, blocking collectives, per_device(): lax.all_to_all(step_matrix, 'section', split_axis=0, concat_axis=0, tiled...  15.2 us
    all_to_all x1, blocking collectives, per_device(): lax.all_to_all(solved, 'section', split_axis=0, concat_axis=0, tiled=True)  12.8 us
    pallas_call x1, Pallas kernels, local_sums(): pl.pallas_call(functools.partial(local_kernel, per_step), grid=(slots //...  8.56 us
    all_to_all x1, starting transfers between devices, per_device(): lax.all_to_all(step_offset, 'section', split_axis=0, concat_axis=0, tiled...  7.15 us
  transfers between devices with their start and end apart: 19, of which 5 were waited for; matrix products, arithmetic and copies ran while one was open for 2% of the time, Pallas kernels for 17%

profile of v1, /device:TPU:1, one launch (start us, length us, event | category | flops | bytes accessed | tf_op | source)
XLA Modules:
  0.0 150.2 jit_solution(15970716616654757244)
XLA Ops:
  1.4 0.7 compare_select_fusion.7.cell_ref
  2.1 2.2 %copy-done.1 = bf16[128,128,128]{2,1,0:T(8,128)(2,1)S(1)} copy-done((bf16[128,128,128]{2,1,0:T(8,128)(2,1)S(1)}, bf16[128,128,128]{2,1,0:T(8,128)(2,1)}, u32[]{:S(2)}) %copy-start.1) | copy-done | bytes 4194328
  4.3 2.2 %copy-done.2 = bf16[128,128,128]{2,1,0:T(8,128)(2,1)S(1)} copy-done((bf16[128,128,128]{2,1,0:T(8,128)(2,1)S(1)}, bf16[128,128,128]{2,1,0:T(8,128)(2,1)}, u32[]{:S(2)}) %copy-start.2) | copy-done | bytes 4194328
  6.5 0.9 copy-done.6
  7.4 0.7 copy-done.11
  8.0 8.1 %cross_sums.3 = (bf16[16,128,128]{2,1,0:T(8,128)(2,1)S(1)}, bf16[16,128,128]{2,1,0:T(8,128)(2,1)S(1)}, bf16[16,128,128]{2,1,0:T(8,128)(2,1)S(1)}, bf16[16,128,128]{2,1,0:T(8,128)(2,1)S(1)}) custom-call(s32[128]{0:T(128)S(1)} %compare_select_fusion.7.cell_ref, s32[128]{0:T(128)S(1)} %copy-done.11, bf16[4,128,128]{2,1,0:T(8,128)(2,1)S(1)} %copy-done.6, ...), custom_call_target="tpu_custom_call" | custom-call | flops 268435456 | bytes 4194304 | tf_op jit(solution)/shard_map/cross_sums/pallas_call | solution.py:100
  16.1 6.1 %collective-permute-start.10 = (bf16[16,128,128]{2,1,0:T(8,128)(2,1)S(1)}, bf16[16,128,128]{2,1,0:T(8,128)(2,1)S(1)}, u32[]{:S(2)}, u32[]{:S(2)}) collective-permute-start(bf16[16,128,128]{2,1,0:T(8,128)(2,1)S(1)} %get-tuple-element.39), channel_id=1, source_target_pairs={{0,3},{1,0},{2,1},{3,2},{4,7},{5,4},{6,5},{7,6},{8,11},{9,8},{10,9... | collective-permute-start | bytes 1572872 | tf_op jit(solution)/shard_map/ppermute | solution.py:291
  22.2 2.5 %collective-permute-start.4 = (bf16[16,128,128]{2,1,0:T(8,128)(2,1)S(1)}, bf16[16,128,128]{2,1,0:T(8,128)(2,1)S(1)}, u32[]{:S(2)}, u32[]{:S(2)}) collective-permute-start(bf16[16,128,128]{2,1,0:T(8,128)(2,1)S(1)} %get-tuple-element.33), channel_id=1, source_target_pairs={{0,12},{1,13},{2,14},{3,15},{4,0},{5,1},{6,2},{7,3},{8,4},{9,5},{1... | collective-permute-start | bytes 1572872 | tf_op jit(solution)/shard_map/ppermute | solution.py:291
  24.7 11.9 %cross_sums.2 = (bf16[16,128,128]{2,1,0:T(8,128)(2,1)S(1)}, bf16[16,128,128]{2,1,0:T(8,128)(2,1)S(1)}, bf16[16,128,128]{2,1,0:T(8,128)(2,1)S(1)}, bf16[16,128,12...) custom-call(s32[128]{0:T(128)S(1)} %compare_select_fusion.7.cell_ref, ...), custom_call_target="tpu_custom_call" | custom-call | flops 805306368 | bytes 12582912 | tf_op jit(solution)/shard_map/cross_sums/pallas_call | solution.py:100
  36.5 10.1 %collective-permute-start.9 = (bf16[16,128,128]{2,1,0:T(8,128)(2,1)S(1)}, bf16[16,128,128]{2,1,0:T(8,128)(2,1)S(1)}, u32[]{:S(2)}, u32[]{:S(2)}) collective-permute-start(bf16[16,128,128]{2,1,0:T(8,128)(2,1)S(1)} %get-tuple-element.37), channel_id=1, source_target_pairs={{0,1},{1,2},{2,3},{3,0},{4,5},{5,6},{6,7},{7,4},{8,9},{9,10},{10,1... | collective-permute-start | bytes 1572872 | tf_op jit(solution)/shard_map/ppermute | solution.py:291
  46.6 2.7 %collective-permute-start.2 = (bf16[16,128,128]{2,1,0:T(8,128)(2,1)S(1)}, bf16[16,128,128]{2,1,0:T(8,128)(2,1)S(1)}, u32[]{:S(2)}, u32[]{:S(2)}) collective-permute-start(bf16[16,128,128]{2,1,0:T(8,128)(2,1)S(1)} %get-tuple-element.30), channel_id=1, source_target_pairs={{0,12},{1,13},{2,14},{3,15},{4,0},{5,1},{6,2},{7,3},{8,4},{9,5},{1... | collective-permute-start | bytes 1572872 | tf_op jit(solution)/shard_map/ppermute | solution.py:291
  49.3 0.1 add_convert_fusion
  49.4 0.1 collective-permute-start.3
  49.5 0.1 add_convert_fusion.2
  49.7 3.5 %collective-permute-start.8 = (bf16[16,128,128]{2,1,0:T(8,128)(2,1)S(1)}, bf16[16,128,128]{2,1,0:T(8,128)(2,1)S(1)}, u32[]{:S(2)}, u32[]{:S(2)}) collective-permute-start(bf16[16,128,128]{2,1,0:T(8,128)(2,1)S(1)} %get-tuple-element.36), channel_id=1, source_target_pairs={{0,3},{1,0},{2,1},{3,2},{4,7},{5,4},{6,5},{7,6},{8,11},{9,8},{10,9... | collective-permute-start | bytes 1572872 | tf_op jit(solution)/shard_map/ppermute | solution.py:291
  53.2 0.1 add_convert_fusion.1
  53.3 1.4 collective-permute-start.11
  54.8 0.1 add_convert_fusion.3.order_ref
  54.9 5.0 %collective-permute-done.9 = bf16[16,128,128]{2,1,0:T(8,128)(2,1)S(1)} collective-permute-done((bf16[16,128,128]{2,1,0:T(8,128)(2,1)S(1)}, bf16[16,128,128]{2,1,0:T(8,128)(2,1)S(1)}, u32[]{:S(2)}, u32[]{:S(2)}) %collective-permute-start.9) | collective-permute-done | bytes 524320 | tf_op jit(solution)/shard_map/ppermute | solution.py:291
  59.9 3.9 %collective-permute-start.5 = (bf16[16,128,128]{2,1,0:T(8,128)(2,1)S(1)}, bf16[16,128,128]{2,1,0:T(8,128)(2,1)S(1)}, u32[]{:S(2)}, u32[]{:S(2)}) collective-permute-start(bf16[16,128,128]{2,1,0:T(8,128)(2,1)S(1)} %add_convert_fusion.2), channel_id=1, source_target_pairs={{0,12},{1,13},{2,14},{3,15},{4,0},{5,1},{6,2},{7,3},{8,4},{9,5},{1... | collective-permute-start | bytes 1572872 | tf_op jit(solution)/shard_map/ppermute | solution.py:291
  63.8 0.1 collective-permute-start.1
  63.9 0.2 collective-permute-done.8
  64.0 11.2 %collective-permute-done.11 = bf16[16,128,128]{2,1,0:T(8,128)(2,1)S(1)} collective-permute-done((bf16[16,128,128]{2,1,0:T(8,128)(2,1)S(1)}, bf16[16,128,128]{2,1,0:T(8,128)(2,1)S(1)}, u32[]{:S(2)}, u32[]{:S(2)}) %collective-permute-start.11) | collective-permute-done | bytes 524320 | tf_op jit(solution)/shard_map/ppermute | solution.py:291
  75.3 1.2 collective-permute-done.7
  76.5 0.1 collective-permute-done.1
  76.6 1.7 %first_totals.1 = (bf16[2,4,128,128]{3,2,1,0:T(8,128)(2,1)S(1)}, bf16[2,4,128,128]{3,2,1,0:T(8,128)(2,1)S(1)}, bf16[2,4,128,128]{3,2,1,0:T(8,128)(2,1)}, bf16[2,...) custom-call(bf16[2,4,4,128,128]{4,3,2,1,0:T(8,128)(2,1)S(1)} %bitcas, ...), custom_call_target="tpu_custom_call" | custom-call | bytes 8388608 | tf_op jit(solution)/shard_map/first_totals/pallas_call | solution.py:187
  78.2 0.7 copy-done.9
  78.9 0.7 copy-done.14
  79.6 0.7 copy-done.15
  80.3 0.7 copy-done.16
  81.0 0.7 copy-done.17
  81.8 0.7 copy-done.18
  82.5 2.5 %collective-permute-start.12 = (bf16[8,128,128]{2,1,0:T(8,128)(2,1)}, bf16[8,128,128]{2,1,0:T(8,128)(2,1)}, u32[]{:S(2)}, u32[]{:S(2)}) collective-permute-start(bf16[8,128,128]{2,1,0:T(8,128)(2,1)} %bitcast.13), channel_id=1, source_target_pairs={{0,2},{1,3},{2,0},{3,1},{4,6},{5,7},{6,4},{7,5},{8,10},{9,11},{10,... | collective-permute-start | bytes 786440 | tf_op jit(solution)/shard_map/ppermute | solution.py:291
  85.0 3.1 %convolution_convert_fusion = bf16[16,128,128]{2,1,0:T(8,128)(2,1)} fusion(f32[16,128,128]{2,1,0:T(8,128)S(1)} %copy-done, f32[16,128,128]{2,1,0:T(8,128)S(1)} %copy-done.5), kind=kOutput, calls=%fused_computation | convolution fusion | flops 402915328 | bytes 2621440 | tf_op jit(solution)/shard_map/kab,knb->kna/dot_general | solution.py:361
  88.1 7.1 %all-to-all-start.1 = ((bf16[16,128,128]{2,1,0:T(8,128)(2,1)}), bf16[16,128,128]{2,1,0:T(8,128)(2,1)S(1)}, u32[]{:S(2)}, u32[]{:S(2)}) async-start(bf16[16,128,128]{2,1,0:T(8,128)(2,1)} %convolution_convert_fusion), calls=%async_computation.1 | async-start | bytes 1048576 | tf_op jit(solution)/shard_map/all_to_all | solution.py:362
  95.2 1.4 collective-permute-start.13
  96.6 1.3 collective-permute-start.14
  97.9 1.0 collective-permute-start.16
  98.9 1.7 %collective-permute-start.17 = (bf16[8,128,128]{2,1,0:T(8,128)(2,1)}, bf16[8,128,128]{2,1,0:T(8,128)(2,1)S(1)}, u32[]{:S(2)}, u32[]{:S(2)}) collective-permute-start(bf16[8,128,128]{2,1,0:T(8,128)(2,1)} %bitcast.49), channel_id=1, source_target_pairs={{0,12},{1,13},{2,14},{3,15},{4,0},{5,1},{6,2},{7,3},{8,4},{9,5},{1... | collective-permute-start | bytes 786440 | tf_op jit(solution)/shard_map/ppermute | solution.py:291
  100.6 2.2 %copy-done.3 = bf16[128,128,128]{2,1,0:T(8,128)(2,1)S(1)} copy-done((bf16[128,128,128]{2,1,0:T(8,128)(2,1)S(1)}, bf16[128,128,128]{2,1,0:T(8,128)(2,1)}, u32[]{:S(2)}) %copy-start.3) | copy-done | bytes 4194328
  102.8 2.2 %copy-done.4 = bf16[128,128,128]{2,1,0:T(8,128)(2,1)S(1)} copy-done((bf16[128,128,128]{2,1,0:T(8,128)(2,1)S(1)}, bf16[128,128,128]{2,1,0:T(8,128)(2,1)}, u32[]{:S(2)}) %copy-start.4) | copy-done | bytes 4194328
  105.0 1.0 copy-done.8
  106.0 8.6 %local_sums.1.base_ref = f32[16,128,128]{2,1,0:T(8,128)S(1)} custom-call(s32[128]{0:T(128)S(1)} %copy-done.12, s32[128]{0:T(128)S(1)} %copy-done.13, bf16[4,128,128]{2,1,0:T(8,128)(2,1)S(1)} %copy-done.7, bf16[16,128,128]{2,1,0:T(8,128)(2,1)S(1)} %copy-done.8, bf16[128,128,128]{2,1,0:T(8,128)(2,1)S(1)} %copy-done.3, bf16[128,128,128]{2,1,0:T(8,128)(2,1)S(1)} %copy-done.4, ...), custom_call_target="tpu_custom_call" | custom-call | flops 1073741824 | bytes 9961472 | tf_op jit(solution)/shard_map/local_sums/pallas_call | solution.py:144
  114.7 5.3 %coupling_and_step.1 = (f32[16,128,128]{2,1,0:T(8,128)}, bf16[16,128,128]{2,1,0:T(8,128)(2,1)S(1)}) custom-call(f32[16,128,128]{2,1,0:T(8,128)S(1)} %local_sums.1.base_ref, f32[16,128,128]{2,1,0:T(8,128)S(1)} %copy-done.5, bf16[8,128,128]{2,1,0:T(8,128)(2,1)S(1)} %bitcast.47, bf16[8,128,128]{2,1,0:T(8,128)(2,1)} %collective-permute-done.12.refs_1_, ...), custom_call_target="tpu_custom_call" | custom-call | flops 201326592 | bytes 5767168 | tf_op jit(solution)/shard_map/coupling_and_step/pallas_call | solution.py:241
  119.9 15.2 %all_to_all.15.step_ref = bf16[16,128,128]{2,1,0:T(8,128)(2,1)S(1)} all-to-all(bf16[16,128,128]{2,1,0:T(8,128)(2,1)S(1)} %get-tuple-element.49), channel_id=1, replica_groups=mesh['section'=8,'row'=16] {'section'}, dimensions={0} | all-to-all | bytes 1048576 | tf_op jit(solution)/shard_map/all_to_all | solution.py:375
  135.1 1.2 run_chains.1
  136.4 12.8 %all_to_all.16 = bf16[16,128,128]{2,1,0:T(8,128)(2,1)S(1)} all-to-all(bf16[16,128,128]{2,1,0:T(8,128)(2,1)S(1)} %run_chains.1), channel_id=1, replica_groups=mesh['section'=8,'row'=16] {'section'}, dimensions={0} | all-to-all | bytes 1048576 | tf_op jit(solution)/shard_map/all_to_all | solution.py:377
  149.2 1.1 convert_element_type.59
  (43 shorter events, 0.1 us)
Async XLA Ops:
  0.6 84.4 %copy-start = (f32[16,128,128]{2,1,0:T(8,128)S(1)}, f32[16,128,128]{2,1,0:T(8,128)}, u32[]{:S(2)}) copy-start(f32[16,128,128]{2,1,0:T(8,128)} %param.27) | copy-start | bytes 3145732
  2.1 2.2 %copy-start.1 = (bf16[128,128,128]{2,1,0:T(8,128)(2,1)S(1)}, bf16[128,128,128]{2,1,0:T(8,128)(2,1)}, u32[]{:S(2)}) copy-start(bf16[128,128,128]{2,1,0:T(8,128)(2,1)} %left_ref.4) | copy-start | bytes 12582916
  4.3 2.2 %copy-start.2 = (bf16[128,128,128]{2,1,0:T(8,128)(2,1)S(1)}, bf16[128,128,128]{2,1,0:T(8,128)(2,1)}, u32[]{:S(2)}) copy-start(bf16[128,128,128]{2,1,0:T(8,128)(2,1)} %right_ref.4) | copy-start | bytes 12582916
  6.5 0.9 copy-start.6
  7.4 0.7 copy-start.11
  16.1 30.5 %collective-permute-start.10 = (bf16[16,128,128]{2,1,0:T(8,128)(2,1)S(1)}, bf16[16,128,128]{2,1,0:T(8,128)(2,1)S(1)}, u32[]{:S(2)}, u32[]{:S(2)}) collective-permute-start(bf16[16,128,128]{2,1,0:T(8,128)(2,1)S(1)} %get-tuple-element.39), channel_id=1, source_target_pairs={{0,3},{1,0},{2,1},{3,2},{4,7},{5,4},{6,5},{7,6},{8,11},{9,8},{10,9... | collective-permute-start | bytes 1572872 | tf_op jit(solution)/shard_map/ppermute | solution.py:291
  22.2 27.2 %collective-permute-start.4 = (bf16[16,128,128]{2,1,0:T(8,128)(2,1)S(1)}, bf16[16,128,128]{2,1,0:T(8,128)(2,1)S(1)}, u32[]{:S(2)}, u32[]{:S(2)}) collective-permute-start(bf16[16,128,128]{2,1,0:T(8,128)(2,1)S(1)} %get-tuple-element.33), channel_id=1, source_target_pairs={{0,12},{1,13},{2,14},{3,15},{4,0},{5,1},{6,2},{7,3},{8,4},{9,5},{1... | collective-permute-start | bytes 1572872 | tf_op jit(solution)/shard_map/ppermute | solution.py:291
  24.7 25.0 %collective-permute-start.6 = (bf16[16,128,128]{2,1,0:T(8,128)(2,1)S(1)}, bf16[16,128,128]{2,1,0:T(8,128)(2,1)S(1)}, u32[]{:S(2)}, u32[]{:S(2)}) collective-permute-start(bf16[16,128,128]{2,1,0:T(8,128)(2,1)S(1)} %get-tuple-element.35), channel_id=1, source_target_pairs={{0,1},{1,2},{2,3},{3,0},{4,5},{5,6},{6,7},{7,4},{8,9},{9,10},{10,1... | collective-permute-start | bytes 1572872 | tf_op jit(solution)/shard_map/ppermute | solution.py:291
  24.7 28.7 %collective-permute-start = (bf16[16,128,128]{2,1,0:T(8,128)(2,1)S(1)}, bf16[16,128,128]{2,1,0:T(8,128)(2,1)S(1)}, u32[]{:S(2)}, u32[]{:S(2)}) collective-permute-start(bf16[16,128,128]{2,1,0:T(8,128)(2,1)S(1)} %get-tuple-element.27), channel_id=1, source_target_pairs={{0,4},{1,5},{2,6},{3,7},{4,8},{5,9},{6,10},{7,11},{8,12},{9,13},{1... | collective-permute-start | bytes 1572872 | tf_op jit(solution)/shard_map/ppermute | solution.py:291
  36.5 23.4 %collective-permute-start.9 = (bf16[16,128,128]{2,1,0:T(8,128)(2,1)S(1)}, bf16[16,128,128]{2,1,0:T(8,128)(2,1)S(1)}, u32[]{:S(2)}, u32[]{:S(2)}) collective-permute-start(bf16[16,128,128]{2,1,0:T(8,128)(2,1)S(1)} %get-tuple-element.37), channel_id=1, source_target_pairs={{0,1},{1,2},{2,3},{3,0},{4,5},{5,6},{6,7},{7,4},{8,9},{9,10},{10,1... | collective-permute-start | bytes 1572872 | tf_op jit(solution)/shard_map/ppermute | solution.py:291
  46.6 17.2 %collective-permute-start.2 = (bf16[16,128,128]{2,1,0:T(8,128)(2,1)S(1)}, bf16[16,128,128]{2,1,0:T(8,128)(2,1)S(1)}, u32[]{:S(2)}, u32[]{:S(2)}) collective-permute-start(bf16[16,128,128]{2,1,0:T(8,128)(2,1)S(1)} %get-tuple-element.30), channel_id=1, source_target_pairs={{0,12},{1,13},{2,14},{3,15},{4,0},{5,1},{6,2},{7,3},{8,4},{9,5},{1... | collective-permute-start | bytes 1572872 | tf_op jit(solution)/shard_map/ppermute | solution.py:291
  49.4 14.4 %collective-permute-start.3 = (bf16[16,128,128]{2,1,0:T(8,128)(2,1)S(1)}, bf16[16,128,128]{2,1,0:T(8,128)(2,1)S(1)}, u32[]{:S(2)}, u32[]{:S(2)}) collective-permute-start(bf16[16,128,128]{2,1,0:T(8,128)(2,1)S(1)} %get-tuple-element.31), channel_id=1, source_target_pairs={{0,4},{1,5},{2,6},{3,7},{4,8},{5,9},{6,10},{7,11},{8,12},{9,13},{1... | collective-permute-start | bytes 1572872 | tf_op jit(solution)/shard_map/ppermute | solution.py:291
  49.7 14.4 %collective-permute-start.8 = (bf16[16,128,128]{2,1,0:T(8,128)(2,1)S(1)}, bf16[16,128,128]{2,1,0:T(8,128)(2,1)S(1)}, u32[]{:S(2)}, u32[]{:S(2)}) collective-permute-start(bf16[16,128,128]{2,1,0:T(8,128)(2,1)S(1)} %get-tuple-element.36), channel_id=1, source_target_pairs={{0,3},{1,0},{2,1},{3,2},{4,7},{5,4},{6,5},{7,6},{8,11},{9,8},{10,9... | collective-permute-start | bytes 1572872 | tf_op jit(solution)/shard_map/ppermute | solution.py:291
  53.3 31.7 %copy-start.5 = (f32[16,128,128]{2,1,0:T(8,128)S(1)}, f32[16,128,128]{2,1,0:T(8,128)}, u32[]{:S(2)}) copy-start(f32[16,128,128]{2,1,0:T(8,128)} %diag_ref.1) | copy-start | bytes 3145732
  53.3 22.0 %collective-permute-start.11 = (bf16[16,128,128]{2,1,0:T(8,128)(2,1)S(1)}, bf16[16,128,128]{2,1,0:T(8,128)(2,1)S(1)}, u32[]{:S(2)}, u32[]{:S(2)}) collective-permute-start(bf16[16,128,128]{2,1,0:T(8,128)(2,1)S(1)} %add_convert_fusion), channel_id=1, source_target_pairs={{0,3},{1,0},{2,1},{3,2},{4,7},{5,4},{6,5},{7,6},{8,11},{9,8},{10,9... | collective-permute-start | bytes 1572872 | tf_op jit(solution)/shard_map/ppermute | solution.py:291
  59.9 15.3 %collective-permute-start.5 = (bf16[16,128,128]{2,1,0:T(8,128)(2,1)S(1)}, bf16[16,128,128]{2,1,0:T(8,128)(2,1)S(1)}, u32[]{:S(2)}, u32[]{:S(2)}) collective-permute-start(bf16[16,128,128]{2,1,0:T(8,128)(2,1)S(1)} %add_convert_fusion.2), channel_id=1, source_target_pairs={{0,12},{1,13},{2,14},{3,15},{4,0},{5,1},{6,2},{7,3},{8,4},{9,5},{1... | collective-permute-start | bytes 1572872 | tf_op jit(solution)/shard_map/ppermute | solution.py:291
  63.8 12.7 %collective-permute-start.7 = (bf16[16,128,128]{2,1,0:T(8,128)(2,1)S(1)}, bf16[16,128,128]{2,1,0:T(8,128)(2,1)S(1)}, u32[]{:S(2)}, u32[]{:S(2)}) collective-permute-start(bf16[16,128,128]{2,1,0:T(8,128)(2,1)S(1)} %add_convert_fusion.1), channel_id=1, source_target_pairs={{0,1},{1,2},{2,3},{3,0},{4,5},{5,6},{6,7},{7,4},{8,9},{9,10},{10,1... | collective-permute-start | bytes 1572872 | tf_op jit(solution)/shard_map/ppermute | solution.py:291
  63.8 12.7 %collective-permute-start.1 = (bf16[16,128,128]{2,1,0:T(8,128)(2,1)S(1)}, bf16[16,128,128]{2,1,0:T(8,128)(2,1)S(1)}, u32[]{:S(2)}, u32[]{:S(2)}) collective-permute-start(bf16[16,128,128]{2,1,0:T(8,128)(2,1)S(1)} %add_convert_fusion.3.order_ref), channel_id=1, source_target_pairs={{0,4},{1,5},{2,6},{3,7},{4,8},{5,9},{6,10},{7,11},{8,12},{9,13},{1... | collective-permute-start | bytes 1572872 | tf_op jit(solution)/shard_map/ppermute | solution.py:291
  76.5 24.1 %copy-start.7 = (bf16[4,128,128]{2,1,0:T(8,128)(2,1)S(1)}, bf16[4,128,128]{2,1,0:T(8,128)(2,1)}, u32[]{:S(2)}) copy-start(bf16[4,128,128]{2,1,0:T(8,128)(2,1)} %table_ref.5) | copy-start | bytes 393220
  76.5 24.1 %copy-start.12 = (s32[128]{0:T(128)S(1)}, s32[128]{0:T(128)}, u32[]{:S(2)}) copy-start(s32[128]{0:T(128)} %pivot_ref.5) | copy-start | bytes 1540
  76.6 24.1 %copy-start.13 = (s32[128]{0:T(128)S(1)}, s32[128]{0:T(128)}, u32[]{:S(2)}) copy-start(s32[128]{0:T(128)} %target_ref.1) | copy-start | bytes 1540
  78.2 0.7 copy-start.9
  78.9 0.7 copy-start.14
  79.6 0.7 copy-start.15
  80.3 0.7 copy-start.16
  81.0 0.7 copy-start.17
  81.8 0.7 copy-start.18
  82.5 16.5 %collective-permute-start.12 = (bf16[8,128,128]{2,1,0:T(8,128)(2,1)}, bf16[8,128,128]{2,1,0:T(8,128)(2,1)}, u32[]{:S(2)}, u32[]{:S(2)}) collective-permute-start(bf16[8,128,128]{2,1,0:T(8,128)(2,1)} %bitcast.13), channel_id=1, source_target_pairs={{0,2},{1,3},{2,0},{3,1},{4,6},{5,7},{6,4},{7,5},{8,10},{9,11},{10,... | collective-permute-start | bytes 786440 | tf_op jit(solution)/shard_map/ppermute | solution.py:291
  88.1 31.8 %all-to-all-start.1 = ((bf16[16,128,128]{2,1,0:T(8,128)(2,1)}), bf16[16,128,128]{2,1,0:T(8,128)(2,1)S(1)}, u32[]{:S(2)}, u32[]{:S(2)}) async-start(bf16[16,128,128]{2,1,0:T(8,128)(2,1)} %convolution_convert_fusion), calls=%async_computation.1 | async-start | bytes 1048576 | tf_op jit(solution)/shard_map/all_to_all | solution.py:362
  95.2 19.4 %collective-permute-start.13 = (bf16[8,128,128]{2,1,0:T(8,128)(2,1)}, bf16[8,128,128]{2,1,0:T(8,128)(2,1)S(1)}, u32[]{:S(2)}, u32[]{:S(2)}) collective-permute-start(bf16[8,128,128]{2,1,0:T(8,128)(2,1)} %bitcast.53), channel_id=1, source_target_pairs={{0,1},{1,2},{2,3},{3,0},{4,5},{5,6},{6,7},{7,4},{8,9},{9,10},{10,1... | collective-permute-start | bytes 786440 | tf_op jit(solution)/shard_map/ppermute | solution.py:291
  96.6 18.0 %collective-permute-start.14 = (bf16[8,128,128]{2,1,0:T(8,128)(2,1)}, bf16[8,128,128]{2,1,0:T(8,128)(2,1)S(1)}, u32[]{:S(2)}, u32[]{:S(2)}) collective-permute-start(bf16[8,128,128]{2,1,0:T(8,128)(2,1)} %bitcast.52), channel_id=1, source_target_pairs={{0,3},{1,0},{2,1},{3,2},{4,7},{5,4},{6,5},{7,6},{8,11},{9,8},{10,9... | collective-permute-start | bytes 786440 | tf_op jit(solution)/shard_map/ppermute | solution.py:291
  97.9 16.7 %collective-permute-start.15 = (bf16[8,128,128]{2,1,0:T(8,128)(2,1)}, bf16[8,128,128]{2,1,0:T(8,128)(2,1)S(1)}, u32[]{:S(2)}, u32[]{:S(2)}) collective-permute-start(bf16[8,128,128]{2,1,0:T(8,128)(2,1)} %bitcast.51), channel_id=1, source_target_pairs={{0,8},{1,9},{2,10},{3,11},{4,12},{5,13},{6,14},{7,15},{8,0},{9,1},... | collective-permute-start | bytes 786440 | tf_op jit(solution)/shard_map/ppermute | solution.py:291
  97.9 16.7 %collective-permute-start.16 = (bf16[8,128,128]{2,1,0:T(8,128)(2,1)}, bf16[8,128,128]{2,1,0:T(8,128)(2,1)S(1)}, u32[]{:S(2)}, u32[]{:S(2)}) collective-permute-start(bf16[8,128,128]{2,1,0:T(8,128)(2,1)} %bitcast.50), channel_id=1, source_target_pairs={{0,4},{1,5},{2,6},{3,7},{4,8},{5,9},{6,10},{7,11},{8,12},{9,13},{1... | collective-permute-start | bytes 786440 | tf_op jit(solution)/shard_map/ppermute | solution.py:291
  98.9 15.7 %collective-permute-start.17 = (bf16[8,128,128]{2,1,0:T(8,128)(2,1)}, bf16[8,128,128]{2,1,0:T(8,128)(2,1)S(1)}, u32[]{:S(2)}, u32[]{:S(2)}) collective-permute-start(bf16[8,128,128]{2,1,0:T(8,128)(2,1)} %bitcast.49), channel_id=1, source_target_pairs={{0,12},{1,13},{2,14},{3,15},{4,0},{5,1},{6,2},{7,3},{8,4},{9,5},{1... | collective-permute-start | bytes 786440 | tf_op jit(solution)/shard_map/ppermute | solution.py:291
  100.6 2.2 %copy-start.3 = (bf16[128,128,128]{2,1,0:T(8,128)(2,1)S(1)}, bf16[128,128,128]{2,1,0:T(8,128)(2,1)}, u32[]{:S(2)}) copy-start(bf16[128,128,128]{2,1,0:T(8,128)(2,1)} %left_ref.5) | copy-start | bytes 12582916
  102.8 2.2 %copy-start.4 = (bf16[128,128,128]{2,1,0:T(8,128)(2,1)S(1)}, bf16[128,128,128]{2,1,0:T(8,128)(2,1)}, u32[]{:S(2)}) copy-start(bf16[128,128,128]{2,1,0:T(8,128)(2,1)} %right_ref.5) | copy-start | bytes 12582916
  105.0 1.0 copy-start.8
  106.0 8.6 %copy-start.10 = (bf16[2,4,128,128]{3,2,1,0:T(8,128)(2,1)S(1)}, bf16[2,4,128,128]{3,2,1,0:T(8,128)(2,1)}, u32[]{:S(2)}) copy-start(bf16[2,4,128,128]{3,2,1,0:T(8,128)(2,1)} %copy-done.9) | copy-start | bytes 786436

commit v2 on v1

v2 whole, which is shorter than its diff:
```python
import functools

import jax
import jax.numpy as jnp
from jax import lax
from jax.experimental import pallas as pl
from jax.experimental.pallas import tpu as pltpu
from jax.sharding import PartitionSpec as P

B = 128
SIDE = 4
UNROLL = 16
CHUNKS = 8
CELL_MASK, PIVOT_BIT, FAR_BIT, NEAR_BIT, SLOT_BIT = 511, 9, 16, 17, 20
MIB = 1 << 20

ANY = pl.BlockSpec(memory_space=pl.ANY)
HBM = pl.BlockSpec(memory_space=pltpu.HBM)
VMEM = pl.BlockSpec(memory_space=pltpu.VMEM)
SMEM = pl.BlockSpec(memory_space=pltpu.SMEM)

bf16 = jnp.bfloat16
f32 = jnp.float32


def mm(a, b):
    return jnp.dot(a, b, preferred_element_type=f32)


def mm_nt(a, b):
    return lax.dot_general(a, b, (((1,), (1,)), ((), ())), preferred_element_type=f32)


def split(x):
    high = x.astype(bf16)
    return high, (x - high.astype(f32)).astype(bf16)


def stay(x):
    return pltpu.with_memory_space_constraint(x, pltpu.HBM)


def bulk(left_ref, right_ref, left, right, lsem, rsem):
    per = left.shape[0] // CHUNKS
    pairs = []
    for k in range(CHUNKS):
        part = pl.ds(k * per, per)
        pair = (
            pltpu.make_async_copy(left_ref.at[part], left.at[part], lsem.at[k]),
            pltpu.make_async_copy(right_ref.at[part], right.at[part], rsem.at[k]),
        )
        for c in pair:
            c.start()
        pairs.append(pair)
    return pairs


def cross_kernel(first, sizes, flag, index_ref, table_ref, left_ref, right_ref, *refs):
    outs = refs[-8 - len(sizes) : -8]
    listed, left, right, total, table, lsem, rsem, tsem = refs[-8:]
    cells = sum(sizes)
    slots = left.shape[0]
    table_copy = pltpu.make_async_copy(table_ref, table, tsem)
    table_copy.start()
    pairs = bulk(left_ref, right_ref, left, right, lsem, rsem)

    def note(i, n):
        word = index_ref[i]
        listed[n] = word
        return n + ((word >> flag) & 1)

    count = lax.fori_loop(0, slots, note, 0, unroll=32)
    for u in range(UNROLL):
        listed[count + u] = first + cells

    def clear(c, _):
        total[c] = jnp.zeros((B, B), bf16)
        return 0

    lax.fori_loop(0, cells + 1, clear, 0, unroll=8)
    table_copy.wait()
    for pair in pairs:
        for c in pair:
            c.wait()

    def work(r, _):
        words = [listed[r * UNROLL + u] for u in range(UNROLL)]
        scaled = [mm(left[w >> SLOT_BIT], table[(w >> PIVOT_BIT) & 3]).astype(bf16) for w in words]
        updates = [mm(x, right[w >> SLOT_BIT]) for x, w in zip(scaled, words)]
        for w, u in zip(words, updates):
            c = (w & CELL_MASK) - first
            total[c] = (total[c].astype(f32) + u).astype(bf16)
        return 0

    lax.fori_loop(0, (count + UNROLL - 1) // UNROLL, work, 0)

    start = 0
    for out, size in zip(outs, sizes):

        def give(c, _, out=out, start=start):
            out[c] = total[start + c]
            return 0

        lax.fori_loop(0, size, give, 0, unroll=8)
        start += size


def cross_sums(first, sizes, flag, index, table, left, right, live, order=()):
    cells = sum(sizes)
    slots = left.shape[0]
    return pl.pallas_call(
        functools.partial(cross_kernel, first, sizes, flag),
        out_shape=[jax.ShapeDtypeStruct((n, B, B), bf16) for n in sizes],
        in_specs=[SMEM, HBM, HBM, HBM] + [ANY] * len(order),
        out_specs=[VMEM] * len(sizes),
        scratch_shapes=[
            pltpu.SMEM((slots + UNROLL,), jnp.int32),
            pltpu.VMEM((slots, B, B), bf16),
            pltpu.VMEM((slots, B, B), bf16),
            pltpu.VMEM((cells + 1, B, B), bf16),
            pltpu.VMEM(table.shape, bf16),
            pltpu.SemaphoreType.DMA((CHUNKS,)),
            pltpu.SemaphoreType.DMA((CHUNKS,)),
            pltpu.SemaphoreType.DMA,
        ],
        compiler_params=pltpu.CompilerParams(vmem_limit_bytes=9 * MIB + cells * 4 * B * B),
        cost_estimate=pl.CostEstimate(
            flops=live * 4 * B**3, bytes_accessed=slots * 4 * B * B + cells * 2 * B * B, transcendentals=0
        ),
        name="cross_sums",
    )(index, stay(table), stay(left), stay(right), *order)


def offset_kernel(diag_ref, seed_ref, out_ref, held, sem):
    rows = held.shape[0]
    group = rows // 2
    copies = []
    for g in range(2):

        def one(i, _, g=g):
            r = g * group + i
            dh, dl = split(diag_ref[r])
            sh, sl = split(seed_ref[r])
            held[r] = (mm_nt(sh, dh) + (mm_nt(sh, dl) + mm_nt(sl, dh))).astype(bf16)
            return 0

        lax.fori_loop(0, group, one, 0, unroll=4)
        part = pl.ds(g * group, group)
        copies.append(pltpu.make_async_copy(held.at[part], out_ref.at[part], sem.at[g]))
        copies[-1].start()
    for c in copies:
        c.wait()


def offsets_of(diag, seed):
    rows = diag.shape[0]
    return pl.pallas_call(
        offset_kernel,
        out_shape=jax.ShapeDtypeStruct((rows, B, B), bf16),
        in_specs=[VMEM, VMEM],
        out_specs=HBM,
        scratch_shapes=[pltpu.VMEM((rows, B, B), bf16), pltpu.SemaphoreType.DMA((2,))],
        compiler_params=pltpu.CompilerParams(vmem_limit_bytes=4 * MIB),
        cost_estimate=pl.CostEstimate(flops=rows * 6 * B**3, bytes_accessed=rows * 10 * B * B, transcendentals=0),
        name="offsets",
    )(diag, seed)


def local_kernel(index_ref, table_ref, coupling_ref, left_ref, right_ref, *refs):
    base_ref, left, right, table, lsem, rsem, tsem = refs[-7:]
    slots = left.shape[0]
    rows = coupling_ref.shape[0]
    table_copy = pltpu.make_async_copy(table_ref, table, tsem)
    table_copy.start()
    pairs = bulk(left_ref, right_ref, left, right, lsem, rsem)
    for r in range(rows):
        base_ref[r] = coupling_ref[r].astype(f32)
    table_copy.wait()
    per = slots // CHUNKS
    for k, pair in enumerate(pairs):
        for c in pair:
            c.wait()

        def work(i, _, k=k):
            at = [k * per + i * UNROLL + u for u in range(UNROLL)]
            words = [index_ref[j] for j in at]
            scaled = [mm(left[j], table[(w >> PIVOT_BIT) & 3]).astype(bf16) for j, w in zip(at, words)]
            updates = [mm(x, right[j]).astype(bf16).astype(f32) for x, j in zip(scaled, at)]
            for w, u in zip(words, updates):
                t = w & CELL_MASK
                base_ref[t] = base_ref[t] - u
            return 0

        lax.fori_loop(0, per // UNROLL, work, 0)


def local_sums(index, table, coupling, left, right, order):
    slots = left.shape[0]
    rows = coupling.shape[0]
    return pl.pallas_call(
        local_kernel,
        out_shape=jax.ShapeDtypeStruct((rows, B, B), f32),
        in_specs=[SMEM, HBM, VMEM, HBM, HBM] + [ANY] * len(order),
        out_specs=VMEM,
        scratch_shapes=[
            pltpu.VMEM((slots, B, B), bf16),
            pltpu.VMEM((slots, B, B), bf16),
            pltpu.VMEM(table.shape, bf16),
            pltpu.SemaphoreType.DMA((CHUNKS,)),
            pltpu.SemaphoreType.DMA((CHUNKS,)),
            pltpu.SemaphoreType.DMA,
        ],
        compiler_params=pltpu.CompilerParams(vmem_limit_bytes=12 * MIB),
        cost_estimate=pl.CostEstimate(
            flops=slots * 4 * B**3, bytes_accessed=slots * 4 * B * B + rows * 6 * B * B, transcendentals=0
        ),
        name="local_sums",
    )(index, stay(table), coupling, stay(left), stay(right), *order)


def first_totals_kernel(own_x, own_z, *refs):
    arrivals = refs[:8]
    outs = refs[-2 * SIDE :]
    q = arrivals[0].shape[0] // SIDE
    for s, own in enumerate((own_x, own_z)):
        for half in range(2):
            for b in range(SIDE):
                t = own[pl.ds((half * SIDE + b) * q, q)].astype(f32)
                for a in arrivals[s * 4 + half * 2 : s * 4 + half * 2 + 2]:
                    t = t + a[pl.ds(b * q, q)].astype(f32)
                outs[s * SIDE + b][pl.ds(half * q, q)] = t.astype(bf16)


def first_totals(own_x, own_z, arrivals, order):
    half = own_x.shape[0] // SIDE
    outs = pl.pallas_call(
        first_totals_kernel,
        out_shape=[jax.ShapeDtypeStruct((half, B, B), bf16)] * (2 * SIDE),
        in_specs=[VMEM] * 10 + [ANY] * len(order),
        out_specs=[VMEM] * (2 * SIDE),
        compiler_params=pltpu.CompilerParams(vmem_limit_bytes=9 * MIB),
        cost_estimate=pl.CostEstimate(flops=0, bytes_accessed=256 * 2 * B * B, transcendentals=0),
        name="first_totals",
    )(own_x, own_z, *arrivals, *order)
    return outs[:SIDE], outs[SIDE:]


def coupling_kernel(base_ref, diag_ref, *refs):
    new_ref, step_ref = refs[8:]
    half = base_ref.shape[0] // 2
    for s in range(2):
        parts = refs[s * 4 : s * 4 + 4]

        def finish(i, _, s=s, parts=parts):
            r = s * half + i
            t = base_ref[r]
            for p in parts:
                t = t - p[i].astype(f32)
            new_ref[r] = t
            th, tl = split(t)
            dh, dl = split(diag_ref[r])
            step_ref[r] = -(mm(dh, th) + (mm(dh, tl) + mm(dl, th))).astype(bf16)
            return 0

        lax.fori_loop(0, half, finish, 0, unroll=4)


def coupling_and_step(base, diag, parts_x, parts_z):
    rows = base.shape[0]
    return pl.pallas_call(
        coupling_kernel,
        out_shape=[jax.ShapeDtypeStruct((rows, B, B), f32), jax.ShapeDtypeStruct((rows, B, B), bf16)],
        in_specs=[VMEM] * 10,
        out_specs=[VMEM, VMEM],
        compiler_params=pltpu.CompilerParams(vmem_limit_bytes=7 * MIB),
        cost_estimate=pl.CostEstimate(flops=rows * 6 * B**3, bytes_accessed=rows * 22 * B * B, transcendentals=0),
        name="coupling_and_step",
    )(base, diag, *parts_x, *parts_z)


def chain_kernel(sections, chains, step_ref, offset_ref, out_ref):
    current = []
    for j in range(chains):
        k = (sections - 1) * chains + j
        o = offset_ref[k]
        out_ref[k] = o
        current.append(o.astype(f32))
    for s in range(sections - 2, -1, -1):
        for j in range(chains):
            k = s * chains + j
            high, low = split(current[j])
            m = step_ref[k]
            new = offset_ref[k].astype(f32) + (mm_nt(high, m) + mm_nt(low, m))
            out_ref[k] = new.astype(bf16)
            current[j] = new


def run_chains(sections, steps, offsets):
    rows = steps.shape[0]
    return pl.pallas_call(
        functools.partial(chain_kernel, sections, rows // sections),
        out_shape=jax.ShapeDtypeStruct((rows, B, B), bf16),
        in_specs=[VMEM, VMEM],
        out_specs=VMEM,
        compiler_params=pltpu.CompilerParams(vmem_limit_bytes=4 * MIB),
        cost_estimate=pl.CostEstimate(flops=rows * 4 * B**3, bytes_accessed=rows * 6 * B * B, transcendentals=0),
        name="run_chains",
    )(steps, offsets)


def moved(x, along, by):
    pairs = []
    for a in range(SIDE):
        for c in range(SIDE):
            if along == 0:
                pairs.append((a * SIDE + c, (a + by) % SIDE * SIDE + c))
            else:
                pairs.append((a * SIDE + c, a * SIDE + (c + by) % SIDE))
    return lax.ppermute(x, "row", pairs)


def add(a, b):
    return (a.astype(f32) + b.astype(f32)).astype(bf16)


def per_device(
    coupling,
    diag_inverse,
    pivot_inverse,
    cross_left,
    cross_right,
    cross_pivot,
    cross_owner,
    foreign_target_row,
    cross_count,
    local_left,
    local_right,
    local_pivot,
    local_target,
    adjoint_seed,
):
    sections = lax.axis_size("section")
    rows = coupling.shape[0]
    slots = cross_left.shape[0]
    half = rows // 2
    quarter = rows // 4
    me = lax.axis_index("row")

    owner = cross_owner[:, 0]
    dx = (owner // SIDE - me // SIDE) % SIDE
    dz = (owner % SIDE - me % SIDE) % SIDE
    second = foreign_target_row // half
    row = foreign_target_row % half
    a = jnp.where(second == 0, dx, dz)
    b = jnp.where(second == 0, dz, dx)
    upper = row // quarter
    spot = b * quarter + row % quarter
    n = SIDE * quarter
    group = 4 * n
    minus = (a == 3).astype(jnp.int32)
    cell = jnp.where(
        a == 2,
        second * 2 * n + upper * n + spot,
        jnp.where(
            a == 0,
            3 * group + second * 2 * n + upper * n + spot,
            jnp.where(minus == upper, 2 * group, group) + second * 2 * n + minus * n + spot,
        ),
    )
    slot = jnp.arange(slots, dtype=jnp.int32)
    live = slot < cross_count[0]
    word = cell | (cross_pivot << PIVOT_BIT) | (slot << SLOT_BIT)
    word = word | jnp.where(live, jnp.where(cell < group, 1 << FAR_BIT, 1 << NEAR_BIT), 0)
    local_word = local_target | (local_pivot << PIVOT_BIT)

    step_offset = offsets_of(diag_inverse, adjoint_seed)
    every = lax.all_gather(step_offset, "section", axis=0, tiled=False)
    chains = rows // sections

    sums = functools.partial(cross_sums, index=word, table=pivot_inverse, left=cross_left, right=cross_right)
    far = sums(0, [n] * 4, FAR_BIT, live=slots // 4, order=[step_offset])
    ways = ((0, 1), (0, -1), (1, 1), (1, -1))
    far_in = [moved(x, *w) for x, w in zip(far, ways)]
    near = sums(group, [n] * 8 + [2 * n] * 2, NEAR_BIT, live=slots * 3 // 4)
    free_in = [moved(x, *w) for x, w in zip(near[:4], ways)]
    joined = [add(x, y) for x, y in zip(near[4:8], far_in)]
    joined_in = [moved(x, *w) for x, w in zip(joined, ways)]

    base = local_sums(local_word, pivot_inverse, coupling, local_left, local_right, joined)

    arrivals = []
    for s in range(2):
        fp, fm = free_in[2 * s : 2 * s + 2]
        jp, jm = joined_in[2 * s : 2 * s + 2]
        arrivals += [jp, fm, fp, jm]
    tot_x, tot_z = first_totals(near[8], near[9], arrivals, [base])
    parts_x = [tot_x[0]] + [moved(tot_x[k], 1, k) for k in (2, 1, 3)]
    parts_z = [tot_z[0]] + [moved(tot_z[k], 0, k) for k in (2, 1, 3)]
    updated, step_matrix = coupling_and_step(base, diag_inverse, parts_x, parts_z)
    steps = lax.all_to_all(step_matrix, "section", split_axis=0, concat_axis=0, tiled=True)
    offsets = lax.dynamic_slice_in_dim(every, lax.axis_index("section") * chains, chains, axis=1)
    offsets = offsets.reshape(rows, B, B)
    solved = run_chains(sections, steps, offsets)
    adjoint = lax.all_to_all(solved, "section", split_axis=0, concat_axis=0, tiled=True).astype(f32)
    return (updated, adjoint)


def solution(mesh):
    spread = ("section", "row")
    block = P(spread, None, None)
    line = P(spread)
    return jax.shard_map(
        per_device,
        mesh=mesh,
        in_specs=(
            block,
            block,
            block,
            block,
            block,
            line,
            P(spread, None),
            line,
            line,
            block,
            block,
            line,
            line,
            block,
        ),
        out_specs=(block, block),
        check_vma=False,
    )
```

time: 152 us -> 122 us (0.80)
  blocking collectives: 28 us -> 12.6 us
  starting transfers between devices: 45.3 us -> 30.2 us
  waiting for transfers between devices: 17.7 us -> 31.1 us
  between operations: 1.61 us -> 14.9 us
  local copies, waits for them, and re-layouts: 15.6 us -> 3.55 us
  Pallas kernels: 36.6 us -> 26.4 us
  matrix products: 3.1 us -> 0 us
    ppermute x18, starting transfers between devices: 38.1 us -> 21.3 us  [moved(): return lax.ppermute(x, 'row', pairs)]
    all_to_all x1 -> x0, blocking collectives: 15.2 us -> none  [per_device(): lax.all_to_all(step_matrix, 'section', split_axis=0, concat_axis=0, tiled...]
    unnamed x38 -> x12, local copies, waits for them, and re-layouts: 15.6 us -> 2.47 us
    pallas_call x5 -> x6, Pallas kernels: 35.4 us -> 25.2 us  [the longest x2 12.6 us: cross_sums(): pl.pallas_call(functools.partial(cross_kernel, first, sizes, flag), out_s...]
    all_to_all x1, waiting for transfers between devices: 0.01 us -> 8.4 us  [per_device(): lax.all_to_all(step_matrix, 'section', split_axis=0, concat_axis=0, tiled...]
    ppermute x18, waiting for transfers between devices: 17.7 us -> 22.7 us  [moved(): return lax.ppermute(x, 'row', pairs)]
    dot_general x1 -> x0, matrix products: 3.1 us -> none  [per_device(): jnp.einsum('kab,knb->kna', diag_inverse, adjoint_seed, precision=precise)]
    all_to_all x1, starting transfers between devices: 7.15 us -> 8.85 us  [per_device(): lax.all_to_all(step_matrix, 'section', split_axis=0, concat_axis=0, tiled...]
  transfers between devices with their start and end apart: 19 -> 20, of which waited for: 5 -> 7; matrix products, arithmetic and copies ran while one was open for 2% -> 2% of each run, Pallas kernels for 17% -> 19%
where the time goes in v2:
time: 122 us; the launch traced here: 121 us
  waiting for transfers between devices  31.1 us (25%)
  starting transfers between devices  30.2 us (25%)
  Pallas kernels  26.4 us (22%)
  between operations  14.9 us (12%)
  blocking collectives  12.6 us (10%)
  local copies, waits for them, and re-layouts  3.55 us (3%)
  other arithmetic  2.36 us (2%)
    ppermute x18, waiting for transfers between devices, moved(): return lax.ppermute(x, 'row', pairs)  22.7 us
    ppermute x18, starting transfers between devices, moved(): return lax.ppermute(x, 'row', pairs)  21.3 us
    pallas_call x2, Pallas kernels, cross_sums(): pl.pallas_call(functools.partial(cross_kernel, first, sizes, flag), out_s...  12.6 us
    all_to_all x1, blocking collectives, per_device(): lax.all_to_all(solved, 'section', split_axis=0, concat_axis=0, tiled=True)  12.6 us
    all_to_all x1, starting transfers between devices, per_device(): lax.all_to_all(step_matrix, 'section', split_axis=0, concat_axis=0, tiled...  8.85 us
    all_to_all x1, waiting for transfers between devices, per_device(): lax.all_to_all(step_matrix, 'section', split_axis=0, concat_axis=0, tiled...  8.4 us
    pallas_call x1, Pallas kernels, local_sums(): pl.pallas_call(local_kernel, out_shape=jax.ShapeDtypeStruct((rows, B, B),...  7.39 us
    unnamed x12, local copies, waits for them, and re-layouts  2.47 us
  transfers between devices with their start and end apart: 20, of which 7 were waited for; matrix products, arithmetic and copies ran while one was open for 2% of the time, Pallas kernels for 19%

profile of v2, /device:TPU:1, one launch (start us, length us, event | category | flops | bytes accessed | tf_op | source)
XLA Modules:
  0.0 121.2 jit_solution(6143530297371975426)
XLA Ops:
  7.2 0.0 all-gather.3.cloned.1.call-start
  7.2 0.0 copy-start
  7.2 1.2 %copy-done = f32[16,128,128]{2,1,0:T(8,128)S(1)} copy-done((f32[16,128,128]{2,1,0:T(8,128)S(1)}, f32[16,128,128]{2,1,0:T(8,128)}, u32[]{:S(2)}) %copy-start) | copy-done | bytes 1048600
  8.4 1.2 %copy-done.2 = f32[16,128,128]{2,1,0:T(8,128)S(1)} copy-done((f32[16,128,128]{2,1,0:T(8,128)S(1)}, f32[16,128,128]{2,1,0:T(8,128)}, u32[]{:S(2)}) %copy-start.2) | copy-done | bytes 1048600
  9.7 2.3 %offsets.1.refs_0_ = bf16[16,128,128]{2,1,0:T(8,128)(2,1)} custom-call(f32[16,128,128]{2,1,0:T(8,128)S(1)} %copy-done, f32[16,128,128]{2,1,0:T(8,128)S(1)} %copy-done.2), custom_call_target="tpu_custom_call" | custom-call | flops 201326592 | bytes 2621440 | tf_op jit(solution)/shard_map/offsets/pallas_call | solution.py:157
  11.9 0.0 all-gather.3.cloned.1.call-update
  12.6 0.7 fusion.6.index_ref
  13.4 5.2 %cross_sums.3 = (bf16[16,128,128]{2,1,0:T(8,128)(2,1)S(1)}, bf16[16,128,128]{2,1,0:T(8,128)(2,1)S(1)}, bf16[16,128,128]{2,1,0:T(8,128)(2,1)S(1)}, bf16[16,128,128]{2,1,0:T(8,128)(2,1)S(1)}) custom-call(s32[128]{0:T(128)S(1)} %fusion.6.index_ref, bf16[4,128,128]{2,1,0:T(8,128)(2,1)} %table_ref.5, bf16[128,128,128]{2,1,0:T(8,128)(2,1)} %left_ref.4, ...), custom_call_target="tpu_custom_call" | custom-call | flops 268435456 | bytes 10485760 | tf_op jit(solution)/shard_map/cross_sums/pallas_call | solution.py:111
  18.6 4.7 %collective-permute-start.3 = (bf16[16,128,128]{2,1,0:T(8,128)(2,1)S(1)}, bf16[16,128,128]{2,1,0:T(8,128)(2,1)S(1)}, u32[]{:S(2)}, u32[]{:S(2)}) collective-permute-start(bf16[16,128,128]{2,1,0:T(8,128)(2,1)S(1)} %get-tuple-element.33), channel_id=1, source_target_pairs={{0,3},{1,0},{2,1},{3,2},{4,7},{5,4},{6,5},{7,6},{8,11},{9,8},{10,9... | collective-permute-start | bytes 1572872 | tf_op jit(solution)/shard_map/ppermute | solution.py:319
  23.2 0.0 collective-permute-start.2
  23.2 1.7 %collective-permute-start = (bf16[16,128,128]{2,1,0:T(8,128)(2,1)S(1)}, bf16[16,128,128]{2,1,0:T(8,128)(2,1)S(1)}, u32[]{:S(2)}, u32[]{:S(2)}) collective-permute-start(bf16[16,128,128]{2,1,0:T(8,128)(2,1)S(1)} %get-tuple-element.27), channel_id=1, source_target_pairs={{0,4},{1,5},{2,6},{3,7},{4,8},{5,9},{6,10},{7,11},{8,12},{9,13},{1... | collective-permute-start | bytes 1572872 | tf_op jit(solution)/shard_map/ppermute | solution.py:319
  24.9 1.0 collective-permute-start.1
  25.9 7.4 %cross_sums.2 = (bf16[16,128,128]{2,1,0:T(8,128)(2,1)S(1)}, bf16[16,128,128]{2,1,0:T(8,128)(2,1)S(1)}, bf16[16,128,128]{2,1,0:T(8,128)(2,1)S(1)}, bf16[16,128,12...) custom-call(s32[128]{0:T(128)S(1)} %fusion.6.index_ref, ...), custom_call_target="tpu_custom_call" | custom-call | flops 805306368 | bytes 14680064 | tf_op jit(solution)/shard_map/cross_sums/pallas_call | solution.py:111
  33.4 0.0 copy-start.4
  33.4 0.0 copy-start.5
  33.4 0.0 copy-start.3
  33.4 1.8 %collective-permute-start.5 = (bf16[16,128,128]{2,1,0:T(8,128)(2,1)S(1)}, bf16[16,128,128]{2,1,0:T(8,128)(2,1)S(1)}, u32[]{:S(2)}, u32[]{:S(2)}) collective-permute-start(bf16[16,128,128]{2,1,0:T(8,128)(2,1)S(1)} %get-tuple-element.36), channel_id=1, source_target_pairs={{0,12},{1,13},{2,14},{3,15},{4,0},{5,1},{6,2},{7,3},{8,4},{9,5},{1... | collective-permute-start | bytes 1572872 | tf_op jit(solution)/shard_map/ppermute | solution.py:319
  35.2 0.0 collective-permute-done.3
  35.2 0.8 collective-permute-start.6
  36.0 0.1 add_convert_fusion.refs_3_
  36.2 0.9 collective-permute-done.2
  37.0 2.7 %collective-permute-start.9 = (bf16[16,128,128]{2,1,0:T(8,128)(2,1)S(1)}, bf16[16,128,128]{2,1,0:T(8,128)(2,1)S(1)}, u32[]{:S(2)}, u32[]{:S(2)}) collective-permute-start(bf16[16,128,128]{2,1,0:T(8,128)(2,1)S(1)} %get-tuple-element.38), channel_id=1, source_target_pairs={{0,3},{1,0},{2,1},{3,2},{4,7},{5,4},{6,5},{7,6},{8,11},{9,8},{10,9... | collective-permute-start | bytes 1572872 | tf_op jit(solution)/shard_map/ppermute | solution.py:319
  39.8 0.1 add_convert_fusion.1.refs_2_
  39.9 0.1 collective-permute-start.10
  40.0 0.1 add_convert_fusion.2.refs_1_
  40.2 0.8 collective-permute-start.7
  41.0 0.1 add_convert_fusion.3.refs_0_
  41.1 7.7 %collective-permute-done.5.refs_1_ = bf16[16,128,128]{2,1,0:T(8,128)(2,1)S(1)} collective-permute-done((bf16[16,128,128]{2,1,0:T(8,128)(2,1)S(1)}, bf16[16,128,128]{2,1,0:T(8,128)(2,1)S(1)}, u32[]{:S(2)}, u32[]{:S(2)}) %collective-permute-start.5) | collective-permute-done | bytes 524320 | tf_op jit(solution)/shard_map/ppermute | solution.py:319
  48.8 0.2 collective-permute-start.4
  49.1 0.7 collective-permute-done.9.refs_5_
  49.8 3.4 %collective-permute-start.11 = (bf16[16,128,128]{2,1,0:T(8,128)(2,1)S(1)}, bf16[16,128,128]{2,1,0:T(8,128)(2,1)S(1)}, u32[]{:S(2)}, u32[]{:S(2)}) collective-permute-start(bf16[16,128,128]{2,1,0:T(8,128)(2,1)S(1)} %add_convert_fusion.refs_3_), channel_id=1, source_target_pairs={{0,3},{1,0},{2,1},{3,2},{4,7},{5,4},{6,5},{7,6},{8,11},{9,8},{10,9... | collective-permute-start | bytes 1572872 | tf_op jit(solution)/shard_map/ppermute | solution.py:319
  53.2 7.4 %local_sums.1.refs_8_.base_ref = f32[16,128,128]{2,1,0:T(8,128)S(1)} custom-call(s32[128]{0:T(128)S(1)} %shift-left_or_fusion.index_ref, bf16[4,128,128]{2,1,0:T(8,128)(2,1)} %table_ref.5, bf16[16,128,128]{2,1,0:T(8,128)(2,1)S(1)} %copy-done.3, bf16[128,128,128]{2,1,0:T(8,128)(2,1)} %left_ref.5, bf16[128,128,128]{2,1,0:T(8,128)(2,1)} %right_ref.5, ...), custom_call_target="tpu_custom_call" | custom-call | flops 1073741824 | bytes 9961472 | tf_op jit(solution)/shard_map/local_sums/pallas_call | solution.py:200
  60.6 0.0 copy-start.1
  60.7 3.1 %collective-permute-done.8.refs_4_ = bf16[16,128,128]{2,1,0:T(8,128)(2,1)S(1)} collective-permute-done((bf16[16,128,128]{2,1,0:T(8,128)(2,1)S(1)}, bf16[16,128,128]{2,1,0:T(8,128)(2,1)S(1)}, u32[]{:S(2)}, u32[]{:S(2)}) %collective-permute-start.8) | collective-permute-done | bytes 524320 | tf_op jit(solution)/shard_map/ppermute | solution.py:319
  63.8 0.7 first_totals.1
  64.5 0.3 collective-permute-start.12
  64.8 1.5 %collective-permute-start.13 = (bf16[8,128,128]{2,1,0:T(8,128)(2,1)S(1)}, bf16[8,128,128]{2,1,0:T(8,128)(2,1)S(1)}, u32[]{:S(2)}, u32[]{:S(2)}) collective-permute-start(bf16[8,128,128]{2,1,0:T(8,128)(2,1)S(1)} %get-tuple-element.42), channel_id=1, source_target_pairs={{0,1},{1,2},{2,3},{3,0},{4,5},{5,6},{6,7},{7,4},{8,9},{9,10},{10,1... | collective-permute-start | bytes 786440 | tf_op jit(solution)/shard_map/ppermute | solution.py:319
  66.3 1.3 %collective-permute-start.14 = (bf16[8,128,128]{2,1,0:T(8,128)(2,1)S(1)}, bf16[8,128,128]{2,1,0:T(8,128)(2,1)S(1)}, u32[]{:S(2)}, u32[]{:S(2)}) collective-permute-start(bf16[8,128,128]{2,1,0:T(8,128)(2,1)S(1)} %get-tuple-element.43), channel_id=1, source_target_pairs={{0,3},{1,0},{2,1},{3,2},{4,7},{5,4},{6,5},{7,6},{8,11},{9,8},{10,9... | collective-permute-start | bytes 786440 | tf_op jit(solution)/shard_map/ppermute | solution.py:319
  67.6 1.1 collective-permute-start.16
  68.6 3.0 %collective-permute-done.12.refs_1_ = bf16[8,128,128]{2,1,0:T(8,128)(2,1)S(1)} collective-permute-done((bf16[8,128,128]{2,1,0:T(8,128)(2,1)S(1)}, bf16[8,128,128]{2,1,0:T(8,128)(2,1)S(1)}, u32[]{:S(2)}, u32[]{:S(2)}) %collective-permute-start.12) | collective-permute-done | bytes 262176 | tf_op jit(solution)/shard_map/ppermute | solution.py:319
  71.6 7.2 %collective-permute-done.13.refs_2_ = bf16[8,128,128]{2,1,0:T(8,128)(2,1)S(1)} collective-permute-done((bf16[8,128,128]{2,1,0:T(8,128)(2,1)S(1)}, bf16[8,128,128]{2,1,0:T(8,128)(2,1)S(1)}, u32[]{:S(2)}, u32[]{:S(2)}) %collective-permute-start.13) | collective-permute-done | bytes 262176 | tf_op jit(solution)/shard_map/ppermute | solution.py:319
  78.9 2.2 %coupling_and_step.1 = (f32[16,128,128]{2,1,0:T(8,128)}, bf16[16,128,128]{2,1,0:T(8,128)(2,1)}) custom-call(f32[16,128,128]{2,1,0:T(8,128)S(1)} %local_sums.1.refs_8_.base_ref, f32[16,128,128]{2,1,0:T(8,128)S(1)} %copy-done.1, bf16[8,128,128]{2,1,0:T(8,128)(2,1)S(1)} %get-tuple-element.40.refs_0_, bf16[8,128,128]{2,1,0:T(8,128)(2,1)S(1)} %collective-permute-done.12.refs_1_, ...), custom_call_target="tpu_custom_call" | custom-call | flops 201326592 | bytes 5767168 | tf_op jit(solution)/shard_map/coupling_and_step/pallas_call | solution.py:270
  81.1 8.9 %all-to-all-start = ((bf16[16,128,128]{2,1,0:T(8,128)(2,1)}), bf16[16,128,128]{2,1,0:T(8,128)(2,1)S(1)}, u32[]{:S(2)}, u32[]{:S(2)}) async-start(bf16[16,128,128]{2,1,0:T(8,128)(2,1)} %get-tuple-element.49), calls=%async_computation | async-start | bytes 1048576 | tf_op jit(solution)/shard_map/all_to_all | solution.py:400
  89.9 1.1 constant_dynamic-slice_fusion
  91.0 8.4 %all-to-all-done.step_ref = bf16[16,128,128]{2,1,0:T(8,128)(2,1)S(1)} async-done(((bf16[16,128,128]{2,1,0:T(8,128)(2,1)}), bf16[16,128,128]{2,1,0:T(8,128)(2,1)S(1)}, u32[]{:S(2)}, u32[]{:S(2)}) %all-to-all-start) | async-done | bytes 524320 | tf_op jit(solution)/shard_map/all_to_all | solution.py:400
  99.4 1.2 %run_chains.1 = bf16[16,128,128]{2,1,0:T(8,128)(2,1)S(1)} custom-call(bf16[16,128,128]{2,1,0:T(8,128)(2,1)S(1)} %all-to-all-done.step_ref, bf16[16,128,128]{2,1,0:T(8,128)(2,1)S(1)} %bitcast.19), custom_call_target="tpu_custom_call" | custom-call | flops 134217728 | bytes 1572864 | tf_op jit(solution)/shard_map/run_chains/pallas_call | solution.py:300
  100.6 12.6 %all_to_all.10 = bf16[16,128,128]{2,1,0:T(8,128)(2,1)S(1)} all-to-all(bf16[16,128,128]{2,1,0:T(8,128)(2,1)S(1)} %run_chains.1), channel_id=1, replica_groups=mesh['section'=8,'row'=16] {'section'}, dimensions={0} | all-to-all | bytes 1048576 | tf_op jit(solution)/shard_map/all_to_all | solution.py:404
  113.2 1.1 convert_element_type.55
  (21 shorter events, 0.1 us)
Async XLA Ops:
  7.2 82.7 %all-gather.3.cloned.1.call-start = ((), (), s32[]{:S(2)}) async-start(), calls=%async_computation.2 | async-start | bytes 4718592 | tf_op jit(solution)/shard_map/all_gather | solution.py:377
  7.2 1.2 %copy-start = (f32[16,128,128]{2,1,0:T(8,128)S(1)}, f32[16,128,128]{2,1,0:T(8,128)}, u32[]{:S(2)}) copy-start(f32[16,128,128]{2,1,0:T(8,128)} %diag_ref.3) | copy-start | bytes 3145732
  8.4 1.2 %copy-start.2 = (f32[16,128,128]{2,1,0:T(8,128)S(1)}, f32[16,128,128]{2,1,0:T(8,128)}, u32[]{:S(2)}) copy-start(f32[16,128,128]{2,1,0:T(8,128)} %seed_ref.1) | copy-start | bytes 3145732
  18.6 16.7 %collective-permute-start.3 = (bf16[16,128,128]{2,1,0:T(8,128)(2,1)S(1)}, bf16[16,128,128]{2,1,0:T(8,128)(2,1)S(1)}, u32[]{:S(2)}, u32[]{:S(2)}) collective-permute-start(bf16[16,128,128]{2,1,0:T(8,128)(2,1)S(1)} %get-tuple-element.33), channel_id=1, source_target_pairs={{0,3},{1,0},{2,1},{3,2},{4,7},{5,4},{6,5},{7,6},{8,11},{9,8},{10,9... | collective-permute-start | bytes 1572872 | tf_op jit(solution)/shard_map/ppermute | solution.py:319
  23.2 13.8 %collective-permute-start.2 = (bf16[16,128,128]{2,1,0:T(8,128)(2,1)S(1)}, bf16[16,128,128]{2,1,0:T(8,128)(2,1)S(1)}, u32[]{:S(2)}, u32[]{:S(2)}) collective-permute-start(bf16[16,128,128]{2,1,0:T(8,128)(2,1)S(1)} %get-tuple-element.31), channel_id=1, source_target_pairs={{0,1},{1,2},{2,3},{3,0},{4,5},{5,6},{6,7},{7,4},{8,9},{9,10},{10,1... | collective-permute-start | bytes 1572872 | tf_op jit(solution)/shard_map/ppermute | solution.py:319
  23.2 16.9 %collective-permute-start = (bf16[16,128,128]{2,1,0:T(8,128)(2,1)S(1)}, bf16[16,128,128]{2,1,0:T(8,128)(2,1)S(1)}, u32[]{:S(2)}, u32[]{:S(2)}) collective-permute-start(bf16[16,128,128]{2,1,0:T(8,128)(2,1)S(1)} %get-tuple-element.27), channel_id=1, source_target_pairs={{0,4},{1,5},{2,6},{3,7},{4,8},{5,9},{6,10},{7,11},{8,12},{9,13},{1... | collective-permute-start | bytes 1572872 | tf_op jit(solution)/shard_map/ppermute | solution.py:319
  24.9 15.0 %collective-permute-start.1 = (bf16[16,128,128]{2,1,0:T(8,128)(2,1)S(1)}, bf16[16,128,128]{2,1,0:T(8,128)(2,1)S(1)}, u32[]{:S(2)}, u32[]{:S(2)}) collective-permute-start(bf16[16,128,128]{2,1,0:T(8,128)(2,1)S(1)} %get-tuple-element.29), channel_id=1, source_target_pairs={{0,12},{1,13},{2,14},{3,15},{4,0},{5,1},{6,2},{7,3},{8,4},{9,5},{1... | collective-permute-start | bytes 1572872 | tf_op jit(solution)/shard_map/ppermute | solution.py:319
  33.4 19.9 %copy-start.4 = (s32[128]{0:T(128)S(1)}, s32[128]{0:T(128)}, u32[]{:S(2)}) copy-start(s32[128]{0:T(128)} %param.26) | copy-start | bytes 1540
  33.4 19.8 %copy-start.5 = (s32[128]{0:T(128)S(1)}, s32[128]{0:T(128)}, u32[]{:S(2)}) copy-start(s32[128]{0:T(128)} %param.25) | copy-start | bytes 1540
  33.4 19.8 %copy-start.3 = (bf16[16,128,128]{2,1,0:T(8,128)(2,1)S(1)}, bf16[16,128,128]{2,1,0:T(8,128)(2,1)}, u32[]{:S(2)}) copy-start(bf16[16,128,128]{2,1,0:T(8,128)(2,1)} %coupling_ref.1) | copy-start | bytes 1572868
  33.4 15.4 %collective-permute-start.5 = (bf16[16,128,128]{2,1,0:T(8,128)(2,1)S(1)}, bf16[16,128,128]{2,1,0:T(8,128)(2,1)S(1)}, u32[]{:S(2)}, u32[]{:S(2)}) collective-permute-start(bf16[16,128,128]{2,1,0:T(8,128)(2,1)S(1)} %get-tuple-element.36), channel_id=1, source_target_pairs={{0,12},{1,13},{2,14},{3,15},{4,0},{5,1},{6,2},{7,3},{8,4},{9,5},{1... | collective-permute-start | bytes 1572872 | tf_op jit(solution)/shard_map/ppermute | solution.py:319
  35.2 13.8 %collective-permute-start.6 = (bf16[16,128,128]{2,1,0:T(8,128)(2,1)S(1)}, bf16[16,128,128]{2,1,0:T(8,128)(2,1)S(1)}, u32[]{:S(2)}, u32[]{:S(2)}) collective-permute-start(bf16[16,128,128]{2,1,0:T(8,128)(2,1)S(1)} %get-tuple-element.37), channel_id=1, source_target_pairs={{0,4},{1,5},{2,6},{3,7},{4,8},{5,9},{6,10},{7,11},{8,12},{9,13},{1... | collective-permute-start | bytes 1572872 | tf_op jit(solution)/shard_map/ppermute | solution.py:319
  37.0 12.8 %collective-permute-start.9 = (bf16[16,128,128]{2,1,0:T(8,128)(2,1)S(1)}, bf16[16,128,128]{2,1,0:T(8,128)(2,1)S(1)}, u32[]{:S(2)}, u32[]{:S(2)}) collective-permute-start(bf16[16,128,128]{2,1,0:T(8,128)(2,1)S(1)} %get-tuple-element.38), channel_id=1, source_target_pairs={{0,3},{1,0},{2,1},{3,2},{4,7},{5,4},{6,5},{7,6},{8,11},{9,8},{10,9... | collective-permute-start | bytes 1572872 | tf_op jit(solution)/shard_map/ppermute | solution.py:319
  39.9 20.7 %collective-permute-start.10 = (bf16[16,128,128]{2,1,0:T(8,128)(2,1)S(1)}, bf16[16,128,128]{2,1,0:T(8,128)(2,1)S(1)}, u32[]{:S(2)}, u32[]{:S(2)}) collective-permute-start(bf16[16,128,128]{2,1,0:T(8,128)(2,1)S(1)} %get-tuple-element.39), channel_id=1, source_target_pairs={{0,1},{1,2},{2,3},{3,0},{4,5},{5,6},{6,7},{7,4},{8,9},{9,10},{10,1... | collective-permute-start | bytes 1572872 | tf_op jit(solution)/shard_map/ppermute | solution.py:319
  40.2 20.5 %collective-permute-start.7 = (bf16[16,128,128]{2,1,0:T(8,128)(2,1)S(1)}, bf16[16,128,128]{2,1,0:T(8,128)(2,1)S(1)}, u32[]{:S(2)}, u32[]{:S(2)}) collective-permute-start(bf16[16,128,128]{2,1,0:T(8,128)(2,1)S(1)} %add_convert_fusion.2.refs_1_), channel_id=1, source_target_pairs={{0,12},{1,13},{2,14},{3,15},{4,0},{5,1},{6,2},{7,3},{8,4},{9,5},{1... | collective-permute-start | bytes 1572872 | tf_op jit(solution)/shard_map/ppermute | solution.py:319
  48.8 11.8 %collective-permute-start.4 = (bf16[16,128,128]{2,1,0:T(8,128)(2,1)S(1)}, bf16[16,128,128]{2,1,0:T(8,128)(2,1)S(1)}, u32[]{:S(2)}, u32[]{:S(2)}) collective-permute-start(bf16[16,128,128]{2,1,0:T(8,128)(2,1)S(1)} %add_convert_fusion.3.refs_0_), channel_id=1, source_target_pairs={{0,4},{1,5},{2,6},{3,7},{4,8},{5,9},{6,10},{7,11},{8,12},{9,13},{1... | collective-permute-start | bytes 1572872 | tf_op jit(solution)/shard_map/ppermute | solution.py:319
  49.1 14.7 %collective-permute-start.8 = (bf16[16,128,128]{2,1,0:T(8,128)(2,1)S(1)}, bf16[16,128,128]{2,1,0:T(8,128)(2,1)S(1)}, u32[]{:S(2)}, u32[]{:S(2)}) collective-permute-start(bf16[16,128,128]{2,1,0:T(8,128)(2,1)S(1)} %add_convert_fusion.1.refs_2_), channel_id=1, source_target_pairs={{0,1},{1,2},{2,3},{3,0},{4,5},{5,6},{6,7},{7,4},{8,9},{9,10},{10,1... | collective-permute-start | bytes 1572872 | tf_op jit(solution)/shard_map/ppermute | solution.py:319
  49.8 14.0 %collective-permute-start.11 = (bf16[16,128,128]{2,1,0:T(8,128)(2,1)S(1)}, bf16[16,128,128]{2,1,0:T(8,128)(2,1)S(1)}, u32[]{:S(2)}, u32[]{:S(2)}) collective-permute-start(bf16[16,128,128]{2,1,0:T(8,128)(2,1)S(1)} %add_convert_fusion.refs_3_), channel_id=1, source_target_pairs={{0,3},{1,0},{2,1},{3,2},{4,7},{5,4},{6,5},{7,6},{8,11},{9,8},{10,9... | collective-permute-start | bytes 1572872 | tf_op jit(solution)/shard_map/ppermute | solution.py:319
  60.6 18.2 %copy-start.1 = (f32[16,128,128]{2,1,0:T(8,128)S(1)}, f32[16,128,128]{2,1,0:T(8,128)}, u32[]{:S(2)}) copy-start(f32[16,128,128]{2,1,0:T(8,128)} %diag_ref.3) | copy-start | bytes 3145732
  64.5 7.1 %collective-permute-start.12 = (bf16[8,128,128]{2,1,0:T(8,128)(2,1)S(1)}, bf16[8,128,128]{2,1,0:T(8,128)(2,1)S(1)}, u32[]{:S(2)}, u32[]{:S(2)}) collective-permute-start(bf16[8,128,128]{2,1,0:T(8,128)(2,1)S(1)} %get-tuple-element.41), channel_id=1, source_target_pairs={{0,2},{1,3},{2,0},{3,1},{4,6},{5,7},{6,4},{7,5},{8,10},{9,11},{10,... | collective-permute-start | bytes 786440 | tf_op jit(solution)/shard_map/ppermute | solution.py:319
  64.8 14.0 %collective-permute-start.13 = (bf16[8,128,128]{2,1,0:T(8,128)(2,1)S(1)}, bf16[8,128,128]{2,1,0:T(8,128)(2,1)S(1)}, u32[]{:S(2)}, u32[]{:S(2)}) collective-permute-start(bf16[8,128,128]{2,1,0:T(8,128)(2,1)S(1)} %get-tuple-element.42), channel_id=1, source_target_pairs={{0,1},{1,2},{2,3},{3,0},{4,5},{5,6},{6,7},{7,4},{8,9},{9,10},{10,1... | collective-permute-start | bytes 786440 | tf_op jit(solution)/shard_map/ppermute | solution.py:319
  66.3 12.6 %collective-permute-start.14 = (bf16[8,128,128]{2,1,0:T(8,128)(2,1)S(1)}, bf16[8,128,128]{2,1,0:T(8,128)(2,1)S(1)}, u32[]{:S(2)}, u32[]{:S(2)}) collective-permute-start(bf16[8,128,128]{2,1,0:T(8,128)(2,1)S(1)} %get-tuple-element.43), channel_id=1, source_target_pairs={{0,3},{1,0},{2,1},{3,2},{4,7},{5,4},{6,5},{7,6},{8,11},{9,8},{10,9... | collective-permute-start | bytes 786440 | tf_op jit(solution)/shard_map/ppermute | solution.py:319
  67.6 11.3 %collective-permute-start.15 = (bf16[8,128,128]{2,1,0:T(8,128)(2,1)S(1)}, bf16[8,128,128]{2,1,0:T(8,128)(2,1)S(1)}, u32[]{:S(2)}, u32[]{:S(2)}) collective-permute-start(bf16[8,128,128]{2,1,0:T(8,128)(2,1)S(1)} %get-tuple-element.45), channel_id=1, source_target_pairs={{0,8},{1,9},{2,10},{3,11},{4,12},{5,13},{6,14},{7,15},{8,0},{9,1},... | collective-permute-start | bytes 786440 | tf_op jit(solution)/shard_map/ppermute | solution.py:319
  67.6 11.3 %collective-permute-start.16 = (bf16[8,128,128]{2,1,0:T(8,128)(2,1)S(1)}, bf16[8,128,128]{2,1,0:T(8,128)(2,1)S(1)}, u32[]{:S(2)}, u32[]{:S(2)}) collective-permute-start(bf16[8,128,128]{2,1,0:T(8,128)(2,1)S(1)} %get-tuple-element.46), channel_id=1, source_target_pairs={{0,4},{1,5},{2,6},{3,7},{4,8},{5,9},{6,10},{7,11},{8,12},{9,13},{1... | collective-permute-start | bytes 786440 | tf_op jit(solution)/shard_map/ppermute | solution.py:319
  71.6 7.2 %collective-permute-start.17 = (bf16[8,128,128]{2,1,0:T(8,128)(2,1)S(1)}, bf16[8,128,128]{2,1,0:T(8,128)(2,1)S(1)}, u32[]{:S(2)}, u32[]{:S(2)}) collective-permute-start(bf16[8,128,128]{2,1,0:T(8,128)(2,1)S(1)} %get-tuple-element.47), channel_id=1, source_target_pairs={{0,12},{1,13},{2,14},{3,15},{4,0},{5,1},{6,2},{7,3},{8,4},{9,5},{1... | collective-permute-start | bytes 786440 | tf_op jit(solution)/shard_map/ppermute | solution.py:319
  81.1 18.3 %all-to-all-start = ((bf16[16,128,128]{2,1,0:T(8,128)(2,1)}), bf16[16,128,128]{2,1,0:T(8,128)(2,1)S(1)}, u32[]{:S(2)}, u32[]{:S(2)}) async-start(bf16[16,128,128]{2,1,0:T(8,128)(2,1)} %get-tuple-element.49), calls=%async_computation | async-start | bytes 1048576 | tf_op jit(solution)/shard_map/all_to_all | solution.py:400
Sparse Core Ops, SparseCore 0:
  12.1 35.7 all-gather.2

commit v3 on v2

--- a/solution.py
+++ b/solution.py
@@ -131,50 +131,26 @@
     )(index, stay(table), stay(left), stay(right), *order)
 
 
-def offset_kernel(diag_ref, seed_ref, out_ref, held, sem):
-    rows = held.shape[0]
-    group = rows // 2
-    copies = []
-    for g in range(2):
-
-        def one(i, _, g=g):
-            r = g * group + i
-            dh, dl = split(diag_ref[r])
-            sh, sl = split(seed_ref[r])
-            held[r] = (mm_nt(sh, dh) + (mm_nt(sh, dl) + mm_nt(sl, dh))).astype(bf16)
-            return 0
-
-        lax.fori_loop(0, group, one, 0, unroll=4)
-        part = pl.ds(g * group, group)
-        copies.append(pltpu.make_async_copy(held.at[part], out_ref.at[part], sem.at[g]))
-        copies[-1].start()
-    for c in copies:
-        c.wait()
-
-
-def offsets_of(diag, seed):
-    rows = diag.shape[0]
-    return pl.pallas_call(
-        offset_kernel,
-        out_shape=jax.ShapeDtypeStruct((rows, B, B), bf16),
-        in_specs=[VMEM, VMEM],
-        out_specs=HBM,
-        scratch_shapes=[pltpu.VMEM((rows, B, B), bf16), pltpu.SemaphoreType.DMA((2,))],
-        compiler_params=pltpu.CompilerParams(vmem_limit_bytes=4 * MIB),
-        cost_estimate=pl.CostEstimate(flops=rows * 6 * B**3, bytes_accessed=rows * 10 * B * B, transcendentals=0),
-        name="offsets",
-    )(diag, seed)
-
-
-def local_kernel(index_ref, table_ref, coupling_ref, left_ref, right_ref, *refs):
-    base_ref, left, right, table, lsem, rsem, tsem = refs[-7:]
+def local_kernel(index_ref, table_ref, coupling_ref, left_ref, right_ref, diag_ref, seed_ref, *refs):
+    base_ref, offset_ref, left, right, table, lsem, rsem, tsem = refs[-8:]
     slots = left.shape[0]
     rows = coupling_ref.shape[0]
+    half = rows // 2
+    core = lax.axis_index("section") % 2
     table_copy = pltpu.make_async_copy(table_ref, table, tsem)
     table_copy.start()
     pairs = bulk(left_ref, right_ref, left, right, lsem, rsem)
     for r in range(rows):
         base_ref[r] = coupling_ref[r].astype(f32)
+
+    def offset(r, _):
+        dh, dl = split(diag_ref[r])
+        sh, sl = split(seed_ref[r])
+        o = mm_nt(sh, dh) + (mm_nt(sh, dl) + mm_nt(sl, dh))
+        offset_ref[(r + core * half) % rows] = o.astype(bf16)
+        return 0
+
+    lax.fori_loop(0, rows, offset, 0, unroll=4)
     table_copy.wait()
     per = slots // CHUNKS
     for k, pair in enumerate(pairs):
@@ -194,14 +170,14 @@
         lax.fori_loop(0, per // UNROLL, work, 0)
 
 
-def local_sums(index, table, coupling, left, right, order):
+def local_and_offset(index, table, coupling, left, right, diag, seed, order):
     slots = left.shape[0]
     rows = coupling.shape[0]
     return pl.pallas_call(
         local_kernel,
-        out_shape=jax.ShapeDtypeStruct((rows, B, B), f32),
-        in_specs=[SMEM, HBM, VMEM, HBM, HBM] + [ANY] * len(order),
-        out_specs=VMEM,
+        out_shape=[jax.ShapeDtypeStruct((rows, B, B), f32), jax.ShapeDtypeStruct((rows, B, B), bf16)],
+        in_specs=[SMEM, HBM, VMEM, HBM, HBM, VMEM, VMEM] + [ANY] * len(order),
+        out_specs=[VMEM, VMEM],
         scratch_shapes=[
             pltpu.VMEM((slots, B, B), bf16),
             pltpu.VMEM((slots, B, B), bf16),
@@ -210,12 +186,12 @@
             pltpu.SemaphoreType.DMA((CHUNKS,)),
             pltpu.SemaphoreType.DMA,
         ],
-        compiler_params=pltpu.CompilerParams(vmem_limit_bytes=12 * MIB),
+        compiler_params=pltpu.CompilerParams(vmem_limit_bytes=16 * MIB),
         cost_estimate=pl.CostEstimate(
-            flops=slots * 4 * B**3, bytes_accessed=slots * 4 * B * B + rows * 6 * B * B, transcendentals=0
+            flops=slots * 4 * B**3, bytes_accessed=slots * 4 * B * B + rows * 16 * B * B, transcendentals=0
         ),
-        name="local_sums",
-    )(index, stay(table), coupling, stay(left), stay(right), *order)
+        name="local_and_offset",
+    )(index, stay(table), coupling, stay(left), stay(right), diag, seed, *order)
 
 
 def first_totals_kernel(own_x, own_z, *refs):
@@ -245,9 +221,11 @@
     return outs[:SIDE], outs[SIDE:]
 
 
-def coupling_kernel(base_ref, diag_ref, *refs):
-    new_ref, step_ref = refs[8:]
-    half = base_ref.shape[0] // 2
+def coupling_kernel(base_ref, diag_ref, offset_ref, *refs):
+    new_ref, keep_ref, give_ref, held = refs[-4:]
+    rows = base_ref.shape[0]
+    half = rows // 2
+    core = lax.axis_index("section") % 2
     for s in range(2):
         parts = refs[s * 4 : s * 4 + 4]
 
@@ -259,53 +237,183 @@
             new_ref[r] = t
             th, tl = split(t)
             dh, dl = split(diag_ref[r])
-            step_ref[r] = -(mm(dh, th) + (mm(dh, tl) + mm(dl, th))).astype(bf16)
+            held[(r + core * half) % rows] = -(mm(dh, th) + (mm(dh, tl) + mm(dl, th))).astype(bf16)
             return 0
 
         lax.fori_loop(0, half, finish, 0, unroll=4)
-
-
-def coupling_and_step(base, diag, parts_x, parts_z):
+    for i in range(half):
+        keep_ref[i] = held[i]
+        give_ref[i] = held[half + i]
+        give_ref[half + i] = offset_ref[half + i]
+
+
+def coupling_and_step(base, diag, offsets, parts_x, parts_z):
     rows = base.shape[0]
+    half = rows // 2
     return pl.pallas_call(
         coupling_kernel,
-        out_shape=[jax.ShapeDtypeStruct((rows, B, B), f32), jax.ShapeDtypeStruct((rows, B, B), bf16)],
-        in_specs=[VMEM] * 10,
-        out_specs=[VMEM, VMEM],
-        compiler_params=pltpu.CompilerParams(vmem_limit_bytes=7 * MIB),
+        out_shape=[
+            jax.ShapeDtypeStruct((rows, B, B), f32),
+            jax.ShapeDtypeStruct((half, B, B), bf16),
+            jax.ShapeDtypeStruct((rows, B, B), bf16),
+        ],
+        in_specs=[VMEM] * 11,
+        out_specs=[VMEM] * 3,
+        scratch_shapes=[pltpu.VMEM((rows, B, B), bf16)],
+        compiler_params=pltpu.CompilerParams(vmem_limit_bytes=9 * MIB),
         cost_estimate=pl.CostEstimate(flops=rows * 6 * B**3, bytes_accessed=rows * 22 * B * B, transcendentals=0),
         name="coupling_and_step",
-    )(base, diag, *parts_x, *parts_z)
-
-
-def chain_kernel(sections, chains, step_ref, offset_ref, out_ref):
-    current = []
-    for j in range(chains):
-        k = (sections - 1) * chains + j
-        o = offset_ref[k]
-        out_ref[k] = o
-        current.append(o.astype(f32))
-    for s in range(sections - 2, -1, -1):
-        for j in range(chains):
-            k = s * chains + j
-            high, low = split(current[j])
-            m = step_ref[k]
-            new = offset_ref[k].astype(f32) + (mm_nt(high, m) + mm_nt(low, m))
-            out_ref[k] = new.astype(bf16)
-            current[j] = new
-
-
-def run_chains(sections, steps, offsets):
-    rows = steps.shape[0]
-    return pl.pallas_call(
-        functools.partial(chain_kernel, sections, rows // sections),
-        out_shape=jax.ShapeDtypeStruct((rows, B, B), bf16),
+    )(base, diag, offsets, *parts_x, *parts_z)
+
+
+def compose_kernel(chips, keep_ref, offset_ref, got_ref, *outs):
+    section = lax.axis_index("section")
+    chip = section // 2
+    half = keep_ref.shape[0]
+    per = half // chips
+
+    def compose(first):
+        for k in range(chips):
+            for j in range(per):
+                i = (chip + k) % chips * per + j
+                mine = (keep_ref[i], offset_ref[i])
+                other = (got_ref[i], got_ref[half + i])
+                (ma, oa), (mb, ob) = (mine, other) if first else (other, mine)
+                outs[k][j] = mm(ma, mb).astype(bf16)
+                outs[k][per + j] = (oa.astype(f32) + mm_nt(ob, ma)).astype(bf16)
+
+    @pl.when(section % 2 == 0)
+    def _():
+        compose(True)
+
+    @pl.when(section % 2 == 1)
+    def _():
+        compose(False)
+
+
+def compose(chips, keep, offsets, got):
+    half = keep.shape[0]
+    return pl.pallas_call(
+        functools.partial(compose_kernel, chips),
+        out_shape=[jax.ShapeDtypeStruct((2 * half // chips, B, B), bf16)] * chips,
+        in_specs=[VMEM] * 3,
+        out_specs=[VMEM] * chips,
+        compiler_params=pltpu.CompilerParams(vmem_limit_bytes=4 * MIB),
+        cost_estimate=pl.CostEstimate(flops=half * 4 * B**3, bytes_accessed=half * 12 * B * B, transcendentals=0),
+        name="compose",
+    )(keep, offsets, got)
+
+
+def chain_kernel(chips, *refs):
+    parts = refs[:chips]
+    outs = refs[chips : 2 * chips]
+    maps, incoming = refs[2 * chips :]
+    chip = lax.axis_index("section") // 2
+    per = outs[0].shape[0]
+    for k in range(chips):
+        for i in range(2 * per):
+            maps[(chip - k + chips) % chips, i] = parts[k][i]
+    current = [jnp.zeros((B, B), f32)] * per
+    for c in range(chips - 1, -1, -1):
+        for j in range(per):
+            incoming[c, j] = current[j].astype(bf16)
+            if c > 0:
+                new = maps[c, per + j].astype(f32)
+                if c < chips - 1:
+                    high, low = split(current[j])
+                    new = new + (mm_nt(high, maps[c, j]) + mm_nt(low, maps[c, j]))
+                current[j] = new
+    for k in range(chips):
+        for j in range(per):
+            outs[k][j] = incoming[(chip + k) % chips, j]
+
+
+def run_chains(parts):
+    chips = len(parts)
+    per = parts[0].shape[0] // 2
+    return pl.pallas_call(
+        functools.partial(chain_kernel, chips),
+        out_shape=[jax.ShapeDtypeStruct((per, B, B), bf16)] * chips,
+        in_specs=[VMEM] * chips,
+        out_specs=[VMEM] * chips,
+        scratch_shapes=[pltpu.VMEM((chips, 2 * per, B, B), bf16), pltpu.VMEM((chips, per, B, B), bf16)],
+        compiler_params=pltpu.CompilerParams(vmem_limit_bytes=4 * MIB),
+        cost_estimate=pl.CostEstimate(
+            flops=chips * per * 4 * B**3, bytes_accessed=chips * per * 6 * B * B, transcendentals=0
+        ),
+        name="run_chains",
+    )(*parts)
+
+
+def expand_kernel(chips, keep_ref, offset_ref, got_ref, *refs):
+    parts = refs[:chips]
+    mine_ref, other_ref = refs[chips:]
+    section = lax.axis_index("section")
+    chip = section // 2
+    half = keep_ref.shape[0]
+    per = half // chips
+
+    def expand(first):
+        for k in range(chips):
+            for j in range(per):
+                i = (chip - k + chips) % chips * per + j
+                mine = (keep_ref[i], offset_ref[i])
+                other = (got_ref[i], got_ref[half + i])
+                (ma, oa), (mb, ob) = (mine, other) if first else (other, mine)
+                b = ob.astype(f32) + mm_nt(parts[k][j], mb)
+                high, low = split(b)
+                a = oa.astype(f32) + (mm_nt(high, ma) + mm_nt(low, ma))
+                mine_ref[i] = a if first else b
+                other_ref[i] = (b if first else a).astype(bf16)
+
+    @pl.when(section % 2 == 0)
+    def _():
+        expand(True)
+
+    @pl.when(section % 2 == 1)
+    def _():
+        expand(False)
+
+
+def expand(keep, offsets, got, parts):
+    chips = len(parts)
+    half = keep.shape[0]
+    return pl.pallas_call(
+        functools.partial(expand_kernel, chips),
+        out_shape=[jax.ShapeDtypeStruct((half, B, B), f32), jax.ShapeDtypeStruct((half, B, B), bf16)],
+        in_specs=[VMEM] * (3 + chips),
+        out_specs=[VMEM] * 2,
+        compiler_params=pltpu.CompilerParams(vmem_limit_bytes=4 * MIB),
+        cost_estimate=pl.CostEstimate(flops=half * 6 * B**3, bytes_accessed=half * 16 * B * B, transcendentals=0),
+        name="expand",
+    )(keep, offsets, got, *parts)
+
+
+def gather_kernel(mine_ref, got_ref, out_ref, held, sem):
+    half = mine_ref.shape[0]
+    core = lax.axis_index("section") % 2
+    own = pltpu.make_async_copy(mine_ref, out_ref.at[pl.ds(core * half, half)], sem.at[0])
+    own.start()
+    for i in range(half):
+        held[i] = got_ref[i].astype(f32)
+    rest = pltpu.make_async_copy(held, out_ref.at[pl.ds((1 - core) * half, half)], sem.at[1])
+    rest.start()
+    own.wait()
+    rest.wait()
+
+
+def gather_rows(mine, got):
+    half = mine.shape[0]
+    return pl.pallas_call(
+        gather_kernel,
+        out_shape=jax.ShapeDtypeStruct((2 * half, B, B), f32),
         in_specs=[VMEM, VMEM],
-        out_specs=VMEM,
+        out_specs=HBM,
+        scratch_shapes=[pltpu.VMEM((half, B, B), f32), pltpu.SemaphoreType.DMA((2,))],
         compiler_params=pltpu.CompilerParams(vmem_limit_bytes=4 * MIB),
-        cost_estimate=pl.CostEstimate(flops=rows * 4 * B**3, bytes_accessed=rows * 6 * B * B, transcendentals=0),
-        name="run_chains",
-    )(steps, offsets)
+        cost_estimate=pl.CostEstimate(flops=0, bytes_accessed=half * 14 * B * B, transcendentals=0),
+        name="gather_rows",
+    )(mine, got)
 
 
 def moved(x, along, by):
@@ -317,6 +425,14 @@
             else:
                 pairs.append((a * SIDE + c, a * SIDE + (c + by) % SIDE))
     return lax.ppermute(x, "row", pairs)
+
+
+def across(x, sections, by):
+    return lax.ppermute(x, "section", [(i, (i + 2 * by) % sections) for i in range(sections)])
+
+
+def partner(x, sections):
+    return lax.ppermute(x, "section", [(i, i ^ 1) for i in range(sections)])
 
 
 def add(a, b):
@@ -373,12 +489,8 @@
     word = word | jnp.where(live, jnp.where(cell < group, 1 << FAR_BIT, 1 << NEAR_BIT), 0)
     local_word = local_target | (local_pivot << PIVOT_BIT)
 
-    step_offset = offsets_of(diag_inverse, adjoint_seed)
-    every = lax.all_gather(step_offset, "section", axis=0, tiled=False)
-    chains = rows // sections
-
     sums = functools.partial(cross_sums, index=word, table=pivot_inverse, left=cross_left, right=cross_right)
-    far = sums(0, [n] * 4, FAR_BIT, live=slots // 4, order=[step_offset])
+    far = sums(0, [n] * 4, FAR_BIT, live=slots // 4)
     ways = ((0, 1), (0, -1), (1, 1), (1, -1))
     far_in = [moved(x, *w) for x, w in zip(far, ways)]
     near = sums(group, [n] * 8 + [2 * n] * 2, NEAR_BIT, live=slots * 3 // 4)
@@ -386,7 +498,9 @@
     joined = [add(x, y) for x, y in zip(near[4:8], far_in)]
     joined_in = [moved(x, *w) for x, w in zip(joined, ways)]
 
-    base = local_sums(local_word, pivot_inverse, coupling, local_left, local_right, joined)
+    base, offsets = local_and_offset(
+        local_word, pivot_inverse, coupling, local_left, local_right, diag_inverse, adjoint_seed, joined
+    )
 
     arrivals = []
     for s in range(2):
@@ -396,12 +510,15 @@
     tot_x, tot_z = first_totals(near[8], near[9], arrivals, [base])
     parts_x = [tot_x[0]] + [moved(tot_x[k], 1, k) for k in (2, 1, 3)]
     parts_z = [tot_z[0]] + [moved(tot_z[k], 0, k) for k in (2, 1, 3)]
-    updated, step_matrix = coupling_and_step(base, diag_inverse, parts_x, parts_z)
-    steps = lax.all_to_all(step_matrix, "section", split_axis=0, concat_axis=0, tiled=True)
-    offsets = lax.dynamic_slice_in_dim(every, lax.axis_index("section") * chains, chains, axis=1)
-    offsets = offsets.reshape(rows, B, B)
-    solved = run_chains(sections, steps, offsets)
-    adjoint = lax.all_to_all(solved, "section", split_axis=0, concat_axis=0, tiled=True).astype(f32)
+    updated, keep, give = coupling_and_step(base, diag_inverse, offsets, parts_x, parts_z)
+    chips = sections // 2
+    got = partner(give, sections)
+    maps = compose(chips, keep, offsets, got)
+    maps = [maps[0]] + [across(maps[k], sections, k) for k in range(1, chips)]
+    incoming = run_chains(maps)
+    incoming = [incoming[0]] + [across(incoming[k], sections, k) for k in range(1, chips)]
+    mine, other = expand(keep, offsets, got, incoming)
+    adjoint = gather_rows(mine, partner(other, sections))
     return (updated, adjoint)
 
 

time: 122 us -> 99.8 us (0.82)
  starting transfers between devices: 30.2 us -> 44.7 us
  between operations: 14.9 us -> 1.7 us
  blocking collectives: 12.6 us -> 0 us
  waiting for transfers between devices: 31.1 us -> 26.2 us
  local copies, waits for them, and re-layouts: 3.55 us -> 0.03 us
    ppermute x0 -> x8, starting transfers between devices: none -> 17.1 us  [the longest x6 11.9 us: across(): lax.ppermute(x, 'section', [(i, (i + 2 * by) % sections) for i in range(s...]
    all_to_all x1 -> x0, blocking collectives: 12.6 us -> none  [per_device(): lax.all_to_all(solved, 'section', split_axis=0, concat_axis=0, tiled=True)]
    ppermute x0 -> x8, waiting for transfers between devices: none -> 9.13 us  [the longest x6 6.43 us: across(): lax.ppermute(x, 'section', [(i, (i + 2 * by) % sections) for i in range(s...]
    all_to_all x1 -> x0, starting transfers between devices: 8.85 us -> none  [per_device(): lax.all_to_all(step_matrix, 'section', split_axis=0, concat_axis=0, tiled...]
    all_to_all x1 -> x0, waiting for transfers between devices: 8.4 us -> none  [per_device(): lax.all_to_all(step_matrix, 'section', split_axis=0, concat_axis=0, tiled...]
    ppermute x18, starting transfers between devices: 21.3 us -> 27.7 us  [moved(): return lax.ppermute(x, 'row', pairs)]
    ppermute x18, waiting for transfers between devices: 22.7 us -> 17.1 us  [moved(): return lax.ppermute(x, 'row', pairs)]
    unnamed x12 -> x10, local copies, waits for them, and re-layouts: 2.47 us -> 0.03 us
  transfers between devices with their start and end apart: 20 -> 26, of which waited for: 7 -> 10; matrix products, arithmetic and copies ran while one was open for 2% -> 1% of each run, Pallas kernels for 19% -> 15%
where the time goes in v3:
time: 99.8 us; the launch traced here: 99.7 us
  starting transfers between devices  44.7 us (45%)
  waiting for transfers between devices  26.2 us (26%)
  Pallas kernels  25.7 us (26%)
  between operations  1.7 us (2%)
  other arithmetic  1.29 us (1%)
    ppermute x18, starting transfers between devices, moved(): return lax.ppermute(x, 'row', pairs)  27.7 us
    ppermute x18, waiting for transfers between devices, moved(): return lax.ppermute(x, 'row', pairs)  17.1 us
    pallas_call x2, Pallas kernels, cross_sums(): pl.pallas_call(functools.partial(cross_kernel, first, sizes, flag), out_s...  12.6 us
    ppermute x6, starting transfers between devices, across(): lax.ppermute(x, 'section', [(i, (i + 2 * by) % sections) for i in range(s...  11.9 us
    pallas_call x1, Pallas kernels, local_and_offset(): pl.pallas_call(local_kernel, out_shape=[jax.ShapeDtypeStruct((rows, B, B)...  7.35 us
    ppermute x6, waiting for transfers between devices, across(): lax.ppermute(x, 'section', [(i, (i + 2 * by) % sections) for i in range(s...  6.43 us
    ppermute x2, starting transfers between devices, partner(): return lax.ppermute(x, 'section', [(i, i ^ 1) for i in range(sections)])  5.16 us
    ppermute x2, waiting for transfers between devices, partner(): return lax.ppermute(x, 'section', [(i, i ^ 1) for i in range(sections)])  2.7 us
  transfers between devices with their start and end apart: 26, of which 10 were waited for; matrix products, arithmetic and copies ran while one was open for 1% of the time, Pallas kernels for 15%

profile of v3, /device:TPU:1, one launch (start us, length us, event | category | flops | bytes accessed | tf_op | source)
XLA Modules:
  0.0 99.7 jit_solution(15733769772504140044)
XLA Ops:
  1.3 0.7 fusion.6.index_ref
  2.0 5.2 %cross_sums.3 = (bf16[16,128,128]{2,1,0:T(8,128)(2,1)S(1)}, bf16[16,128,128]{2,1,0:T(8,128)(2,1)S(1)}, bf16[16,128,128]{2,1,0:T(8,128)(2,1)S(1)}, bf16[16,128,128]{2,1,0:T(8,128)(2,1)S(1)}) custom-call(s32[128]{0:T(128)S(1)} %fusion.6.index_ref, bf16[4,128,128]{2,1,0:T(8,128)(2,1)} %table_ref.5, bf16[128,128,128]{2,1,0:T(8,128)(2,1)} %left_ref.4, ...), custom_call_target="tpu_custom_call" | custom-call | flops 268435456 | bytes 10485760 | tf_op jit(solution)/shard_map/cross_sums/pallas_call | solution.py:111
  7.2 1.6 %collective-permute-start = (bf16[16,128,128]{2,1,0:T(8,128)(2,1)S(1)}, bf16[16,128,128]{2,1,0:T(8,128)(2,1)S(1)}, u32[]{:S(2)}, u32[]{:S(2)}) collective-permute-start(bf16[16,128,128]{2,1,0:T(8,128)(2,1)S(1)} %get-tuple-element.40), channel_id=1, source_target_pairs={{0,4},{1,5},{2,6},{3,7},{4,8},{5,9},{6,10},{7,11},{8,12},{9,13},{1... | collective-permute-start | bytes 1572872 | tf_op jit(solution)/shard_map/ppermute | solution.py:427
  8.9 1.4 %collective-permute-start.1 = (bf16[16,128,128]{2,1,0:T(8,128)(2,1)S(1)}, bf16[16,128,128]{2,1,0:T(8,128)(2,1)S(1)}, u32[]{:S(2)}, u32[]{:S(2)}) collective-permute-start(bf16[16,128,128]{2,1,0:T(8,128)(2,1)S(1)} %get-tuple-element.42), channel_id=1, source_target_pairs={{0,12},{1,13},{2,14},{3,15},{4,0},{5,1},{6,2},{7,3},{8,4},{9,5},{1... | collective-permute-start | bytes 1572872 | tf_op jit(solution)/shard_map/ppermute | solution.py:427
  10.2 2.6 %collective-permute-start.2 = (bf16[16,128,128]{2,1,0:T(8,128)(2,1)S(1)}, bf16[16,128,128]{2,1,0:T(8,128)(2,1)S(1)}, u32[]{:S(2)}, u32[]{:S(2)}) collective-permute-start(bf16[16,128,128]{2,1,0:T(8,128)(2,1)S(1)} %get-tuple-element.44), channel_id=1, source_target_pairs={{0,1},{1,2},{2,3},{3,0},{4,5},{5,6},{6,7},{7,4},{8,9},{9,10},{10,1... | collective-permute-start | bytes 1572872 | tf_op jit(solution)/shard_map/ppermute | solution.py:427
  12.8 1.6 %collective-permute-start.3 = (bf16[16,128,128]{2,1,0:T(8,128)(2,1)S(1)}, bf16[16,128,128]{2,1,0:T(8,128)(2,1)S(1)}, u32[]{:S(2)}, u32[]{:S(2)}) collective-permute-start(bf16[16,128,128]{2,1,0:T(8,128)(2,1)S(1)} %get-tuple-element.46), channel_id=1, source_target_pairs={{0,3},{1,0},{2,1},{3,2},{4,7},{5,4},{6,5},{7,6},{8,11},{9,8},{10,9... | collective-permute-start | bytes 1572872 | tf_op jit(solution)/shard_map/ppermute | solution.py:427
  14.5 7.4 %cross_sums.2 = (bf16[16,128,128]{2,1,0:T(8,128)(2,1)S(1)}, bf16[16,128,128]{2,1,0:T(8,128)(2,1)S(1)}, bf16[16,128,128]{2,1,0:T(8,128)(2,1)S(1)}, bf16[16,128,12...) custom-call(s32[128]{0:T(128)S(1)} %fusion.6.index_ref, ...), custom_call_target="tpu_custom_call" | custom-call | flops 805306368 | bytes 14680064 | tf_op jit(solution)/shard_map/cross_sums/pallas_call | solution.py:111
  21.9 0.1 collective-permute-start.5
  22.0 1.4 %collective-permute-start.6 = (bf16[16,128,128]{2,1,0:T(8,128)(2,1)S(1)}, bf16[16,128,128]{2,1,0:T(8,128)(2,1)S(1)}, u32[]{:S(2)}, u32[]{:S(2)}) collective-permute-start(bf16[16,128,128]{2,1,0:T(8,128)(2,1)S(1)} %get-tuple-element.52), channel_id=1, source_target_pairs={{0,4},{1,5},{2,6},{3,7},{4,8},{5,9},{6,10},{7,11},{8,12},{9,13},{1... | collective-permute-start | bytes 1572872 | tf_op jit(solution)/shard_map/ppermute | solution.py:427
  23.5 0.1 add_convert_fusion.3.refs_0_
  23.6 2.5 %collective-permute-start.9 = (bf16[16,128,128]{2,1,0:T(8,128)(2,1)S(1)}, bf16[16,128,128]{2,1,0:T(8,128)(2,1)S(1)}, u32[]{:S(2)}, u32[]{:S(2)}) collective-permute-start(bf16[16,128,128]{2,1,0:T(8,128)(2,1)S(1)} %get-tuple-element.53), channel_id=1, source_target_pairs={{0,3},{1,0},{2,1},{3,2},{4,7},{5,4},{6,5},{7,6},{8,11},{9,8},{10,9... | collective-permute-start | bytes 1572872 | tf_op jit(solution)/shard_map/ppermute | solution.py:427
  26.1 0.1 add_convert_fusion.2.refs_1_
  26.3 0.1 collective-permute-start.10
  26.4 0.1 add_convert_fusion.1.refs_2_
  26.5 1.3 %collective-permute-start.4 = (bf16[16,128,128]{2,1,0:T(8,128)(2,1)S(1)}, bf16[16,128,128]{2,1,0:T(8,128)(2,1)S(1)}, u32[]{:S(2)}, u32[]{:S(2)}) collective-permute-start(bf16[16,128,128]{2,1,0:T(8,128)(2,1)S(1)} %add_convert_fusion.3.refs_0_), channel_id=1, source_target_pairs={{0,4},{1,5},{2,6},{3,7},{4,8},{5,9},{6,10},{7,11},{8,12},{9,13},{1... | collective-permute-start | bytes 1572872 | tf_op jit(solution)/shard_map/ppermute | solution.py:427
  27.8 0.1 add_convert_fusion.refs_3_
  28.0 5.7 %collective-permute-done.5.refs_1_ = bf16[16,128,128]{2,1,0:T(8,128)(2,1)S(1)} collective-permute-done((bf16[16,128,128]{2,1,0:T(8,128)(2,1)S(1)}, bf16[16,128,128]{2,1,0:T(8,128)(2,1)S(1)}, u32[]{:S(2)}, u32[]{:S(2)}) %collective-permute-start.5) | collective-permute-done | bytes 524320 | tf_op jit(solution)/shard_map/ppermute | solution.py:427
  33.7 0.5 collective-permute-start.7
  34.2 4.4 %collective-permute-start.8 = (bf16[16,128,128]{2,1,0:T(8,128)(2,1)S(1)}, bf16[16,128,128]{2,1,0:T(8,128)(2,1)S(1)}, u32[]{:S(2)}, u32[]{:S(2)}) collective-permute-start(bf16[16,128,128]{2,1,0:T(8,128)(2,1)S(1)} %add_convert_fusion.1.refs_2_), channel_id=1, source_target_pairs={{0,1},{1,2},{2,3},{3,0},{4,5},{5,6},{6,7},{7,4},{8,9},{9,10},{10,1... | collective-permute-start | bytes 1572872 | tf_op jit(solution)/shard_map/ppermute | solution.py:427
  38.6 0.3 collective-permute-start.11
  39.0 7.4 %local_and_offset.1 = (f32[16,128,128]{2,1,0:T(8,128)S(1)}, bf16[16,128,128]{2,1,0:T(8,128)(2,1)S(1)}) custom-call(s32[128]{0:T(128)S(1)} %shift-left_or_fusion.index_ref, bf16[4,128,128]{2,1,0:T(8,128)(2,1)} %table_ref.5, bf16[16,128,128]{2,1,0:T(8,128)(2,1)S(1)} %copy-done.2, bf16[128,128,128]{2,1,0:T(8,128)(2,1)} %left_ref.5, ...), custom_call_target="tpu_custom_call" | custom-call | flops 1073741824 | bytes 12582912 | tf_op jit(solution)/shard_map/local_and_offset/pallas_call | solution.py:176
  46.4 2.6 %collective-permute-done.8.refs_4_ = bf16[16,128,128]{2,1,0:T(8,128)(2,1)S(1)} collective-permute-done((bf16[16,128,128]{2,1,0:T(8,128)(2,1)S(1)}, bf16[16,128,128]{2,1,0:T(8,128)(2,1)S(1)}, u32[]{:S(2)}, u32[]{:S(2)}) %collective-permute-start.8) | collective-permute-done | bytes 524320 | tf_op jit(solution)/shard_map/ppermute | solution.py:427
  49.0 0.7 first_totals.1
  49.7 2.7 %collective-permute-start.12 = (bf16[8,128,128]{2,1,0:T(8,128)(2,1)S(1)}, bf16[8,128,128]{2,1,0:T(8,128)(2,1)S(1)}, u32[]{:S(2)}, u32[]{:S(2)}) collective-permute-start(bf16[8,128,128]{2,1,0:T(8,128)(2,1)S(1)} %get-tuple-element.56), channel_id=1, source_target_pairs={{0,2},{1,3},{2,0},{3,1},{4,6},{5,7},{6,4},{7,5},{8,10},{9,11},{10,... | collective-permute-start | bytes 786440 | tf_op jit(solution)/shard_map/ppermute | solution.py:427
  52.5 2.7 %collective-permute-start.14 = (bf16[8,128,128]{2,1,0:T(8,128)(2,1)S(1)}, bf16[8,128,128]{2,1,0:T(8,128)(2,1)S(1)}, u32[]{:S(2)}, u32[]{:S(2)}) collective-permute-start(bf16[8,128,128]{2,1,0:T(8,128)(2,1)S(1)} %get-tuple-element.58), channel_id=1, source_target_pairs={{0,3},{1,0},{2,1},{3,2},{4,7},{5,4},{6,5},{7,6},{8,11},{9,8},{10,9... | collective-permute-start | bytes 786440 | tf_op jit(solution)/shard_map/ppermute | solution.py:427
  55.1 1.2 %collective-permute-start.15 = (bf16[8,128,128]{2,1,0:T(8,128)(2,1)S(1)}, bf16[8,128,128]{2,1,0:T(8,128)(2,1)S(1)}, u32[]{:S(2)}, u32[]{:S(2)}) collective-permute-start(bf16[8,128,128]{2,1,0:T(8,128)(2,1)S(1)} %get-tuple-element.60), channel_id=1, source_target_pairs={{0,8},{1,9},{2,10},{3,11},{4,12},{5,13},{6,14},{7,15},{8,0},{9,1},... | collective-permute-start | bytes 786440 | tf_op jit(solution)/shard_map/ppermute | solution.py:427
  56.4 0.4 collective-permute-start.16
  56.8 2.8 %collective-permute-start.17 = (bf16[8,128,128]{2,1,0:T(8,128)(2,1)S(1)}, bf16[8,128,128]{2,1,0:T(8,128)(2,1)S(1)}, u32[]{:S(2)}, u32[]{:S(2)}) collective-permute-start(bf16[8,128,128]{2,1,0:T(8,128)(2,1)S(1)} %get-tuple-element.62), channel_id=1, source_target_pairs={{0,12},{1,13},{2,14},{3,15},{4,0},{5,1},{6,2},{7,3},{8,4},{9,5},{1... | collective-permute-start | bytes 786440 | tf_op jit(solution)/shard_map/ppermute | solution.py:427
  59.6 1.1 %collective-permute-done.13.refs_2_ = bf16[8,128,128]{2,1,0:T(8,128)(2,1)S(1)} collective-permute-done((bf16[8,128,128]{2,1,0:T(8,128)(2,1)S(1)}, bf16[8,128,128]{2,1,0:T(8,128)(2,1)S(1)}, u32[]{:S(2)}, u32[]{:S(2)}) %collective-permute-start.13) | collective-permute-done | bytes 262176 | tf_op jit(solution)/shard_map/ppermute | solution.py:427
  60.7 1.7 %collective-permute-done.14.refs_3_ = bf16[8,128,128]{2,1,0:T(8,128)(2,1)S(1)} collective-permute-done((bf16[8,128,128]{2,1,0:T(8,128)(2,1)S(1)}, bf16[8,128,128]{2,1,0:T(8,128)(2,1)S(1)}, u32[]{:S(2)}, u32[]{:S(2)}) %collective-permute-start.14) | collective-permute-done | bytes 262176 | tf_op jit(solution)/shard_map/ppermute | solution.py:427
  62.4 5.9 %collective-permute-done.16.refs_6_ = bf16[8,128,128]{2,1,0:T(8,128)(2,1)S(1)} collective-permute-done((bf16[8,128,128]{2,1,0:T(8,128)(2,1)S(1)}, bf16[8,128,128]{2,1,0:T(8,128)(2,1)S(1)}, u32[]{:S(2)}, u32[]{:S(2)}) %collective-permute-start.16) | collective-permute-done | bytes 262176 | tf_op jit(solution)/shard_map/ppermute | solution.py:427
  68.3 2.2 %coupling_and_step.1 = (f32[16,128,128]{2,1,0:T(8,128)}, bf16[8,128,128]{2,1,0:T(8,128)(2,1)S(1)}, bf16[16,128,128]{2,1,0:T(8,128)(2,1)S(1)}) custom-call(f32[16,128,128]{2,1,0:T(8,128)S(1)} %get-tuple-element.47.refs_8_.base_ref, f32[16,128,128]{2,1,0:T(8,128)S(1)} %copy-done, bf16[16,128,128]{2,1,0:T(8,128)(2,1)S(1)} %get-tuple-element.48.offset_ref, ...), custom_call_target="tpu_custom_call" | custom-call | flops 201326592 | bytes 5767168 | tf_op jit(solution)/shard_map/coupling_and_step/pallas_call | solution.py:253
  70.5 2.7 %collective-permute-start.18 = (bf16[16,128,128]{2,1,0:T(8,128)(2,1)S(1)}, bf16[16,128,128]{2,1,0:T(8,128)(2,1)S(1)}, u32[]{:S(2)}, u32[]{:S(2)}) collective-permute-start(bf16[16,128,128]{2,1,0:T(8,128)(2,1)S(1)} %get-tuple-element.65), channel_id=1, source_target_pairs={{0,16},{16,0},{32,48},{48,32},{64,80},{80,64},{96,112},{112,96},{1... | collective-permute-start | bytes 1572872 | tf_op jit(solution)/shard_map/ppermute | solution.py:435
  73.2 1.5 %collective-permute-done.18.got_ref = bf16[16,128,128]{2,1,0:T(8,128)(2,1)S(1)} collective-permute-done((bf16[16,128,128]{2,1,0:T(8,128)(2,1)S(1)}, bf16[16,128,128]{2,1,0:T(8,128)(2,1)S(1)}, u32[]{:S(2)}, u32[]{:S(2)}) %collective-permute-start.18) | collective-permute-done | bytes 524320 | tf_op jit(solution)/shard_map/ppermute | solution.py:435
  74.7 0.4 compose.1
  75.1 1.4 %collective-permute-start.19 = (bf16[4,128,128]{2,1,0:T(8,128)(2,1)S(1)}, bf16[4,128,128]{2,1,0:T(8,128)(2,1)S(1)}, u32[]{:S(2)}, u32[]{:S(2)}) collective-permute-start(bf16[4,128,128]{2,1,0:T(8,128)(2,1)S(1)} %get-tuple-element.67), channel_id=1, source_target_pairs={{0,32},{16,48},{32,64},{48,80},{64,96},{80,112},{96,0},{112,16},{1... | collective-permute-start | bytes 393224 | tf_op jit(solution)/shard_map/ppermute | solution.py:431
  76.5 3.7 %collective-permute-start.20 = (bf16[4,128,128]{2,1,0:T(8,128)(2,1)S(1)}, bf16[4,128,128]{2,1,0:T(8,128)(2,1)S(1)}, u32[]{:S(2)}, u32[]{:S(2)}) collective-permute-start(bf16[4,128,128]{2,1,0:T(8,128)(2,1)S(1)} %get-tuple-element.68), channel_id=1, source_target_pairs={{0,64},{16,80},{32,96},{48,112},{64,0},{80,16},{96,32},{112,48},{1... | collective-permute-start | bytes 393224 | tf_op jit(solution)/shard_map/ppermute | solution.py:431
  80.2 2.0 %collective-permute-start.21 = (bf16[4,128,128]{2,1,0:T(8,128)(2,1)S(1)}, bf16[4,128,128]{2,1,0:T(8,128)(2,1)S(1)}, u32[]{:S(2)}, u32[]{:S(2)}) collective-permute-start(bf16[4,128,128]{2,1,0:T(8,128)(2,1)S(1)} %get-tuple-element.69), channel_id=1, source_target_pairs={{0,96},{16,112},{32,0},{48,16},{64,32},{80,48},{96,64},{112,80},{1... | collective-permute-start | bytes 393224 | tf_op jit(solution)/shard_map/ppermute | solution.py:431
  82.2 4.3 %collective-permute-done.20.refs_2_ = bf16[4,128,128]{2,1,0:T(8,128)(2,1)S(1)} collective-permute-done((bf16[4,128,128]{2,1,0:T(8,128)(2,1)S(1)}, bf16[4,128,128]{2,1,0:T(8,128)(2,1)S(1)}, u32[]{:S(2)}, u32[]{:S(2)}) %collective-permute-start.20) | collective-permute-done | bytes 131104 | tf_op jit(solution)/shard_map/ppermute | solution.py:431
  86.5 0.4 run_chains.1
  87.0 3.1 %collective-permute-start.23 = (bf16[2,128,128]{2,1,0:T(8,128)(2,1)S(1)}, bf16[2,128,128]{2,1,0:T(8,128)(2,1)S(1)}, u32[]{:S(2)}, u32[]{:S(2)}) collective-permute-start(bf16[2,128,128]{2,1,0:T(8,128)(2,1)S(1)} %get-tuple-element.72), channel_id=1, source_target_pairs={{0,64},{16,80},{32,96},{48,112},{64,0},{80,16},{96,32},{112,48},{1... | collective-permute-start | bytes 196616 | tf_op jit(solution)/shard_map/ppermute | solution.py:431
  90.1 1.7 %collective-permute-start.24 = (bf16[2,128,128]{2,1,0:T(8,128)(2,1)S(1)}, bf16[2,128,128]{2,1,0:T(8,128)(2,1)S(1)}, u32[]{:S(2)}, u32[]{:S(2)}) collective-permute-start(bf16[2,128,128]{2,1,0:T(8,128)(2,1)S(1)} %get-tuple-element.73), channel_id=1, source_target_pairs={{0,96},{16,112},{32,0},{48,16},{64,32},{80,48},{96,64},{112,80},{1... | collective-permute-start | bytes 196616 | tf_op jit(solution)/shard_map/ppermute | solution.py:431
  91.8 0.7 collective-permute-done.23.refs_2_
  92.5 1.4 %collective-permute-done.24.refs_3_ = bf16[2,128,128]{2,1,0:T(8,128)(2,1)S(1)} collective-permute-done((bf16[2,128,128]{2,1,0:T(8,128)(2,1)S(1)}, bf16[2,128,128]{2,1,0:T(8,128)(2,1)S(1)}, u32[]{:S(2)}, u32[]{:S(2)}) %collective-permute-start.24) | collective-permute-done | bytes 65568 | tf_op jit(solution)/shard_map/ppermute | solution.py:431
  93.9 1.0 expand.1
  94.9 2.5 %collective-permute-start.25 = (bf16[8,128,128]{2,1,0:T(8,128)(2,1)S(1)}, bf16[8,128,128]{2,1,0:T(8,128)(2,1)S(1)}, u32[]{:S(2)}, u32[]{:S(2)}) collective-permute-start(bf16[8,128,128]{2,1,0:T(8,128)(2,1)S(1)} %get-tuple-element.75), channel_id=1, source_target_pairs={{0,16},{16,0},{32,48},{48,32},{64,80},{80,64},{96,112},{112,96},{1... | collective-permute-start | bytes 786440 | tf_op jit(solution)/shard_map/ppermute | solution.py:435
  97.4 1.2 %collective-permute-done.25.got_ref = bf16[8,128,128]{2,1,0:T(8,128)(2,1)S(1)} collective-permute-done((bf16[8,128,128]{2,1,0:T(8,128)(2,1)S(1)}, bf16[8,128,128]{2,1,0:T(8,128)(2,1)S(1)}, u32[]{:S(2)}, u32[]{:S(2)}) %collective-permute-start.25) | collective-permute-done | bytes 262176 | tf_op jit(solution)/shard_map/ppermute | solution.py:435
  98.5 1.0 gather_rows.1
  (29 shorter events, 0.2 us)
Async XLA Ops:
  7.2 14.8 %collective-permute-start = (bf16[16,128,128]{2,1,0:T(8,128)(2,1)S(1)}, bf16[16,128,128]{2,1,0:T(8,128)(2,1)S(1)}, u32[]{:S(2)}, u32[]{:S(2)}) collective-permute-start(bf16[16,128,128]{2,1,0:T(8,128)(2,1)S(1)} %get-tuple-element.40), channel_id=1, source_target_pairs={{0,4},{1,5},{2,6},{3,7},{4,8},{5,9},{6,10},{7,11},{8,12},{9,13},{1... | collective-permute-start | bytes 1572872 | tf_op jit(solution)/shard_map/ppermute | solution.py:427
  8.9 14.8 %collective-permute-start.1 = (bf16[16,128,128]{2,1,0:T(8,128)(2,1)S(1)}, bf16[16,128,128]{2,1,0:T(8,128)(2,1)S(1)}, u32[]{:S(2)}, u32[]{:S(2)}) collective-permute-start(bf16[16,128,128]{2,1,0:T(8,128)(2,1)S(1)} %get-tuple-element.42), channel_id=1, source_target_pairs={{0,12},{1,13},{2,14},{3,15},{4,0},{5,1},{6,2},{7,3},{8,4},{9,5},{1... | collective-permute-start | bytes 1572872 | tf_op jit(solution)/shard_map/ppermute | solution.py:427
  10.2 16.0 %collective-permute-start.2 = (bf16[16,128,128]{2,1,0:T(8,128)(2,1)S(1)}, bf16[16,128,128]{2,1,0:T(8,128)(2,1)S(1)}, u32[]{:S(2)}, u32[]{:S(2)}) collective-permute-start(bf16[16,128,128]{2,1,0:T(8,128)(2,1)S(1)} %get-tuple-element.44), channel_id=1, source_target_pairs={{0,1},{1,2},{2,3},{3,0},{4,5},{5,6},{6,7},{7,4},{8,9},{9,10},{10,1... | collective-permute-start | bytes 1572872 | tf_op jit(solution)/shard_map/ppermute | solution.py:427
  12.8 13.7 %collective-permute-start.3 = (bf16[16,128,128]{2,1,0:T(8,128)(2,1)S(1)}, bf16[16,128,128]{2,1,0:T(8,128)(2,1)S(1)}, u32[]{:S(2)}, u32[]{:S(2)}) collective-permute-start(bf16[16,128,128]{2,1,0:T(8,128)(2,1)S(1)} %get-tuple-element.46), channel_id=1, source_target_pairs={{0,3},{1,0},{2,1},{3,2},{4,7},{5,4},{6,5},{7,6},{8,11},{9,8},{10,9... | collective-permute-start | bytes 1572872 | tf_op jit(solution)/shard_map/ppermute | solution.py:427
  21.9 17.0 %copy-start.3 = (s32[128]{0:T(128)S(1)}, s32[128]{0:T(128)}, u32[]{:S(2)}) copy-start(s32[128]{0:T(128)} %param.26) | copy-start | bytes 1540
  21.9 17.0 %copy-start.4 = (s32[128]{0:T(128)S(1)}, s32[128]{0:T(128)}, u32[]{:S(2)}) copy-start(s32[128]{0:T(128)} %param.25) | copy-start | bytes 1540
  21.9 17.0 %copy-start = (f32[16,128,128]{2,1,0:T(8,128)S(1)}, f32[16,128,128]{2,1,0:T(8,128)}, u32[]{:S(2)}) copy-start(f32[16,128,128]{2,1,0:T(8,128)} %diag_ref.3) | copy-start | bytes 3145732
  21.9 17.0 %copy-start.1 = (f32[16,128,128]{2,1,0:T(8,128)S(1)}, f32[16,128,128]{2,1,0:T(8,128)}, u32[]{:S(2)}) copy-start(f32[16,128,128]{2,1,0:T(8,128)} %seed_ref.1) | copy-start | bytes 3145732
  21.9 17.0 %copy-start.2 = (bf16[16,128,128]{2,1,0:T(8,128)(2,1)S(1)}, bf16[16,128,128]{2,1,0:T(8,128)(2,1)}, u32[]{:S(2)}) copy-start(bf16[16,128,128]{2,1,0:T(8,128)(2,1)} %coupling_ref.1) | copy-start | bytes 1572868
  21.9 11.8 %collective-permute-start.5 = (bf16[16,128,128]{2,1,0:T(8,128)(2,1)S(1)}, bf16[16,128,128]{2,1,0:T(8,128)(2,1)S(1)}, u32[]{:S(2)}, u32[]{:S(2)}) collective-permute-start(bf16[16,128,128]{2,1,0:T(8,128)(2,1)S(1)} %get-tuple-element.51), channel_id=1, source_target_pairs={{0,12},{1,13},{2,14},{3,15},{4,0},{5,1},{6,2},{7,3},{8,4},{9,5},{1... | collective-permute-start | bytes 1572872 | tf_op jit(solution)/shard_map/ppermute | solution.py:427
  22.0 12.2 %collective-permute-start.6 = (bf16[16,128,128]{2,1,0:T(8,128)(2,1)S(1)}, bf16[16,128,128]{2,1,0:T(8,128)(2,1)S(1)}, u32[]{:S(2)}, u32[]{:S(2)}) collective-permute-start(bf16[16,128,128]{2,1,0:T(8,128)(2,1)S(1)} %get-tuple-element.52), channel_id=1, source_target_pairs={{0,4},{1,5},{2,6},{3,7},{4,8},{5,9},{6,10},{7,11},{8,12},{9,13},{1... | collective-permute-start | bytes 1572872 | tf_op jit(solution)/shard_map/ppermute | solution.py:427
  23.6 15.0 %collective-permute-start.9 = (bf16[16,128,128]{2,1,0:T(8,128)(2,1)S(1)}, bf16[16,128,128]{2,1,0:T(8,128)(2,1)S(1)}, u32[]{:S(2)}, u32[]{:S(2)}) collective-permute-start(bf16[16,128,128]{2,1,0:T(8,128)(2,1)S(1)} %get-tuple-element.53), channel_id=1, source_target_pairs={{0,3},{1,0},{2,1},{3,2},{4,7},{5,4},{6,5},{7,6},{8,11},{9,8},{10,9... | collective-permute-start | bytes 1572872 | tf_op jit(solution)/shard_map/ppermute | solution.py:427
  26.3 20.0 %collective-permute-start.10 = (bf16[16,128,128]{2,1,0:T(8,128)(2,1)S(1)}, bf16[16,128,128]{2,1,0:T(8,128)(2,1)S(1)}, u32[]{:S(2)}, u32[]{:S(2)}) collective-permute-start(bf16[16,128,128]{2,1,0:T(8,128)(2,1)S(1)} %get-tuple-element.54), channel_id=1, source_target_pairs={{0,1},{1,2},{2,3},{3,0},{4,5},{5,6},{6,7},{7,4},{8,9},{9,10},{10,1... | collective-permute-start | bytes 1572872 | tf_op jit(solution)/shard_map/ppermute | solution.py:427
  26.5 19.8 %collective-permute-start.4 = (bf16[16,128,128]{2,1,0:T(8,128)(2,1)S(1)}, bf16[16,128,128]{2,1,0:T(8,128)(2,1)S(1)}, u32[]{:S(2)}, u32[]{:S(2)}) collective-permute-start(bf16[16,128,128]{2,1,0:T(8,128)(2,1)S(1)} %add_convert_fusion.3.refs_0_), channel_id=1, source_target_pairs={{0,4},{1,5},{2,6},{3,7},{4,8},{5,9},{6,10},{7,11},{8,12},{9,13},{1... | collective-permute-start | bytes 1572872 | tf_op jit(solution)/shard_map/ppermute | solution.py:427
  33.7 12.7 %collective-permute-start.7 = (bf16[16,128,128]{2,1,0:T(8,128)(2,1)S(1)}, bf16[16,128,128]{2,1,0:T(8,128)(2,1)S(1)}, u32[]{:S(2)}, u32[]{:S(2)}) collective-permute-start(bf16[16,128,128]{2,1,0:T(8,128)(2,1)S(1)} %add_convert_fusion.2.refs_1_), channel_id=1, source_target_pairs={{0,12},{1,13},{2,14},{3,15},{4,0},{5,1},{6,2},{7,3},{8,4},{9,5},{1... | collective-permute-start | bytes 1572872 | tf_op jit(solution)/shard_map/ppermute | solution.py:427
  34.2 14.8 %collective-permute-start.8 = (bf16[16,128,128]{2,1,0:T(8,128)(2,1)S(1)}, bf16[16,128,128]{2,1,0:T(8,128)(2,1)S(1)}, u32[]{:S(2)}, u32[]{:S(2)}) collective-permute-start(bf16[16,128,128]{2,1,0:T(8,128)(2,1)S(1)} %add_convert_fusion.1.refs_2_), channel_id=1, source_target_pairs={{0,1},{1,2},{2,3},{3,0},{4,5},{5,6},{6,7},{7,4},{8,9},{9,10},{10,1... | collective-permute-start | bytes 1572872 | tf_op jit(solution)/shard_map/ppermute | solution.py:427
  38.6 10.4 %collective-permute-start.11 = (bf16[16,128,128]{2,1,0:T(8,128)(2,1)S(1)}, bf16[16,128,128]{2,1,0:T(8,128)(2,1)S(1)}, u32[]{:S(2)}, u32[]{:S(2)}) collective-permute-start(bf16[16,128,128]{2,1,0:T(8,128)(2,1)S(1)} %add_convert_fusion.refs_3_), channel_id=1, source_target_pairs={{0,3},{1,0},{2,1},{3,2},{4,7},{5,4},{6,5},{7,6},{8,11},{9,8},{10,9... | collective-permute-start | bytes 1572872 | tf_op jit(solution)/shard_map/ppermute | solution.py:427
  49.7 7.1 %collective-permute-start.12 = (bf16[8,128,128]{2,1,0:T(8,128)(2,1)S(1)}, bf16[8,128,128]{2,1,0:T(8,128)(2,1)S(1)}, u32[]{:S(2)}, u32[]{:S(2)}) collective-permute-start(bf16[8,128,128]{2,1,0:T(8,128)(2,1)S(1)} %get-tuple-element.56), channel_id=1, source_target_pairs={{0,2},{1,3},{2,0},{3,1},{4,6},{5,7},{6,4},{7,5},{8,10},{9,11},{10,... | collective-permute-start | bytes 786440 | tf_op jit(solution)/shard_map/ppermute | solution.py:427
  52.5 8.2 %collective-permute-start.13 = (bf16[8,128,128]{2,1,0:T(8,128)(2,1)S(1)}, bf16[8,128,128]{2,1,0:T(8,128)(2,1)S(1)}, u32[]{:S(2)}, u32[]{:S(2)}) collective-permute-start(bf16[8,128,128]{2,1,0:T(8,128)(2,1)S(1)} %get-tuple-element.57), channel_id=1, source_target_pairs={{0,1},{1,2},{2,3},{3,0},{4,5},{5,6},{6,7},{7,4},{8,9},{9,10},{10,1... | collective-permute-start | bytes 786440 | tf_op jit(solution)/shard_map/ppermute | solution.py:427
  52.5 9.9 %collective-permute-start.14 = (bf16[8,128,128]{2,1,0:T(8,128)(2,1)S(1)}, bf16[8,128,128]{2,1,0:T(8,128)(2,1)S(1)}, u32[]{:S(2)}, u32[]{:S(2)}) collective-permute-start(bf16[8,128,128]{2,1,0:T(8,128)(2,1)S(1)} %get-tuple-element.58), channel_id=1, source_target_pairs={{0,3},{1,0},{2,1},{3,2},{4,7},{5,4},{6,5},{7,6},{8,11},{9,8},{10,9... | collective-permute-start | bytes 786440 | tf_op jit(solution)/shard_map/ppermute | solution.py:427
  55.1 7.2 %collective-permute-start.15 = (bf16[8,128,128]{2,1,0:T(8,128)(2,1)S(1)}, bf16[8,128,128]{2,1,0:T(8,128)(2,1)S(1)}, u32[]{:S(2)}, u32[]{:S(2)}) collective-permute-start(bf16[8,128,128]{2,1,0:T(8,128)(2,1)S(1)} %get-tuple-element.60), channel_id=1, source_target_pairs={{0,8},{1,9},{2,10},{3,11},{4,12},{5,13},{6,14},{7,15},{8,0},{9,1},... | collective-permute-start | bytes 786440 | tf_op jit(solution)/shard_map/ppermute | solution.py:427
  56.4 11.9 %collective-permute-start.16 = (bf16[8,128,128]{2,1,0:T(8,128)(2,1)S(1)}, bf16[8,128,128]{2,1,0:T(8,128)(2,1)S(1)}, u32[]{:S(2)}, u32[]{:S(2)}) collective-permute-start(bf16[8,128,128]{2,1,0:T(8,128)(2,1)S(1)} %get-tuple-element.61), channel_id=1, source_target_pairs={{0,4},{1,5},{2,6},{3,7},{4,8},{5,9},{6,10},{7,11},{8,12},{9,13},{1... | collective-permute-start | bytes 786440 | tf_op jit(solution)/shard_map/ppermute | solution.py:427
  56.8 11.5 %collective-permute-start.17 = (bf16[8,128,128]{2,1,0:T(8,128)(2,1)S(1)}, bf16[8,128,128]{2,1,0:T(8,128)(2,1)S(1)}, u32[]{:S(2)}, u32[]{:S(2)}) collective-permute-start(bf16[8,128,128]{2,1,0:T(8,128)(2,1)S(1)} %get-tuple-element.62), channel_id=1, source_target_pairs={{0,12},{1,13},{2,14},{3,15},{4,0},{5,1},{6,2},{7,3},{8,4},{9,5},{1... | collective-permute-start | bytes 786440 | tf_op jit(solution)/shard_map/ppermute | solution.py:427
  70.5 4.2 %collective-permute-start.18 = (bf16[16,128,128]{2,1,0:T(8,128)(2,1)S(1)}, bf16[16,128,128]{2,1,0:T(8,128)(2,1)S(1)}, u32[]{:S(2)}, u32[]{:S(2)}) collective-permute-start(bf16[16,128,128]{2,1,0:T(8,128)(2,1)S(1)} %get-tuple-element.65), channel_id=1, source_target_pairs={{0,16},{16,0},{32,48},{48,32},{64,80},{80,64},{96,112},{112,96},{1... | collective-permute-start | bytes 1572872 | tf_op jit(solution)/shard_map/ppermute | solution.py:435
  75.1 7.1 %collective-permute-start.19 = (bf16[4,128,128]{2,1,0:T(8,128)(2,1)S(1)}, bf16[4,128,128]{2,1,0:T(8,128)(2,1)S(1)}, u32[]{:S(2)}, u32[]{:S(2)}) collective-permute-start(bf16[4,128,128]{2,1,0:T(8,128)(2,1)S(1)} %get-tuple-element.67), channel_id=1, source_target_pairs={{0,32},{16,48},{32,64},{48,80},{64,96},{80,112},{96,0},{112,16},{1... | collective-permute-start | bytes 393224 | tf_op jit(solution)/shard_map/ppermute | solution.py:431
  76.5 10.0 %collective-permute-start.20 = (bf16[4,128,128]{2,1,0:T(8,128)(2,1)S(1)}, bf16[4,128,128]{2,1,0:T(8,128)(2,1)S(1)}, u32[]{:S(2)}, u32[]{:S(2)}) collective-permute-start(bf16[4,128,128]{2,1,0:T(8,128)(2,1)S(1)} %get-tuple-element.68), channel_id=1, source_target_pairs={{0,64},{16,80},{32,96},{48,112},{64,0},{80,16},{96,32},{112,48},{1... | collective-permute-start | bytes 393224 | tf_op jit(solution)/shard_map/ppermute | solution.py:431
  80.2 6.3 %collective-permute-start.21 = (bf16[4,128,128]{2,1,0:T(8,128)(2,1)S(1)}, bf16[4,128,128]{2,1,0:T(8,128)(2,1)S(1)}, u32[]{:S(2)}, u32[]{:S(2)}) collective-permute-start(bf16[4,128,128]{2,1,0:T(8,128)(2,1)S(1)} %get-tuple-element.69), channel_id=1, source_target_pairs={{0,96},{16,112},{32,0},{48,16},{64,32},{80,48},{96,64},{112,80},{1... | collective-permute-start | bytes 393224 | tf_op jit(solution)/shard_map/ppermute | solution.py:431
  86.9 4.8 %collective-permute-start.22 = (bf16[2,128,128]{2,1,0:T(8,128)(2,1)S(1)}, bf16[2,128,128]{2,1,0:T(8,128)(2,1)S(1)}, u32[]{:S(2)}, u32[]{:S(2)}) collective-permute-start(bf16[2,128,128]{2,1,0:T(8,128)(2,1)S(1)} %get-tuple-element.71), channel_id=1, source_target_pairs={{0,32},{16,48},{32,64},{48,80},{64,96},{80,112},{96,0},{112,16},{1... | collective-permute-start | bytes 196616 | tf_op jit(solution)/shard_map/ppermute | solution.py:431
  87.0 5.5 %collective-permute-start.23 = (bf16[2,128,128]{2,1,0:T(8,128)(2,1)S(1)}, bf16[2,128,128]{2,1,0:T(8,128)(2,1)S(1)}, u32[]{:S(2)}, u32[]{:S(2)}) collective-permute-start(bf16[2,128,128]{2,1,0:T(8,128)(2,1)S(1)} %get-tuple-element.72), channel_id=1, source_target_pairs={{0,64},{16,80},{32,96},{48,112},{64,0},{80,16},{96,32},{112,48},{1... | collective-permute-start | bytes 196616 | tf_op jit(solution)/shard_map/ppermute | solution.py:431
  90.1 3.8 %collective-permute-start.24 = (bf16[2,128,128]{2,1,0:T(8,128)(2,1)S(1)}, bf16[2,128,128]{2,1,0:T(8,128)(2,1)S(1)}, u32[]{:S(2)}, u32[]{:S(2)}) collective-permute-start(bf16[2,128,128]{2,1,0:T(8,128)(2,1)S(1)} %get-tuple-element.73), channel_id=1, source_target_pairs={{0,96},{16,112},{32,0},{48,16},{64,32},{80,48},{96,64},{112,80},{1... | collective-permute-start | bytes 196616 | tf_op jit(solution)/shard_map/ppermute | solution.py:431
  94.9 3.6 %collective-permute-start.25 = (bf16[8,128,128]{2,1,0:T(8,128)(2,1)S(1)}, bf16[8,128,128]{2,1,0:T(8,128)(2,1)S(1)}, u32[]{:S(2)}, u32[]{:S(2)}) collective-permute-start(bf16[8,128,128]{2,1,0:T(8,128)(2,1)S(1)} %get-tuple-element.75), channel_id=1, source_target_pairs={{0,16},{16,0},{32,48},{48,32},{64,80},{80,64},{96,112},{112,96},{1... | collective-permute-start | bytes 786440 | tf_op jit(solution)/shard_map/ppermute | solution.py:435

commit v4 on v3

--- a/solution.py
+++ b/solution.py
@@ -12,6 +12,7 @@
 UNROLL = 16
 CHUNKS = 8
 CELL_MASK, PIVOT_BIT, FAR_BIT, NEAR_BIT, SLOT_BIT = 511, 9, 16, 17, 20
+SECOND = ((0, 3), (1, 2), (0, 2), (1, 1), (0, 1), (1, 3))
 MIB = 1 << 20
 
 ANY = pl.BlockSpec(memory_space=pl.ANY)
@@ -55,14 +56,14 @@
     return pairs
 
 
-def cross_kernel(first, sizes, flag, index_ref, table_ref, left_ref, right_ref, *refs):
+def cross_kernel(first, sizes, flag, unroll, index_ref, table_ref, left_ref, right_ref, *refs):
     outs = refs[-8 - len(sizes) : -8]
     listed, left, right, total, table, lsem, rsem, tsem = refs[-8:]
     cells = sum(sizes)
     slots = left.shape[0]
     table_copy = pltpu.make_async_copy(table_ref, table, tsem)
     table_copy.start()
-    pairs = bulk(left_ref, right_ref, left, right, lsem, rsem)
+    bulk(left_ref, right_ref, left, right, lsem, rsem)
 
     def note(i, n):
         word = index_ref[i]
@@ -70,7 +71,7 @@
         return n + ((word >> flag) & 1)
 
     count = lax.fori_loop(0, slots, note, 0, unroll=32)
-    for u in range(UNROLL):
+    for u in range(unroll):
         listed[count + u] = first + cells
 
     def clear(c, _):
@@ -79,20 +80,27 @@
 
     lax.fori_loop(0, cells + 1, clear, 0, unroll=8)
     table_copy.wait()
-    for pair in pairs:
-        for c in pair:
-            c.wait()
-
-    def work(r, _):
-        words = [listed[r * UNROLL + u] for u in range(UNROLL)]
+    per = slots // CHUNKS
+
+    def landed(k, _):
+        part = pl.ds(k * per, per)
+        pltpu.make_async_copy(left_ref.at[part], left.at[part], lsem.at[k]).wait()
+        pltpu.make_async_copy(right_ref.at[part], right.at[part], rsem.at[k]).wait()
+        return 0
+
+    def work(r, ready):
+        words = [listed[r * unroll + u] for u in range(unroll)]
+        last = listed[jnp.minimum(r * unroll + unroll, count) - 1] >> SLOT_BIT
+        lax.fori_loop(ready, last // per + 1, landed, 0)
         scaled = [mm(left[w >> SLOT_BIT], table[(w >> PIVOT_BIT) & 3]).astype(bf16) for w in words]
         updates = [mm(x, right[w >> SLOT_BIT]) for x, w in zip(scaled, words)]
         for w, u in zip(words, updates):
             c = (w & CELL_MASK) - first
             total[c] = (total[c].astype(f32) + u).astype(bf16)
-        return 0
-
-    lax.fori_loop(0, (count + UNROLL - 1) // UNROLL, work, 0)
+        return last // per + 1
+
+    ready = lax.fori_loop(0, (count + unroll - 1) // unroll, work, 0)
+    lax.fori_loop(ready, CHUNKS, landed, 0)
 
     start = 0
     for out, size in zip(outs, sizes):
@@ -105,16 +113,16 @@
         start += size
 
 
-def cross_sums(first, sizes, flag, index, table, left, right, live, order=()):
+def cross_sums(first, sizes, flag, unroll, index, table, left, right, live):
     cells = sum(sizes)
     slots = left.shape[0]
     return pl.pallas_call(
-        functools.partial(cross_kernel, first, sizes, flag),
+        functools.partial(cross_kernel, first, sizes, flag, unroll),
         out_shape=[jax.ShapeDtypeStruct((n, B, B), bf16) for n in sizes],
-        in_specs=[SMEM, HBM, HBM, HBM] + [ANY] * len(order),
+        in_specs=[SMEM, HBM, HBM, HBM],
         out_specs=[VMEM] * len(sizes),
         scratch_shapes=[
-            pltpu.SMEM((slots + UNROLL,), jnp.int32),
+            pltpu.SMEM((slots + unroll,), jnp.int32),
             pltpu.VMEM((slots, B, B), bf16),
             pltpu.VMEM((slots, B, B), bf16),
             pltpu.VMEM((cells + 1, B, B), bf16),
@@ -128,11 +136,11 @@
             flops=live * 4 * B**3, bytes_accessed=slots * 4 * B * B + cells * 2 * B * B, transcendentals=0
         ),
         name="cross_sums",
-    )(index, stay(table), stay(left), stay(right), *order)
+    )(index, stay(table), stay(left), stay(right))
 
 
 def local_kernel(index_ref, table_ref, coupling_ref, left_ref, right_ref, diag_ref, seed_ref, *refs):
-    base_ref, offset_ref, left, right, table, lsem, rsem, tsem = refs[-8:]
+    base_ref, keep_ref, give_ref, held, left, right, table, lsem, rsem, tsem = refs[-10:]
     slots = left.shape[0]
     rows = coupling_ref.shape[0]
     half = rows // 2
@@ -147,10 +155,13 @@
         dh, dl = split(diag_ref[r])
         sh, sl = split(seed_ref[r])
         o = mm_nt(sh, dh) + (mm_nt(sh, dl) + mm_nt(sl, dh))
-        offset_ref[(r + core * half) % rows] = o.astype(bf16)
+        held[(r + core * half) % rows] = o.astype(bf16)
         return 0
 
     lax.fori_loop(0, rows, offset, 0, unroll=4)
+    for i in range(half):
+        keep_ref[i] = held[i]
+        give_ref[i] = held[half + i]
     table_copy.wait()
     per = slots // CHUNKS
     for k, pair in enumerate(pairs):
@@ -175,10 +186,11 @@
     rows = coupling.shape[0]
     return pl.pallas_call(
         local_kernel,
-        out_shape=[jax.ShapeDtypeStruct((rows, B, B), f32), jax.ShapeDtypeStruct((rows, B, B), bf16)],
+        out_shape=[jax.ShapeDtypeStruct((rows, B, B), f32)] + [jax.ShapeDtypeStruct((rows // 2, B, B), bf16)] * 2,
         in_specs=[SMEM, HBM, VMEM, HBM, HBM, VMEM, VMEM] + [ANY] * len(order),
-        out_specs=[VMEM, VMEM],
+        out_specs=[VMEM] * 3,
         scratch_shapes=[
+            pltpu.VMEM((rows, B, B), bf16),
             pltpu.VMEM((slots, B, B), bf16),
             pltpu.VMEM((slots, B, B), bf16),
             pltpu.VMEM(table.shape, bf16),
@@ -195,15 +207,15 @@
 
 
 def first_totals_kernel(own_x, own_z, *refs):
-    arrivals = refs[:8]
     outs = refs[-2 * SIDE :]
-    q = arrivals[0].shape[0] // SIDE
+    q = own_x.shape[0] // (2 * SIDE)
     for s, own in enumerate((own_x, own_z)):
+        plus, minus = refs[2 * s : 2 * s + 2]
         for half in range(2):
             for b in range(SIDE):
                 t = own[pl.ds((half * SIDE + b) * q, q)].astype(f32)
-                for a in arrivals[s * 4 + half * 2 : s * 4 + half * 2 + 2]:
-                    t = t + a[pl.ds(b * q, q)].astype(f32)
+                t = t + plus[pl.ds(((1 - half) * SIDE + b) * q, q)].astype(f32)
+                t = t + minus[pl.ds((half * SIDE + b) * q, q)].astype(f32)
                 outs[s * SIDE + b][pl.ds(half * q, q)] = t.astype(bf16)
 
 
@@ -212,7 +224,7 @@
     outs = pl.pallas_call(
         first_totals_kernel,
         out_shape=[jax.ShapeDtypeStruct((half, B, B), bf16)] * (2 * SIDE),
-        in_specs=[VMEM] * 10 + [ANY] * len(order),
+        in_specs=[VMEM] * 6 + [ANY] * len(order),
         out_specs=[VMEM] * (2 * SIDE),
         compiler_params=pltpu.CompilerParams(vmem_limit_bytes=9 * MIB),
         cost_estimate=pl.CostEstimate(flops=0, bytes_accessed=256 * 2 * B * B, transcendentals=0),
@@ -221,13 +233,13 @@
     return outs[:SIDE], outs[SIDE:]
 
 
-def coupling_kernel(base_ref, diag_ref, offset_ref, *refs):
+def coupling_kernel(base_ref, diag_ref, *refs):
     new_ref, keep_ref, give_ref, held = refs[-4:]
     rows = base_ref.shape[0]
     half = rows // 2
     core = lax.axis_index("section") % 2
     for s in range(2):
-        parts = refs[s * 4 : s * 4 + 4]
+        parts = [refs[s]] + [refs[2 + i] for i, (t, _) in enumerate(SECOND) if t == s]
 
         def finish(i, _, s=s, parts=parts):
             r = s * half + i
@@ -244,10 +256,9 @@
     for i in range(half):
         keep_ref[i] = held[i]
         give_ref[i] = held[half + i]
-        give_ref[half + i] = offset_ref[half + i]
-
-
-def coupling_and_step(base, diag, offsets, parts_x, parts_z):
+
+
+def coupling_and_step(base, diag, own, parts):
     rows = base.shape[0]
     half = rows // 2
     return pl.pallas_call(
@@ -255,18 +266,18 @@
         out_shape=[
             jax.ShapeDtypeStruct((rows, B, B), f32),
             jax.ShapeDtypeStruct((half, B, B), bf16),
-            jax.ShapeDtypeStruct((rows, B, B), bf16),
+            jax.ShapeDtypeStruct((half, B, B), bf16),
         ],
-        in_specs=[VMEM] * 11,
+        in_specs=[VMEM] * 10,
         out_specs=[VMEM] * 3,
         scratch_shapes=[pltpu.VMEM((rows, B, B), bf16)],
         compiler_params=pltpu.CompilerParams(vmem_limit_bytes=9 * MIB),
         cost_estimate=pl.CostEstimate(flops=rows * 6 * B**3, bytes_accessed=rows * 22 * B * B, transcendentals=0),
         name="coupling_and_step",
-    )(base, diag, offsets, *parts_x, *parts_z)
-
-
-def compose_kernel(chips, keep_ref, offset_ref, got_ref, *outs):
+    )(base, diag, *own, *parts)
+
+
+def compose_kernel(chips, keep_ref, offset_ref, got_ref, got_offset_ref, *outs):
     section = lax.axis_index("section")
     chip = section // 2
     half = keep_ref.shape[0]
@@ -277,7 +288,7 @@
             for j in range(per):
                 i = (chip + k) % chips * per + j
                 mine = (keep_ref[i], offset_ref[i])
-                other = (got_ref[i], got_ref[half + i])
+                other = (got_ref[i], got_offset_ref[i])
                 (ma, oa), (mb, ob) = (mine, other) if first else (other, mine)
                 outs[k][j] = mm(ma, mb).astype(bf16)
                 outs[k][per + j] = (oa.astype(f32) + mm_nt(ob, ma)).astype(bf16)
@@ -291,17 +302,17 @@
         compose(False)
 
 
-def compose(chips, keep, offsets, got):
+def compose(chips, keep, offsets, got, got_offsets):
     half = keep.shape[0]
     return pl.pallas_call(
         functools.partial(compose_kernel, chips),
         out_shape=[jax.ShapeDtypeStruct((2 * half // chips, B, B), bf16)] * chips,
-        in_specs=[VMEM] * 3,
+        in_specs=[VMEM] * 4,
         out_specs=[VMEM] * chips,
         compiler_params=pltpu.CompilerParams(vmem_limit_bytes=4 * MIB),
         cost_estimate=pl.CostEstimate(flops=half * 4 * B**3, bytes_accessed=half * 12 * B * B, transcendentals=0),
         name="compose",
-    )(keep, offsets, got)
+    )(keep, offsets, got, got_offsets)
 
 
 def chain_kernel(chips, *refs):
@@ -345,7 +356,7 @@
     )(*parts)
 
 
-def expand_kernel(chips, keep_ref, offset_ref, got_ref, *refs):
+def expand_kernel(chips, keep_ref, offset_ref, got_ref, got_offset_ref, *refs):
     parts = refs[:chips]
     mine_ref, other_ref = refs[chips:]
     section = lax.axis_index("section")
@@ -358,7 +369,7 @@
             for j in range(per):
                 i = (chip - k + chips) % chips * per + j
                 mine = (keep_ref[i], offset_ref[i])
-                other = (got_ref[i], got_ref[half + i])
+                other = (got_ref[i], got_offset_ref[i])
                 (ma, oa), (mb, ob) = (mine, other) if first else (other, mine)
                 b = ob.astype(f32) + mm_nt(parts[k][j], mb)
                 high, low = split(b)
@@ -375,18 +386,18 @@
         expand(False)
 
 
-def expand(keep, offsets, got, parts):
+def expand(keep, offsets, got, got_offsets, parts):
     chips = len(parts)
     half = keep.shape[0]
     return pl.pallas_call(
         functools.partial(expand_kernel, chips),
         out_shape=[jax.ShapeDtypeStruct((half, B, B), f32), jax.ShapeDtypeStruct((half, B, B), bf16)],
-        in_specs=[VMEM] * (3 + chips),
+        in_specs=[VMEM] * (4 + chips),
         out_specs=[VMEM] * 2,
         compiler_params=pltpu.CompilerParams(vmem_limit_bytes=4 * MIB),
         cost_estimate=pl.CostEstimate(flops=half * 6 * B**3, bytes_accessed=half * 16 * B * B, transcendentals=0),
         name="expand",
-    )(keep, offsets, got, *parts)
+    )(keep, offsets, got, got_offsets, *parts)
 
 
 def gather_kernel(mine_ref, got_ref, out_ref, held, sem):
@@ -427,8 +438,13 @@
     return lax.ppermute(x, "row", pairs)
 
 
-def across(x, sections, by):
-    return lax.ppermute(x, "section", [(i, (i + 2 * by) % sections) for i in range(sections)])
+def maps_across(x, sections, by):
+    return lax.ppermute(x, "section", [(i, (i + 2 * by) % sections) for i in range(2, sections)])
+
+
+def incoming_across(x, sections, by):
+    pairs = [(i, (i + 2 * by) % sections) for i in range(sections)]
+    return lax.ppermute(x, "section", [p for p in pairs if p[1] < sections - 2])
 
 
 def partner(x, sections):
@@ -480,7 +496,7 @@
         jnp.where(
             a == 0,
             3 * group + second * 2 * n + upper * n + spot,
-            jnp.where(minus == upper, 2 * group, group) + second * 2 * n + minus * n + spot,
+            group + (second * 2 + minus) * 2 * n + jnp.where(minus == upper, n, 0) + spot,
         ),
     )
     slot = jnp.arange(slots, dtype=jnp.int32)
@@ -490,34 +506,29 @@
     local_word = local_target | (local_pivot << PIVOT_BIT)
 
     sums = functools.partial(cross_sums, index=word, table=pivot_inverse, left=cross_left, right=cross_right)
-    far = sums(0, [n] * 4, FAR_BIT, live=slots // 4)
+    far = sums(0, [n] * 4, FAR_BIT, 8, live=slots // 4)
     ways = ((0, 1), (0, -1), (1, 1), (1, -1))
     far_in = [moved(x, *w) for x, w in zip(far, ways)]
-    near = sums(group, [n] * 8 + [2 * n] * 2, NEAR_BIT, live=slots * 3 // 4)
-    free_in = [moved(x, *w) for x, w in zip(near[:4], ways)]
-    joined = [add(x, y) for x, y in zip(near[4:8], far_in)]
-    joined_in = [moved(x, *w) for x, w in zip(joined, ways)]
-
-    base, offsets = local_and_offset(
+    near = sums(group, [2 * n] * 6, NEAR_BIT, UNROLL, live=slots * 3 // 4)
+    joined = [lax.dynamic_update_slice_in_dim(x, add(x[n:], y), n, 0) for x, y in zip(near, far_in)]
+    arrivals = [moved(x, *w) for x, w in zip(joined, ways)]
+
+    base, offsets, give_offsets = local_and_offset(
         local_word, pivot_inverse, coupling, local_left, local_right, diag_inverse, adjoint_seed, joined
     )
-
-    arrivals = []
-    for s in range(2):
-        fp, fm = free_in[2 * s : 2 * s + 2]
-        jp, jm = joined_in[2 * s : 2 * s + 2]
-        arrivals += [jp, fm, fp, jm]
-    tot_x, tot_z = first_totals(near[8], near[9], arrivals, [base])
-    parts_x = [tot_x[0]] + [moved(tot_x[k], 1, k) for k in (2, 1, 3)]
-    parts_z = [tot_z[0]] + [moved(tot_z[k], 0, k) for k in (2, 1, 3)]
-    updated, keep, give = coupling_and_step(base, diag_inverse, offsets, parts_x, parts_z)
+    got_offsets = partner(give_offsets, sections)
+
+    tot_x, tot_z = first_totals(near[4], near[5], arrivals, [base, got_offsets])
+    totals = (tot_x, tot_z)
+    parts = [moved(totals[s][k], 1 - s, k) for s, k in SECOND]
+    updated, keep, give = coupling_and_step(base, diag_inverse, (tot_x[0], tot_z[0]), parts)
     chips = sections // 2
     got = partner(give, sections)
-    maps = compose(chips, keep, offsets, got)
-    maps = [maps[0]] + [across(maps[k], sections, k) for k in range(1, chips)]
+    maps = compose(chips, keep, offsets, got, got_offsets)
+    maps = [maps[0]] + [maps_across(maps[k], sections, k) for k in range(1, chips)]
     incoming = run_chains(maps)
-    incoming = [incoming[0]] + [across(incoming[k], sections, k) for k in range(1, chips)]
-    mine, other = expand(keep, offsets, got, incoming)
+    incoming = [incoming[0]] + [incoming_across(incoming[k], sections, k) for k in range(1, chips)]
+    mine, other = expand(keep, offsets, got, got_offsets, incoming)
     adjoint = gather_rows(mine, partner(other, sections))
     return (updated, adjoint)
 

time: 99.8 us -> 110 us (1.10)
  waiting for transfers between devices: 26.2 us -> 40.7 us
  starting transfers between devices: 44.7 us -> 38.8 us
    ppermute x18 -> x14, starting transfers between devices: 27.7 us -> 19.8 us  [moved(): return lax.ppermute(x, 'row', pairs)]
    ppermute x6, waiting for transfers between devices: 6.43 us -> 13.7 us  [the longest x3 10 us: maps_across(): lax.ppermute(x, 'section', [(i, (i + 2 * by) % sections) for i in range(2...]
    ppermute x18 -> x14, waiting for transfers between devices: 17.1 us -> 23.5 us  [moved(): return lax.ppermute(x, 'row', pairs)]
    ppermute x2 -> x3, starting transfers between devices: 5.16 us -> 9.71 us  [partner(): return lax.ppermute(x, 'section', [(i, i ^ 1) for i in range(sections)])]
    ppermute x6, starting transfers between devices: 11.9 us -> 9.24 us  [the longest x3 5.37 us: incoming_across(): return lax.ppermute(x, 'section', [p for p in pairs if p[1] < sections - 2])]
    dynamic_update_slice x0 -> x4, other arithmetic: none -> 1.17 us  [per_device(): lax.dynamic_update_slice_in_dim(x, add(x[n:], y), n, 0)]
    ppermute x2 -> x3, waiting for transfers between devices: 2.7 us -> 3.49 us  [partner(): return lax.ppermute(x, 'section', [(i, i ^ 1) for i in range(sections)])]
  transfers between devices with their start and end apart: 26 -> 23, of which waited for: 10 -> 17; matrix products, arithmetic and copies ran while one was open for 1% -> 1% of each run, Pallas kernels for 15% -> 13%
where the time goes in v4:
time: 110 us; the launch traced here: 109 us
  waiting for transfers between devices  40.7 us (37%)
  starting transfers between devices  38.8 us (35%)
  Pallas kernels  25.7 us (23%)
  other arithmetic  1.89 us (2%)
  between operations  1.69 us (2%)
    ppermute x14, waiting for transfers between devices, moved(): return lax.ppermute(x, 'row', pairs)  23.5 us
    ppermute x14, starting transfers between devices, moved(): return lax.ppermute(x, 'row', pairs)  19.8 us
    pallas_call x2, Pallas kernels, cross_sums(): pl.pallas_call(functools.partial(cross_kernel, first, sizes, flag, unroll...  12.8 us
    ppermute x3, waiting for transfers between devices, maps_across(): lax.ppermute(x, 'section', [(i, (i + 2 * by) % sections) for i in range(2...  10 us
    ppermute x3, starting transfers between devices, partner(): return lax.ppermute(x, 'section', [(i, i ^ 1) for i in range(sections)])  9.71 us
    pallas_call x1, Pallas kernels, local_and_offset(): pl.pallas_call(local_kernel, out_shape=[jax.ShapeDtypeStruct((rows, B, B)...  7.38 us
    ppermute x3, starting transfers between devices, incoming_across(): return lax.ppermute(x, 'section', [p for p in pairs if p[1] < sections - 2])  5.37 us
    ppermute x3, starting transfers between devices, maps_across(): lax.ppermute(x, 'section', [(i, (i + 2 * by) % sections) for i in range(2...  3.87 us
  transfers between devices with their start and end apart: 23, of which 17 were waited for; matrix products, arithmetic and copies ran while one was open for 1% of the time, Pallas kernels for 13%

profile of v4, /device:TPU:1, one launch (start us, length us, event | category | flops | bytes accessed | tf_op | source)
XLA Modules:
  0.0 108.8 jit_solution(11692777881951370638)
XLA Ops:
  1.3 0.7 fusion.9.index_ref
  2.0 5.5 %cross_sums.3 = (bf16[16,128,128]{2,1,0:T(8,128)(2,1)S(1)}, bf16[16,128,128]{2,1,0:T(8,128)(2,1)S(1)}, bf16[16,128,128]{2,1,0:T(8,128)(2,1)S(1)}, bf16[16,128,128]{2,1,0:T(8,128)(2,1)S(1)}) custom-call(s32[128]{0:T(128)S(1)} %fusion.9.index_ref, bf16[4,128,128]{2,1,0:T(8,128)(2,1)} %table_ref.5, bf16[128,128,128]{2,1,0:T(8,128)(2,1)} %left_ref.4, ...), custom_call_target="tpu_custom_call" | custom-call | flops 268435456 | bytes 10485760 | tf_op jit(solution)/shard_map/cross_sums/pallas_call | solution.py:119
  7.5 3.8 %collective-permute-start.1 = (bf16[16,128,128]{2,1,0:T(8,128)(2,1)S(1)}, bf16[16,128,128]{2,1,0:T(8,128)(2,1)S(1)}, u32[]{:S(2)}, u32[]{:S(2)}) collective-permute-start(bf16[16,128,128]{2,1,0:T(8,128)(2,1)S(1)} %get-tuple-element.39), channel_id=1, source_target_pairs={{0,12},{1,13},{2,14},{3,15},{4,0},{5,1},{6,2},{7,3},{8,4},{9,5},{1... | collective-permute-start | bytes 1572872 | tf_op jit(solution)/shard_map/ppermute | solution.py:438
  11.3 1.2 %collective-permute-start.2 = (bf16[16,128,128]{2,1,0:T(8,128)(2,1)S(1)}, bf16[16,128,128]{2,1,0:T(8,128)(2,1)S(1)}, u32[]{:S(2)}, u32[]{:S(2)}) collective-permute-start(bf16[16,128,128]{2,1,0:T(8,128)(2,1)S(1)} %get-tuple-element.41), channel_id=1, source_target_pairs={{0,1},{1,2},{2,3},{3,0},{4,5},{5,6},{6,7},{7,4},{8,9},{9,10},{10,1... | collective-permute-start | bytes 1572872 | tf_op jit(solution)/shard_map/ppermute | solution.py:438
  12.5 2.5 %collective-permute-start.3 = (bf16[16,128,128]{2,1,0:T(8,128)(2,1)S(1)}, bf16[16,128,128]{2,1,0:T(8,128)(2,1)S(1)}, u32[]{:S(2)}, u32[]{:S(2)}) collective-permute-start(bf16[16,128,128]{2,1,0:T(8,128)(2,1)S(1)} %get-tuple-element.43), channel_id=1, source_target_pairs={{0,3},{1,0},{2,1},{3,2},{4,7},{5,4},{6,5},{7,6},{8,11},{9,8},{10,9... | collective-permute-start | bytes 1572872 | tf_op jit(solution)/shard_map/ppermute | solution.py:438
  15.0 7.3 %cross_sums.2 = (bf16[32,128,128]{2,1,0:T(8,128)(2,1)S(1)}, bf16[32,128,128]{2,1,0:T(8,128)(2,1)S(1)}, bf16[32,128,128]{2,1,0:T(8,128)(2,1)S(1)}, bf16[32,128,12...) custom-call(s32[128]{0:T(128)S(1)} %fusion.9.index_ref, ...), custom_call_target="tpu_custom_call" | custom-call | flops 805306368 | bytes 14680064 | tf_op jit(solution)/shard_map/cross_sums/pallas_call | solution.py:119
  22.4 0.3 fusion.1.refs_1_
  22.7 3.0 %collective-permute-start.5 = (bf16[32,128,128]{2,1,0:T(8,128)(2,1)S(1)}, bf16[32,128,128]{2,1,0:T(8,128)(2,1)S(1)}, u32[]{:S(2)}, u32[]{:S(2)}) collective-permute-start(bf16[32,128,128]{2,1,0:T(8,128)(2,1)S(1)} %fusion.1.refs_1_), channel_id=1, source_target_pairs={{0,12},{1,13},{2,14},{3,15},{4,0},{5,1},{6,2},{7,3},{8,4},{9,5},{1... | collective-permute-start | bytes 3145736 | tf_op jit(solution)/shard_map/ppermute | solution.py:438
  25.6 1.1 %collective-permute-done.2 = bf16[16,128,128]{2,1,0:T(8,128)(2,1)S(1)} collective-permute-done((bf16[16,128,128]{2,1,0:T(8,128)(2,1)S(1)}, bf16[16,128,128]{2,1,0:T(8,128)(2,1)S(1)}, u32[]{:S(2)}, u32[]{:S(2)}) %collective-permute-start.2) | collective-permute-done | bytes 524320 | tf_op jit(solution)/shard_map/ppermute | solution.py:438
  26.8 0.3 fusion.2.refs_2_
  27.2 0.3 fusion.3.refs_3_
  27.5 3.0 %collective-permute-start.7 = (bf16[32,128,128]{2,1,0:T(8,128)(2,1)S(1)}, bf16[32,128,128]{2,1,0:T(8,128)(2,1)S(1)}, u32[]{:S(2)}, u32[]{:S(2)}) collective-permute-start(bf16[32,128,128]{2,1,0:T(8,128)(2,1)S(1)} %fusion.3.refs_3_), channel_id=1, source_target_pairs={{0,3},{1,0},{2,1},{3,2},{4,7},{5,4},{6,5},{7,6},{8,11},{9,8},{10,9... | collective-permute-start | bytes 3145736 | tf_op jit(solution)/shard_map/ppermute | solution.py:438
  30.6 0.3 fusion.refs_0_
  31.0 7.4 %local_and_offset.1 = (f32[16,128,128]{2,1,0:T(8,128)S(1)}, bf16[8,128,128]{2,1,0:T(8,128)(2,1)S(1)}, bf16[8,128,128]{2,1,0:T(8,128)(2,1)S(1)}) custom-call(s32[128]{0:T(128)S(1)} %shift-left_or_fusion.index_ref, bf16[4,128,128]{2,1,0:T(8,128)(2,1)} %table_ref.5, bf16[16,128,128]{2,1,0:T(8,128)(2,1)S(1)} %copy-done.2, bf16[128,128,128]{2,1,0:T(8,128)(2,1)} %left_ref.5, ...), custom_call_target="tpu_custom_call" | custom-call | flops 1073741824 | bytes 12582912 | tf_op jit(solution)/shard_map/local_and_offset/pallas_call | solution.py:187
  38.4 1.7 %collective-permute-start.8 = (bf16[8,128,128]{2,1,0:T(8,128)(2,1)S(1)}, bf16[8,128,128]{2,1,0:T(8,128)(2,1)S(1)}, u32[]{:S(2)}, u32[]{:S(2)}) collective-permute-start(bf16[8,128,128]{2,1,0:T(8,128)(2,1)S(1)} %get-tuple-element.47), channel_id=1, source_target_pairs={{0,16},{16,0},{32,48},{48,32},{64,80},{80,64},{96,112},{112,96},{1... | collective-permute-start | bytes 786440 | tf_op jit(solution)/shard_map/ppermute | solution.py:451
  40.1 1.2 %collective-permute-done.8.refs_5_.got_offset_ref = bf16[8,128,128]{2,1,0:T(8,128)(2,1)S(1)} collective-permute-done((bf16[8,128,128]{2,1,0:T(8,128)(2,1)S(1)}, bf16[8,128,128]{2,1,0:T(8,128)(2,1)S(1)}, u32[]{:S(2)}, u32[]{:S(2)}) %collective-permute-start.8) | collective-permute-done | bytes 262176 | tf_op jit(solution)/shard_map/ppermute | solution.py:451
  41.3 5.2 %collective-permute-done.5.refs_1_ = bf16[32,128,128]{2,1,0:T(8,128)(2,1)S(1)} collective-permute-done((bf16[32,128,128]{2,1,0:T(8,128)(2,1)S(1)}, bf16[32,128,128]{2,1,0:T(8,128)(2,1)S(1)}, u32[]{:S(2)}, u32[]{:S(2)}) %collective-permute-start.5) | collective-permute-done | bytes 1048608 | tf_op jit(solution)/shard_map/ppermute | solution.py:438
  46.5 5.7 %collective-permute-done.6.refs_2_ = bf16[32,128,128]{2,1,0:T(8,128)(2,1)S(1)} collective-permute-done((bf16[32,128,128]{2,1,0:T(8,128)(2,1)S(1)}, bf16[32,128,128]{2,1,0:T(8,128)(2,1)S(1)}, u32[]{:S(2)}, u32[]{:S(2)}) %collective-permute-start.6) | collective-permute-done | bytes 1048608 | tf_op jit(solution)/shard_map/ppermute | solution.py:438
  52.3 0.6 collective-permute-done.7.refs_3_
  52.9 2.3 %collective-permute-done.4.refs_0_ = bf16[32,128,128]{2,1,0:T(8,128)(2,1)S(1)} collective-permute-done((bf16[32,128,128]{2,1,0:T(8,128)(2,1)S(1)}, bf16[32,128,128]{2,1,0:T(8,128)(2,1)S(1)}, u32[]{:S(2)}, u32[]{:S(2)}) %collective-permute-start.4) | collective-permute-done | bytes 1048608 | tf_op jit(solution)/shard_map/ppermute | solution.py:438
  55.1 0.7 first_totals.1
  55.9 0.3 collective-permute-start.10
  56.2 1.9 %collective-permute-start.11 = (bf16[8,128,128]{2,1,0:T(8,128)(2,1)S(1)}, bf16[8,128,128]{2,1,0:T(8,128)(2,1)S(1)}, u32[]{:S(2)}, u32[]{:S(2)}) collective-permute-start(bf16[8,128,128]{2,1,0:T(8,128)(2,1)S(1)} %get-tuple-element.52), channel_id=1, source_target_pairs={{0,2},{1,3},{2,0},{3,1},{4,6},{5,7},{6,4},{7,5},{8,10},{9,11},{10,... | collective-permute-start | bytes 786440 | tf_op jit(solution)/shard_map/ppermute | solution.py:438
  58.1 2.7 %collective-permute-start.14 = (bf16[8,128,128]{2,1,0:T(8,128)(2,1)S(1)}, bf16[8,128,128]{2,1,0:T(8,128)(2,1)S(1)}, u32[]{:S(2)}, u32[]{:S(2)}) collective-permute-start(bf16[8,128,128]{2,1,0:T(8,128)(2,1)S(1)} %get-tuple-element.55), channel_id=1, source_target_pairs={{0,12},{1,13},{2,14},{3,15},{4,0},{5,1},{6,2},{7,3},{8,4},{9,5},{1... | collective-permute-start | bytes 786440 | tf_op jit(solution)/shard_map/ppermute | solution.py:438
  60.8 2.0 %collective-permute-done.10.refs_3_ = bf16[8,128,128]{2,1,0:T(8,128)(2,1)S(1)} collective-permute-done((bf16[8,128,128]{2,1,0:T(8,128)(2,1)S(1)}, bf16[8,128,128]{2,1,0:T(8,128)(2,1)S(1)}, u32[]{:S(2)}, u32[]{:S(2)}) %collective-permute-start.10) | collective-permute-done | bytes 262176 | tf_op jit(solution)/shard_map/ppermute | solution.py:438
  62.8 1.2 %collective-permute-start.9 = (bf16[8,128,128]{2,1,0:T(8,128)(2,1)S(1)}, bf16[8,128,128]{2,1,0:T(8,128)(2,1)S(1)}, u32[]{:S(2)}, u32[]{:S(2)}) collective-permute-start(bf16[8,128,128]{2,1,0:T(8,128)(2,1)S(1)} %get-tuple-element.50), channel_id=1, source_target_pairs={{0,3},{1,0},{2,1},{3,2},{4,7},{5,4},{6,5},{7,6},{8,11},{9,8},{10,9... | collective-permute-start | bytes 786440 | tf_op jit(solution)/shard_map/ppermute | solution.py:438
  64.0 6.3 %collective-permute-done.12.refs_5_ = bf16[8,128,128]{2,1,0:T(8,128)(2,1)S(1)} collective-permute-done((bf16[8,128,128]{2,1,0:T(8,128)(2,1)S(1)}, bf16[8,128,128]{2,1,0:T(8,128)(2,1)S(1)}, u32[]{:S(2)}, u32[]{:S(2)}) %collective-permute-start.12) | collective-permute-done | bytes 262176 | tf_op jit(solution)/shard_map/ppermute | solution.py:438
  70.5 2.0 %coupling_and_step.1 = (f32[16,128,128]{2,1,0:T(8,128)}, bf16[8,128,128]{2,1,0:T(8,128)(2,1)S(1)}, bf16[8,128,128]{2,1,0:T(8,128)(2,1)S(1)}) custom-call(f32[16,128,128]{2,1,0:T(8,128)S(1)} %get-tuple-element.44.refs_4_.base_ref, f32[16,128,128]{2,1,0:T(8,128)S(1)} %copy-done, bf16[8,128,128]{2,1,0:T(8,128)(2,1)S(1)} %get-tuple-element.48.refs_0_, ...), custom_call_target="tpu_custom_call" | custom-call | flops 201326592 | bytes 5767168 | tf_op jit(solution)/shard_map/coupling_and_step/pallas_call | solution.py:264
  72.5 4.9 %collective-permute-start.15 = (bf16[8,128,128]{2,1,0:T(8,128)(2,1)S(1)}, bf16[8,128,128]{2,1,0:T(8,128)(2,1)S(1)}, u32[]{:S(2)}, u32[]{:S(2)}) collective-permute-start(bf16[8,128,128]{2,1,0:T(8,128)(2,1)S(1)} %get-tuple-element.59), channel_id=1, source_target_pairs={{0,16},{16,0},{32,48},{48,32},{64,80},{80,64},{96,112},{112,96},{1... | collective-permute-start | bytes 786440 | tf_op jit(solution)/shard_map/ppermute | solution.py:451
  77.4 1.2 %collective-permute-done.15.got_ref = bf16[8,128,128]{2,1,0:T(8,128)(2,1)S(1)} collective-permute-done((bf16[8,128,128]{2,1,0:T(8,128)(2,1)S(1)}, bf16[8,128,128]{2,1,0:T(8,128)(2,1)S(1)}, u32[]{:S(2)}, u32[]{:S(2)}) %collective-permute-start.15) | collective-permute-done | bytes 262176 | tf_op jit(solution)/shard_map/ppermute | solution.py:451
  78.6 0.4 compose.1
  79.0 1.3 %collective-permute-start.16 = (bf16[4,128,128]{2,1,0:T(8,128)(2,1)S(1)}, bf16[4,128,128]{2,1,0:T(8,128)(2,1)S(1)}, u32[]{:S(2)}, u32[]{:S(2)}) collective-permute-start(bf16[4,128,128]{2,1,0:T(8,128)(2,1)S(1)} %get-tuple-element.61), channel_id=1, source_target_pairs={{32,64},{48,80},{64,96},{80,112},{96,0},{112,16},{33,65},{49,81},{... | collective-permute-start | bytes 393224 | tf_op jit(solution)/shard_map/ppermute | solution.py:442
  80.3 1.3 %collective-permute-start.17 = (bf16[4,128,128]{2,1,0:T(8,128)(2,1)S(1)}, bf16[4,128,128]{2,1,0:T(8,128)(2,1)S(1)}, u32[]{:S(2)}, u32[]{:S(2)}) collective-permute-start(bf16[4,128,128]{2,1,0:T(8,128)(2,1)S(1)} %get-tuple-element.62), channel_id=1, source_target_pairs={{32,96},{48,112},{64,0},{80,16},{96,32},{112,48},{33,97},{49,113},... | collective-permute-start | bytes 393224 | tf_op jit(solution)/shard_map/ppermute | solution.py:442
  81.6 1.3 %collective-permute-start.18 = (bf16[4,128,128]{2,1,0:T(8,128)(2,1)S(1)}, bf16[4,128,128]{2,1,0:T(8,128)(2,1)S(1)}, u32[]{:S(2)}, u32[]{:S(2)}) collective-permute-start(bf16[4,128,128]{2,1,0:T(8,128)(2,1)S(1)} %get-tuple-element.63), channel_id=1, source_target_pairs={{32,0},{48,16},{64,32},{80,48},{96,64},{112,80},{33,1},{49,17},{65... | collective-permute-start | bytes 393224 | tf_op jit(solution)/shard_map/ppermute | solution.py:442
  82.9 5.0 %collective-permute-done.16.refs_1_ = bf16[4,128,128]{2,1,0:T(8,128)(2,1)S(1)} collective-permute-done((bf16[4,128,128]{2,1,0:T(8,128)(2,1)S(1)}, bf16[4,128,128]{2,1,0:T(8,128)(2,1)S(1)}, u32[]{:S(2)}, u32[]{:S(2)}) %collective-permute-start.16) | collective-permute-done | bytes 131104 | tf_op jit(solution)/shard_map/ppermute | solution.py:442
  87.9 3.7 %collective-permute-done.17.refs_2_ = bf16[4,128,128]{2,1,0:T(8,128)(2,1)S(1)} collective-permute-done((bf16[4,128,128]{2,1,0:T(8,128)(2,1)S(1)}, bf16[4,128,128]{2,1,0:T(8,128)(2,1)S(1)}, u32[]{:S(2)}, u32[]{:S(2)}) %collective-permute-start.17) | collective-permute-done | bytes 131104 | tf_op jit(solution)/shard_map/ppermute | solution.py:442
  91.6 1.3 %collective-permute-done.18.refs_3_ = bf16[4,128,128]{2,1,0:T(8,128)(2,1)S(1)} collective-permute-done((bf16[4,128,128]{2,1,0:T(8,128)(2,1)S(1)}, bf16[4,128,128]{2,1,0:T(8,128)(2,1)S(1)}, u32[]{:S(2)}, u32[]{:S(2)}) %collective-permute-start.18) | collective-permute-done | bytes 131104 | tf_op jit(solution)/shard_map/ppermute | solution.py:442
  92.9 0.4 run_chains.1
  93.4 2.2 %collective-permute-start.19 = (bf16[2,128,128]{2,1,0:T(8,128)(2,1)S(1)}, bf16[2,128,128]{2,1,0:T(8,128)(2,1)S(1)}, u32[]{:S(2)}, u32[]{:S(2)}) collective-permute-start(bf16[2,128,128]{2,1,0:T(8,128)(2,1)S(1)} %get-tuple-element.65), channel_id=1, source_target_pairs={{0,32},{16,48},{32,64},{48,80},{96,0},{112,16},{1,33},{17,49},{33,... | collective-permute-start | bytes 196616 | tf_op jit(solution)/shard_map/ppermute | solution.py:447
  95.5 1.9 %collective-permute-start.20 = (bf16[2,128,128]{2,1,0:T(8,128)(2,1)S(1)}, bf16[2,128,128]{2,1,0:T(8,128)(2,1)S(1)}, u32[]{:S(2)}, u32[]{:S(2)}) collective-permute-start(bf16[2,128,128]{2,1,0:T(8,128)(2,1)S(1)} %get-tuple-element.66), channel_id=1, source_target_pairs={{0,64},{16,80},{64,0},{80,16},{96,32},{112,48},{1,65},{17,81},{65,... | collective-permute-start | bytes 196616 | tf_op jit(solution)/shard_map/ppermute | solution.py:447
  97.5 1.3 %collective-permute-start.21 = (bf16[2,128,128]{2,1,0:T(8,128)(2,1)S(1)}, bf16[2,128,128]{2,1,0:T(8,128)(2,1)S(1)}, u32[]{:S(2)}, u32[]{:S(2)}) collective-permute-start(bf16[2,128,128]{2,1,0:T(8,128)(2,1)S(1)} %get-tuple-element.67), channel_id=1, source_target_pairs={{32,0},{48,16},{64,32},{80,48},{96,64},{112,80},{33,1},{49,17},{65... | collective-permute-start | bytes 196616 | tf_op jit(solution)/shard_map/ppermute | solution.py:447
  98.8 0.8 collective-permute-done.19.refs_1_
  99.6 2.5 %collective-permute-done.20.refs_2_ = bf16[2,128,128]{2,1,0:T(8,128)(2,1)S(1)} collective-permute-done((bf16[2,128,128]{2,1,0:T(8,128)(2,1)S(1)}, bf16[2,128,128]{2,1,0:T(8,128)(2,1)S(1)}, u32[]{:S(2)}, u32[]{:S(2)}) %collective-permute-start.20) | collective-permute-done | bytes 65568 | tf_op jit(solution)/shard_map/ppermute | solution.py:447
  102.0 0.4 collective-permute-done.21.refs_3_
  102.5 1.0 expand.1
  103.4 3.0 %collective-permute-start.22 = (bf16[8,128,128]{2,1,0:T(8,128)(2,1)S(1)}, bf16[8,128,128]{2,1,0:T(8,128)(2,1)S(1)}, u32[]{:S(2)}, u32[]{:S(2)}) collective-permute-start(bf16[8,128,128]{2,1,0:T(8,128)(2,1)S(1)} %get-tuple-element.69), channel_id=1, source_target_pairs={{0,16},{16,0},{32,48},{48,32},{64,80},{80,64},{96,112},{112,96},{1... | collective-permute-start | bytes 786440 | tf_op jit(solution)/shard_map/ppermute | solution.py:451
  106.5 1.2 %collective-permute-done.22.got_ref = bf16[8,128,128]{2,1,0:T(8,128)(2,1)S(1)} collective-permute-done((bf16[8,128,128]{2,1,0:T(8,128)(2,1)S(1)}, bf16[8,128,128]{2,1,0:T(8,128)(2,1)S(1)}, u32[]{:S(2)}, u32[]{:S(2)}) %collective-permute-start.22) | collective-permute-done | bytes 262176 | tf_op jit(solution)/shard_map/ppermute | solution.py:451
  107.7 1.0 gather_rows.1
  (23 shorter events, 0.5 us)
Async XLA Ops:
  7.5 14.9 %collective-permute-start.1 = (bf16[16,128,128]{2,1,0:T(8,128)(2,1)S(1)}, bf16[16,128,128]{2,1,0:T(8,128)(2,1)S(1)}, u32[]{:S(2)}, u32[]{:S(2)}) collective-permute-start(bf16[16,128,128]{2,1,0:T(8,128)(2,1)S(1)} %get-tuple-element.39), channel_id=1, source_target_pairs={{0,12},{1,13},{2,14},{3,15},{4,0},{5,1},{6,2},{7,3},{8,4},{9,5},{1... | collective-permute-start | bytes 1572872 | tf_op jit(solution)/shard_map/ppermute | solution.py:438
  11.3 15.5 %collective-permute-start.2 = (bf16[16,128,128]{2,1,0:T(8,128)(2,1)S(1)}, bf16[16,128,128]{2,1,0:T(8,128)(2,1)S(1)}, u32[]{:S(2)}, u32[]{:S(2)}) collective-permute-start(bf16[16,128,128]{2,1,0:T(8,128)(2,1)S(1)} %get-tuple-element.41), channel_id=1, source_target_pairs={{0,1},{1,2},{2,3},{3,0},{4,5},{5,6},{6,7},{7,4},{8,9},{9,10},{10,1... | collective-permute-start | bytes 1572872 | tf_op jit(solution)/shard_map/ppermute | solution.py:438
  12.5 14.7 %collective-permute-start.3 = (bf16[16,128,128]{2,1,0:T(8,128)(2,1)S(1)}, bf16[16,128,128]{2,1,0:T(8,128)(2,1)S(1)}, u32[]{:S(2)}, u32[]{:S(2)}) collective-permute-start(bf16[16,128,128]{2,1,0:T(8,128)(2,1)S(1)} %get-tuple-element.43), channel_id=1, source_target_pairs={{0,3},{1,0},{2,1},{3,2},{4,7},{5,4},{6,5},{7,6},{8,11},{9,8},{10,9... | collective-permute-start | bytes 1572872 | tf_op jit(solution)/shard_map/ppermute | solution.py:438
  15.0 15.6 %collective-permute-start = (bf16[16,128,128]{2,1,0:T(8,128)(2,1)S(1)}, bf16[16,128,128]{2,1,0:T(8,128)(2,1)S(1)}, u32[]{:S(2)}, u32[]{:S(2)}) collective-permute-start(bf16[16,128,128]{2,1,0:T(8,128)(2,1)S(1)} %get-tuple-element.37), channel_id=1, source_target_pairs={{0,4},{1,5},{2,6},{3,7},{4,8},{5,9},{6,10},{7,11},{8,12},{9,13},{1... | collective-permute-start | bytes 1572872 | tf_op jit(solution)/shard_map/ppermute | solution.py:438
  22.3 8.7 %copy-start.3 = (s32[128]{0:T(128)S(1)}, s32[128]{0:T(128)}, u32[]{:S(2)}) copy-start(s32[128]{0:T(128)} %param.26) | copy-start | bytes 1540
  22.3 8.7 %copy-start.4 = (s32[128]{0:T(128)S(1)}, s32[128]{0:T(128)}, u32[]{:S(2)}) copy-start(s32[128]{0:T(128)} %param.25) | copy-start | bytes 1540
  22.3 8.7 %copy-start = (f32[16,128,128]{2,1,0:T(8,128)S(1)}, f32[16,128,128]{2,1,0:T(8,128)}, u32[]{:S(2)}) copy-start(f32[16,128,128]{2,1,0:T(8,128)} %diag_ref.3) | copy-start | bytes 3145732
  22.3 8.7 %copy-start.1 = (f32[16,128,128]{2,1,0:T(8,128)S(1)}, f32[16,128,128]{2,1,0:T(8,128)}, u32[]{:S(2)}) copy-start(f32[16,128,128]{2,1,0:T(8,128)} %seed_ref.1) | copy-start | bytes 3145732
  22.4 8.7 %copy-start.2 = (bf16[16,128,128]{2,1,0:T(8,128)(2,1)S(1)}, bf16[16,128,128]{2,1,0:T(8,128)(2,1)}, u32[]{:S(2)}) copy-start(bf16[16,128,128]{2,1,0:T(8,128)(2,1)} %coupling_ref.1) | copy-start | bytes 1572868
  22.7 23.9 %collective-permute-start.5 = (bf16[32,128,128]{2,1,0:T(8,128)(2,1)S(1)}, bf16[32,128,128]{2,1,0:T(8,128)(2,1)S(1)}, u32[]{:S(2)}, u32[]{:S(2)}) collective-permute-start(bf16[32,128,128]{2,1,0:T(8,128)(2,1)S(1)} %fusion.1.refs_1_), channel_id=1, source_target_pairs={{0,12},{1,13},{2,14},{3,15},{4,0},{5,1},{6,2},{7,3},{8,4},{9,5},{1... | collective-permute-start | bytes 3145736 | tf_op jit(solution)/shard_map/ppermute | solution.py:438
  27.1 25.2 %collective-permute-start.6 = (bf16[32,128,128]{2,1,0:T(8,128)(2,1)S(1)}, bf16[32,128,128]{2,1,0:T(8,128)(2,1)S(1)}, u32[]{:S(2)}, u32[]{:S(2)}) collective-permute-start(bf16[32,128,128]{2,1,0:T(8,128)(2,1)S(1)} %fusion.2.refs_2_), channel_id=1, source_target_pairs={{0,1},{1,2},{2,3},{3,0},{4,5},{5,6},{6,7},{7,4},{8,9},{9,10},{10,1... | collective-permute-start | bytes 3145736 | tf_op jit(solution)/shard_map/ppermute | solution.py:438
  27.5 25.3 %collective-permute-start.7 = (bf16[32,128,128]{2,1,0:T(8,128)(2,1)S(1)}, bf16[32,128,128]{2,1,0:T(8,128)(2,1)S(1)}, u32[]{:S(2)}, u32[]{:S(2)}) collective-permute-start(bf16[32,128,128]{2,1,0:T(8,128)(2,1)S(1)} %fusion.3.refs_3_), channel_id=1, source_target_pairs={{0,3},{1,0},{2,1},{3,2},{4,7},{5,4},{6,5},{7,6},{8,11},{9,8},{10,9... | collective-permute-start | bytes 3145736 | tf_op jit(solution)/shard_map/ppermute | solution.py:438
  30.9 24.3 %collective-permute-start.4 = (bf16[32,128,128]{2,1,0:T(8,128)(2,1)S(1)}, bf16[32,128,128]{2,1,0:T(8,128)(2,1)S(1)}, u32[]{:S(2)}, u32[]{:S(2)}) collective-permute-start(bf16[32,128,128]{2,1,0:T(8,128)(2,1)S(1)} %fusion.refs_0_), channel_id=1, source_target_pairs={{0,4},{1,5},{2,6},{3,7},{4,8},{5,9},{6,10},{7,11},{8,12},{9,13},{1... | collective-permute-start | bytes 3145736 | tf_op jit(solution)/shard_map/ppermute | solution.py:438
  38.4 2.9 %collective-permute-start.8 = (bf16[8,128,128]{2,1,0:T(8,128)(2,1)S(1)}, bf16[8,128,128]{2,1,0:T(8,128)(2,1)S(1)}, u32[]{:S(2)}, u32[]{:S(2)}) collective-permute-start(bf16[8,128,128]{2,1,0:T(8,128)(2,1)S(1)} %get-tuple-element.47), channel_id=1, source_target_pairs={{0,16},{16,0},{32,48},{48,32},{64,80},{80,64},{96,112},{112,96},{1... | collective-permute-start | bytes 786440 | tf_op jit(solution)/shard_map/ppermute | solution.py:451
  55.9 6.9 %collective-permute-start.10 = (bf16[8,128,128]{2,1,0:T(8,128)(2,1)S(1)}, bf16[8,128,128]{2,1,0:T(8,128)(2,1)S(1)}, u32[]{:S(2)}, u32[]{:S(2)}) collective-permute-start(bf16[8,128,128]{2,1,0:T(8,128)(2,1)S(1)} %get-tuple-element.51), channel_id=1, source_target_pairs={{0,8},{1,9},{2,10},{3,11},{4,12},{5,13},{6,14},{7,15},{8,0},{9,1},... | collective-permute-start | bytes 786440 | tf_op jit(solution)/shard_map/ppermute | solution.py:438
  56.2 7.8 %collective-permute-start.11 = (bf16[8,128,128]{2,1,0:T(8,128)(2,1)S(1)}, bf16[8,128,128]{2,1,0:T(8,128)(2,1)S(1)}, u32[]{:S(2)}, u32[]{:S(2)}) collective-permute-start(bf16[8,128,128]{2,1,0:T(8,128)(2,1)S(1)} %get-tuple-element.52), channel_id=1, source_target_pairs={{0,2},{1,3},{2,0},{3,1},{4,6},{5,7},{6,4},{7,5},{8,10},{9,11},{10,... | collective-permute-start | bytes 786440 | tf_op jit(solution)/shard_map/ppermute | solution.py:438
  58.1 12.1 %collective-permute-start.12 = (bf16[8,128,128]{2,1,0:T(8,128)(2,1)S(1)}, bf16[8,128,128]{2,1,0:T(8,128)(2,1)S(1)}, u32[]{:S(2)}, u32[]{:S(2)}) collective-permute-start(bf16[8,128,128]{2,1,0:T(8,128)(2,1)S(1)} %get-tuple-element.53), channel_id=1, source_target_pairs={{0,4},{1,5},{2,6},{3,7},{4,8},{5,9},{6,10},{7,11},{8,12},{9,13},{1... | collective-permute-start | bytes 786440 | tf_op jit(solution)/shard_map/ppermute | solution.py:438
  58.1 12.3 %collective-permute-start.13 = (bf16[8,128,128]{2,1,0:T(8,128)(2,1)S(1)}, bf16[8,128,128]{2,1,0:T(8,128)(2,1)S(1)}, u32[]{:S(2)}, u32[]{:S(2)}) collective-permute-start(bf16[8,128,128]{2,1,0:T(8,128)(2,1)S(1)} %get-tuple-element.54), channel_id=1, source_target_pairs={{0,1},{1,2},{2,3},{3,0},{4,5},{5,6},{6,7},{7,4},{8,9},{9,10},{10,1... | collective-permute-start | bytes 786440 | tf_op jit(solution)/shard_map/ppermute | solution.py:438
  58.1 12.3 %collective-permute-start.14 = (bf16[8,128,128]{2,1,0:T(8,128)(2,1)S(1)}, bf16[8,128,128]{2,1,0:T(8,128)(2,1)S(1)}, u32[]{:S(2)}, u32[]{:S(2)}) collective-permute-start(bf16[8,128,128]{2,1,0:T(8,128)(2,1)S(1)} %get-tuple-element.55), channel_id=1, source_target_pairs={{0,12},{1,13},{2,14},{3,15},{4,0},{5,1},{6,2},{7,3},{8,4},{9,5},{1... | collective-permute-start | bytes 786440 | tf_op jit(solution)/shard_map/ppermute | solution.py:438
  62.8 7.7 %collective-permute-start.9 = (bf16[8,128,128]{2,1,0:T(8,128)(2,1)S(1)}, bf16[8,128,128]{2,1,0:T(8,128)(2,1)S(1)}, u32[]{:S(2)}, u32[]{:S(2)}) collective-permute-start(bf16[8,128,128]{2,1,0:T(8,128)(2,1)S(1)} %get-tuple-element.50), channel_id=1, source_target_pairs={{0,3},{1,0},{2,1},{3,2},{4,7},{5,4},{6,5},{7,6},{8,11},{9,8},{10,9... | collective-permute-start | bytes 786440 | tf_op jit(solution)/shard_map/ppermute | solution.py:438
  72.5 6.1 %collective-permute-start.15 = (bf16[8,128,128]{2,1,0:T(8,128)(2,1)S(1)}, bf16[8,128,128]{2,1,0:T(8,128)(2,1)S(1)}, u32[]{:S(2)}, u32[]{:S(2)}) collective-permute-start(bf16[8,128,128]{2,1,0:T(8,128)(2,1)S(1)} %get-tuple-element.59), channel_id=1, source_target_pairs={{0,16},{16,0},{32,48},{48,32},{64,80},{80,64},{96,112},{112,96},{1... | collective-permute-start | bytes 786440 | tf_op jit(solution)/shard_map/ppermute | solution.py:451
  79.0 8.9 %collective-permute-start.16 = (bf16[4,128,128]{2,1,0:T(8,128)(2,1)S(1)}, bf16[4,128,128]{2,1,0:T(8,128)(2,1)S(1)}, u32[]{:S(2)}, u32[]{:S(2)}) collective-permute-start(bf16[4,128,128]{2,1,0:T(8,128)(2,1)S(1)} %get-tuple-element.61), channel_id=1, source_target_pairs={{32,64},{48,80},{64,96},{80,112},{96,0},{112,16},{33,65},{49,81},{... | collective-permute-start | bytes 393224 | tf_op jit(solution)/shard_map/ppermute | solution.py:442
  80.3 11.3 %collective-permute-start.17 = (bf16[4,128,128]{2,1,0:T(8,128)(2,1)S(1)}, bf16[4,128,128]{2,1,0:T(8,128)(2,1)S(1)}, u32[]{:S(2)}, u32[]{:S(2)}) collective-permute-start(bf16[4,128,128]{2,1,0:T(8,128)(2,1)S(1)} %get-tuple-element.62), channel_id=1, source_target_pairs={{32,96},{48,112},{64,0},{80,16},{96,32},{112,48},{33,97},{49,113},... | collective-permute-start | bytes 393224 | tf_op jit(solution)/shard_map/ppermute | solution.py:442
  81.6 11.3 %collective-permute-start.18 = (bf16[4,128,128]{2,1,0:T(8,128)(2,1)S(1)}, bf16[4,128,128]{2,1,0:T(8,128)(2,1)S(1)}, u32[]{:S(2)}, u32[]{:S(2)}) collective-permute-start(bf16[4,128,128]{2,1,0:T(8,128)(2,1)S(1)} %get-tuple-element.63), channel_id=1, source_target_pairs={{32,0},{48,16},{64,32},{80,48},{96,64},{112,80},{33,1},{49,17},{65... | collective-permute-start | bytes 393224 | tf_op jit(solution)/shard_map/ppermute | solution.py:442
  93.4 6.2 %collective-permute-start.19 = (bf16[2,128,128]{2,1,0:T(8,128)(2,1)S(1)}, bf16[2,128,128]{2,1,0:T(8,128)(2,1)S(1)}, u32[]{:S(2)}, u32[]{:S(2)}) collective-permute-start(bf16[2,128,128]{2,1,0:T(8,128)(2,1)S(1)} %get-tuple-element.65), channel_id=1, source_target_pairs={{0,32},{16,48},{32,64},{48,80},{96,0},{112,16},{1,33},{17,49},{33,... | collective-permute-start | bytes 196616 | tf_op jit(solution)/shard_map/ppermute | solution.py:447
  95.5 6.5 %collective-permute-start.20 = (bf16[2,128,128]{2,1,0:T(8,128)(2,1)S(1)}, bf16[2,128,128]{2,1,0:T(8,128)(2,1)S(1)}, u32[]{:S(2)}, u32[]{:S(2)}) collective-permute-start(bf16[2,128,128]{2,1,0:T(8,128)(2,1)S(1)} %get-tuple-element.66), channel_id=1, source_target_pairs={{0,64},{16,80},{64,0},{80,16},{96,32},{112,48},{1,65},{17,81},{65,... | collective-permute-start | bytes 196616 | tf_op jit(solution)/shard_map/ppermute | solution.py:447
  97.5 5.0 %collective-permute-start.21 = (bf16[2,128,128]{2,1,0:T(8,128)(2,1)S(1)}, bf16[2,128,128]{2,1,0:T(8,128)(2,1)S(1)}, u32[]{:S(2)}, u32[]{:S(2)}) collective-permute-start(bf16[2,128,128]{2,1,0:T(8,128)(2,1)S(1)} %get-tuple-element.67), channel_id=1, source_target_pairs={{32,0},{48,16},{64,32},{80,48},{96,64},{112,80},{33,1},{49,17},{65... | collective-permute-start | bytes 196616 | tf_op jit(solution)/shard_map/ppermute | solution.py:447
  103.4 4.2 %collective-permute-start.22 = (bf16[8,128,128]{2,1,0:T(8,128)(2,1)S(1)}, bf16[8,128,128]{2,1,0:T(8,128)(2,1)S(1)}, u32[]{:S(2)}, u32[]{:S(2)}) collective-permute-start(bf16[8,128,128]{2,1,0:T(8,128)(2,1)S(1)} %get-tuple-element.69), channel_id=1, source_target_pairs={{0,16},{16,0},{32,48},{48,32},{64,80},{80,64},{96,112},{112,96},{1... | collective-permute-start | bytes 786440 | tf_op jit(solution)/shard_map/ppermute | solution.py:451

commit v5 on v4

--- a/solution.py
+++ b/solution.py
@@ -12,7 +12,6 @@
 UNROLL = 16
 CHUNKS = 8
 CELL_MASK, PIVOT_BIT, FAR_BIT, NEAR_BIT, SLOT_BIT = 511, 9, 16, 17, 20
-SECOND = ((0, 3), (1, 2), (0, 2), (1, 1), (0, 1), (1, 3))
 MIB = 1 << 20
 
 ANY = pl.BlockSpec(memory_space=pl.ANY)
@@ -56,14 +55,9 @@
     return pairs
 
 
-def cross_kernel(first, sizes, flag, unroll, index_ref, table_ref, left_ref, right_ref, *refs):
-    outs = refs[-8 - len(sizes) : -8]
-    listed, left, right, total, table, lsem, rsem, tsem = refs[-8:]
-    cells = sum(sizes)
+def sum_cells(first, flag, index_ref, listed, total, outs, ready, left, right, table):
     slots = left.shape[0]
-    table_copy = pltpu.make_async_copy(table_ref, table, tsem)
-    table_copy.start()
-    bulk(left_ref, right_ref, left, right, lsem, rsem)
+    cells = total.shape[0] - 1
 
     def note(i, n):
         word = index_ref[i]
@@ -71,7 +65,7 @@
         return n + ((word >> flag) & 1)
 
     count = lax.fori_loop(0, slots, note, 0, unroll=32)
-    for u in range(unroll):
+    for u in range(UNROLL):
         listed[count + u] = first + cells
 
     def clear(c, _):
@@ -79,64 +73,93 @@
         return 0
 
     lax.fori_loop(0, cells + 1, clear, 0, unroll=8)
-    table_copy.wait()
-    per = slots // CHUNKS
-
-    def landed(k, _):
-        part = pl.ds(k * per, per)
-        pltpu.make_async_copy(left_ref.at[part], left.at[part], lsem.at[k]).wait()
-        pltpu.make_async_copy(right_ref.at[part], right.at[part], rsem.at[k]).wait()
-        return 0
-
-    def work(r, ready):
-        words = [listed[r * unroll + u] for u in range(unroll)]
-        last = listed[jnp.minimum(r * unroll + unroll, count) - 1] >> SLOT_BIT
-        lax.fori_loop(ready, last // per + 1, landed, 0)
+    ready()
+
+    def work(r, _):
+        words = [listed[r * UNROLL + u] for u in range(UNROLL)]
         scaled = [mm(left[w >> SLOT_BIT], table[(w >> PIVOT_BIT) & 3]).astype(bf16) for w in words]
         updates = [mm(x, right[w >> SLOT_BIT]) for x, w in zip(scaled, words)]
         for w, u in zip(words, updates):
             c = (w & CELL_MASK) - first
             total[c] = (total[c].astype(f32) + u).astype(bf16)
-        return last // per + 1
-
-    ready = lax.fori_loop(0, (count + unroll - 1) // unroll, work, 0)
-    lax.fori_loop(ready, CHUNKS, landed, 0)
-
+        return 0
+
+    lax.fori_loop(0, (count + UNROLL - 1) // UNROLL, work, 0)
     start = 0
-    for out, size in zip(outs, sizes):
+    for out in outs:
 
         def give(c, _, out=out, start=start):
             out[c] = total[start + c]
             return 0
 
-        lax.fori_loop(0, size, give, 0, unroll=8)
-        start += size
-
-
-def cross_sums(first, sizes, flag, unroll, index, table, left, right, live):
+        lax.fori_loop(0, out.shape[0], give, 0, unroll=8)
+        start += out.shape[0]
+
+
+def far_kernel(first, index_ref, table_ref, left_ref, right_ref, *refs):
+    *outs, left, right, table, listed, total, lsem, rsem, tsem = refs
+    table_copy = pltpu.make_async_copy(table_ref, table, tsem)
+    table_copy.start()
+    pairs = bulk(left_ref, right_ref, left, right, lsem, rsem)
+
+    def ready():
+        table_copy.wait()
+        for pair in pairs:
+            for c in pair:
+                c.wait()
+
+    sum_cells(first, FAR_BIT, index_ref, listed, total, outs, ready, left, right, table)
+
+
+def near_kernel(first, index_ref, table, left, right, *refs):
+    *outs, listed, total = refs
+    sum_cells(first, NEAR_BIT, index_ref, listed, total, outs, lambda: None, left, right, table)
+
+
+def cell_shapes(sizes):
+    return [jax.ShapeDtypeStruct((n, B, B), bf16) for n in sizes]
+
+
+def far_sums(first, sizes, index, table, left, right):
     cells = sum(sizes)
     slots = left.shape[0]
-    return pl.pallas_call(
-        functools.partial(cross_kernel, first, sizes, flag, unroll),
-        out_shape=[jax.ShapeDtypeStruct((n, B, B), bf16) for n in sizes],
+    outs = pl.pallas_call(
+        functools.partial(far_kernel, first),
+        out_shape=cell_shapes(sizes) + [jax.ShapeDtypeStruct(x.shape, bf16) for x in (left, right, table)],
         in_specs=[SMEM, HBM, HBM, HBM],
-        out_specs=[VMEM] * len(sizes),
+        out_specs=[VMEM] * (len(sizes) + 3),
         scratch_shapes=[
-            pltpu.SMEM((slots + unroll,), jnp.int32),
-            pltpu.VMEM((slots, B, B), bf16),
-            pltpu.VMEM((slots, B, B), bf16),
+            pltpu.SMEM((slots + UNROLL,), jnp.int32),
             pltpu.VMEM((cells + 1, B, B), bf16),
-            pltpu.VMEM(table.shape, bf16),
             pltpu.SemaphoreType.DMA((CHUNKS,)),
             pltpu.SemaphoreType.DMA((CHUNKS,)),
             pltpu.SemaphoreType.DMA,
         ],
         compiler_params=pltpu.CompilerParams(vmem_limit_bytes=9 * MIB + cells * 4 * B * B),
         cost_estimate=pl.CostEstimate(
-            flops=live * 4 * B**3, bytes_accessed=slots * 4 * B * B + cells * 2 * B * B, transcendentals=0
+            flops=slots * B**3, bytes_accessed=slots * 8 * B * B + cells * 2 * B * B, transcendentals=0
         ),
-        name="cross_sums",
+        name="far_sums",
     )(index, stay(table), stay(left), stay(right))
+    return outs[: len(sizes)], outs[len(sizes) :]
+
+
+def near_sums(first, sizes, index, held):
+    left, right, table = held
+    cells = sum(sizes)
+    slots = left.shape[0]
+    return pl.pallas_call(
+        functools.partial(near_kernel, first),
+        out_shape=cell_shapes(sizes),
+        in_specs=[SMEM, VMEM, VMEM, VMEM],
+        out_specs=[VMEM] * len(sizes),
+        scratch_shapes=[pltpu.SMEM((slots + UNROLL,), jnp.int32), pltpu.VMEM((cells + 1, B, B), bf16)],
+        compiler_params=pltpu.CompilerParams(vmem_limit_bytes=9 * MIB + cells * 4 * B * B),
+        cost_estimate=pl.CostEstimate(
+            flops=slots * 3 * B**3, bytes_accessed=slots * 4 * B * B + cells * 2 * B * B, transcendentals=0
+        ),
+        name="near_sums",
+    )(index, table, left, right)
 
 
 def local_kernel(index_ref, table_ref, coupling_ref, left_ref, right_ref, diag_ref, seed_ref, *refs):
@@ -206,31 +229,29 @@
     )(index, stay(table), coupling, stay(left), stay(right), diag, seed, *order)
 
 
-def first_totals_kernel(own_x, own_z, *refs):
-    outs = refs[-2 * SIDE :]
-    q = own_x.shape[0] // (2 * SIDE)
-    for s, own in enumerate((own_x, own_z)):
-        plus, minus = refs[2 * s : 2 * s + 2]
-        for half in range(2):
-            for b in range(SIDE):
-                t = own[pl.ds((half * SIDE + b) * q, q)].astype(f32)
-                t = t + plus[pl.ds(((1 - half) * SIDE + b) * q, q)].astype(f32)
-                t = t + minus[pl.ds((half * SIDE + b) * q, q)].astype(f32)
-                outs[s * SIDE + b][pl.ds(half * q, q)] = t.astype(bf16)
-
-
-def first_totals(own_x, own_z, arrivals, order):
-    half = own_x.shape[0] // SIDE
-    outs = pl.pallas_call(
+def first_totals_kernel(own, *refs):
+    arrivals = (refs[:2], refs[2:4])
+    outs = refs[-SIDE:]
+    h = own.shape[0] // (2 * SIDE)
+    for half in range(2):
+        for b in range(SIDE):
+            t = own[pl.ds((half * SIDE + b) * h, h)].astype(f32)
+            for a in arrivals[half]:
+                t = t + a[pl.ds(b * h, h)].astype(f32)
+            outs[b][pl.ds(half * h, h)] = t.astype(bf16)
+
+
+def first_totals(own, arrivals, order):
+    rows = own.shape[0] // SIDE
+    return pl.pallas_call(
         first_totals_kernel,
-        out_shape=[jax.ShapeDtypeStruct((half, B, B), bf16)] * (2 * SIDE),
-        in_specs=[VMEM] * 6 + [ANY] * len(order),
-        out_specs=[VMEM] * (2 * SIDE),
+        out_shape=[jax.ShapeDtypeStruct((rows, B, B), bf16)] * SIDE,
+        in_specs=[VMEM] * 5 + [ANY] * len(order),
+        out_specs=[VMEM] * SIDE,
         compiler_params=pltpu.CompilerParams(vmem_limit_bytes=9 * MIB),
         cost_estimate=pl.CostEstimate(flops=0, bytes_accessed=256 * 2 * B * B, transcendentals=0),
         name="first_totals",
-    )(own_x, own_z, *arrivals, *order)
-    return outs[:SIDE], outs[SIDE:]
+    )(own, *arrivals, *order)
 
 
 def coupling_kernel(base_ref, diag_ref, *refs):
@@ -238,27 +259,25 @@
     rows = base_ref.shape[0]
     half = rows // 2
     core = lax.axis_index("section") % 2
-    for s in range(2):
-        parts = [refs[s]] + [refs[2 + i] for i, (t, _) in enumerate(SECOND) if t == s]
-
-        def finish(i, _, s=s, parts=parts):
-            r = s * half + i
-            t = base_ref[r]
-            for p in parts:
-                t = t - p[i].astype(f32)
-            new_ref[r] = t
-            th, tl = split(t)
-            dh, dl = split(diag_ref[r])
-            held[(r + core * half) % rows] = -(mm(dh, th) + (mm(dh, tl) + mm(dl, th))).astype(bf16)
-            return 0
-
-        lax.fori_loop(0, half, finish, 0, unroll=4)
+    parts = refs[:SIDE]
+
+    def finish(r, _):
+        t = base_ref[r]
+        for p in parts:
+            t = t - p[r].astype(f32)
+        new_ref[r] = t
+        th, tl = split(t)
+        dh, dl = split(diag_ref[r])
+        held[(r + core * half) % rows] = -(mm(dh, th) + (mm(dh, tl) + mm(dl, th))).astype(bf16)
+        return 0
+
+    lax.fori_loop(0, rows, finish, 0, unroll=4)
     for i in range(half):
         keep_ref[i] = held[i]
         give_ref[i] = held[half + i]
 
 
-def coupling_and_step(base, diag, own, parts):
+def coupling_and_step(base, diag, parts):
     rows = base.shape[0]
     half = rows // 2
     return pl.pallas_call(
@@ -268,13 +287,13 @@
             jax.ShapeDtypeStruct((half, B, B), bf16),
             jax.ShapeDtypeStruct((half, B, B), bf16),
         ],
-        in_specs=[VMEM] * 10,
+        in_specs=[VMEM] * (2 + SIDE),
         out_specs=[VMEM] * 3,
         scratch_shapes=[pltpu.VMEM((rows, B, B), bf16)],
         compiler_params=pltpu.CompilerParams(vmem_limit_bytes=9 * MIB),
         cost_estimate=pl.CostEstimate(flops=rows * 6 * B**3, bytes_accessed=rows * 22 * B * B, transcendentals=0),
         name="coupling_and_step",
-    )(base, diag, *own, *parts)
+    )(base, diag, *parts)
 
 
 def compose_kernel(chips, keep_ref, offset_ref, got_ref, got_offset_ref, *outs):
@@ -427,24 +446,21 @@
     )(mine, got)
 
 
-def moved(x, along, by):
+def moved(x, stage, by, sections):
     pairs = []
-    for a in range(SIDE):
-        for c in range(SIDE):
-            if along == 0:
-                pairs.append((a * SIDE + c, (a + by) % SIDE * SIDE + c))
-            else:
-                pairs.append((a * SIDE + c, a * SIDE + (c + by) % SIDE))
-    return lax.ppermute(x, "row", pairs)
-
-
-def maps_across(x, sections, by):
-    return lax.ppermute(x, "section", [(i, (i + 2 * by) % sections) for i in range(2, sections)])
-
-
-def incoming_across(x, sections, by):
-    pairs = [(i, (i + 2 * by) % sections) for i in range(sections)]
-    return lax.ppermute(x, "section", [p for p in pairs if p[1] < sections - 2])
+    for s in range(sections):
+        for a in range(SIDE):
+            for c in range(SIDE):
+                if (s + stage) % 2 == 0:
+                    to = (a + by) % SIDE * SIDE + c
+                else:
+                    to = a * SIDE + (c + by) % SIDE
+                pairs.append((s * SIDE * SIDE + a * SIDE + c, s * SIDE * SIDE + to))
+    return lax.ppermute(x, ("section", "row"), pairs)
+
+
+def across(x, sections, by):
+    return lax.ppermute(x, "section", [(i, (i + 2 * by) % sections) for i in range(sections)])
 
 
 def partner(x, sections):
@@ -475,29 +491,23 @@
     rows = coupling.shape[0]
     slots = cross_left.shape[0]
     half = rows // 2
-    quarter = rows // 4
     me = lax.axis_index("row")
+    odd = lax.axis_index("section") % 2
 
     owner = cross_owner[:, 0]
     dx = (owner // SIDE - me // SIDE) % SIDE
     dz = (owner % SIDE - me % SIDE) % SIDE
-    second = foreign_target_row // half
-    row = foreign_target_row % half
-    a = jnp.where(second == 0, dx, dz)
-    b = jnp.where(second == 0, dz, dx)
-    upper = row // quarter
-    spot = b * quarter + row % quarter
-    n = SIDE * quarter
-    group = 4 * n
+    a = jnp.where(odd == 0, dx, dz)
+    b = jnp.where(odd == 0, dz, dx)
+    upper = foreign_target_row // half
+    spot = b * half + foreign_target_row % half
+    n = SIDE * half
+    group = 2 * n
     minus = (a == 3).astype(jnp.int32)
-    cell = jnp.where(
+    cell = spot + jnp.where(
         a == 2,
-        second * 2 * n + upper * n + spot,
-        jnp.where(
-            a == 0,
-            3 * group + second * 2 * n + upper * n + spot,
-            group + (second * 2 + minus) * 2 * n + jnp.where(minus == upper, n, 0) + spot,
-        ),
+        upper * n,
+        jnp.where(a == 0, 3 * group + upper * n, jnp.where(minus == upper, 2 * group, group) + minus * n),
     )
     slot = jnp.arange(slots, dtype=jnp.int32)
     live = slot < cross_count[0]
@@ -505,29 +515,28 @@
     word = word | jnp.where(live, jnp.where(cell < group, 1 << FAR_BIT, 1 << NEAR_BIT), 0)
     local_word = local_target | (local_pivot << PIVOT_BIT)
 
-    sums = functools.partial(cross_sums, index=word, table=pivot_inverse, left=cross_left, right=cross_right)
-    far = sums(0, [n] * 4, FAR_BIT, 8, live=slots // 4)
-    ways = ((0, 1), (0, -1), (1, 1), (1, -1))
-    far_in = [moved(x, *w) for x, w in zip(far, ways)]
-    near = sums(group, [2 * n] * 6, NEAR_BIT, UNROLL, live=slots * 3 // 4)
-    joined = [lax.dynamic_update_slice_in_dim(x, add(x[n:], y), n, 0) for x, y in zip(near, far_in)]
-    arrivals = [moved(x, *w) for x, w in zip(joined, ways)]
+    far, on_chip = far_sums(0, [n] * 2, word, pivot_inverse, cross_left, cross_right)
+    far_in = [moved(x, 0, w, sections) for x, w in zip(far, (1, -1))]
+    near = near_sums(group, [n] * 4 + [2 * n], word, on_chip)
+    alone_in = [moved(x, 0, w, sections) for x, w in zip(near[:2], (1, -1))]
+    joined = [add(x, y) for x, y in zip(near[2:4], far_in)]
+    joined_in = [moved(x, 0, w, sections) for x, w in zip(joined, (1, -1))]
 
     base, offsets, give_offsets = local_and_offset(
         local_word, pivot_inverse, coupling, local_left, local_right, diag_inverse, adjoint_seed, joined
     )
     got_offsets = partner(give_offsets, sections)
 
-    tot_x, tot_z = first_totals(near[4], near[5], arrivals, [base, got_offsets])
-    totals = (tot_x, tot_z)
-    parts = [moved(totals[s][k], 1 - s, k) for s, k in SECOND]
-    updated, keep, give = coupling_and_step(base, diag_inverse, (tot_x[0], tot_z[0]), parts)
+    arrivals = (joined_in[0], alone_in[1], alone_in[0], joined_in[1])
+    totals = first_totals(near[4], arrivals, [base, got_offsets])
+    parts = [totals[0]] + [moved(totals[k], 1, k, sections) for k in (2, 1, 3)]
+    updated, keep, give = coupling_and_step(base, diag_inverse, parts)
     chips = sections // 2
     got = partner(give, sections)
     maps = compose(chips, keep, offsets, got, got_offsets)
-    maps = [maps[0]] + [maps_across(maps[k], sections, k) for k in range(1, chips)]
+    maps = [maps[0]] + [across(maps[k], sections, k) for k in range(1, chips)]
     incoming = run_chains(maps)
-    incoming = [incoming[0]] + [incoming_across(incoming[k], sections, k) for k in range(1, chips)]
+    incoming = [incoming[0]] + [across(incoming[k], sections, k) for k in range(1, chips)]
     mine, other = expand(keep, offsets, got, got_offsets, incoming)
     adjoint = gather_rows(mine, partner(other, sections))
     return (updated, adjoint)

time: 110 us -> 97.5 us (0.89); the launches traced: 109 us -> 99.4 us
  starting transfers between devices: 38.8 us -> 31.3 us
  Pallas kernels: 25.7 us -> 22.2 us
  waiting for transfers between devices: 40.7 us -> 42.5 us
    ppermute x20 -> x15, starting transfers between devices: 29.1 us -> 21.5 us  [the longest x9 14.8 us: moved(): return lax.ppermute(x, ('section', 'row'), pairs)]
    pallas_call x3, Pallas kernels: 13.5 us -> 10 us  [the longest x1 5.22 us: far_sums(): pl.pallas_call(functools.partial(far_kernel, first), out_shape=cell_shape...]
    ppermute x20 -> x15, waiting for transfers between devices: 37.2 us -> 40.2 us  [the longest x9 29.8 us: moved(): return lax.ppermute(x, ('section', 'row'), pairs)]
    dynamic_update_slice x4 -> x0, other arithmetic: 1.17 us -> none  [per_device(): lax.dynamic_update_slice_in_dim(x, add(x[n:], y), n, 0)]
    ppermute x3, waiting for transfers between devices: 3.49 us -> 2.33 us  [partner(): return lax.ppermute(x, 'section', [(i, i ^ 1) for i in range(sections)])]
  transfers between devices with their start and end apart: 23 -> 18, of which waited for: 17 -> 14; matrix products, arithmetic and copies ran while one was open for 1% -> 1% of each run, Pallas kernels for 13% -> 12%
where the time goes in v5:
time: 97.5 us; the launch traced here: 99.4 us
  waiting for transfers between devices  42.5 us (44%)
  starting transfers between devices  31.3 us (32%)
  Pallas kernels  22.2 us (23%)
  between operations  1.65 us (2%)
  other arithmetic  1.63 us (2%)
    ppermute x9, waiting for transfers between devices, moved(): return lax.ppermute(x, ('section', 'row'), pairs)  29.8 us
    ppermute x9, starting transfers between devices, moved(): return lax.ppermute(x, ('section', 'row'), pairs)  14.8 us
    ppermute x6, waiting for transfers between devices, across(): lax.ppermute(x, 'section', [(i, (i + 2 * by) % sections) for i in range(s...  10.4 us
    ppermute x3, starting transfers between devices, partner(): return lax.ppermute(x, 'section', [(i, i ^ 1) for i in range(sections)])  9.85 us
    pallas_call x1, Pallas kernels, local_and_offset(): pl.pallas_call(local_kernel, out_shape=[jax.ShapeDtypeStruct((rows, B, B)...  7.4 us
    ppermute x6, starting transfers between devices, across(): lax.ppermute(x, 'section', [(i, (i + 2 * by) % sections) for i in range(s...  6.73 us
    pallas_call x1, Pallas kernels, far_sums(): pl.pallas_call(functools.partial(far_kernel, first), out_shape=cell_shape...  5.22 us
    pallas_call x1, Pallas kernels, near_sums(): pl.pallas_call(functools.partial(near_kernel, first), out_shape=cell_shap...  4.04 us
  transfers between devices with their start and end apart: 18, of which 14 were waited for; matrix products, arithmetic and copies ran while one was open for 1% of the time, Pallas kernels for 12%

profile of v5, /device:TPU:1, one launch (start us, length us, event | category | flops | bytes accessed | tf_op | source)
XLA Modules:
  0.0 99.4 jit_solution(4708806281869209016)
XLA Ops:
  1.3 0.7 fusion.5.index_ref
  2.0 5.2 %far_sums.1 = (bf16[32,128,128]{2,1,0:T(8,128)(2,1)S(1)}, bf16[32,128,128]{2,1,0:T(8,128)(2,1)S(1)}, bf16[128,128,128]{2,1,0:T(8,128)(2,1)S(1)}, bf16[128,128,12...) custom-call(s32[128]{0:T(128)S(1)} %fusion.5.index_ref, bf16[4,128,128]{2,1,0:T(8,128)(2,1)} %table_ref.3, ...), custom_call_target="tpu_custom_call" | custom-call | flops 268435456 | bytes 18874368 | tf_op jit(solution)/shard_map/far_sums/pallas_call | solution.py:126
  7.2 4.2 %collective-permute-start.1 = (bf16[32,128,128]{2,1,0:T(8,128)(2,1)S(1)}, bf16[32,128,128]{2,1,0:T(8,128)(2,1)S(1)}, u32[]{:S(2)}, u32[]{:S(2)}) collective-permute-start(bf16[32,128,128]{2,1,0:T(8,128)(2,1)S(1)} %get-tuple-element.38), channel_id=1, source_target_pairs={{0,12},{1,13},{2,14},{3,15},{4,0},{5,1},{6,2},{7,3},{8,4},{9,5},{1... | collective-permute-start | bytes 3145736 | tf_op jit(solution)/shard_map/ppermute | solution.py:459
  11.4 4.0 %near_sums.1 = (bf16[32,128,128]{2,1,0:T(8,128)(2,1)S(1)}, bf16[32,128,128]{2,1,0:T(8,128)(2,1)S(1)}, bf16[32,128,128]{2,1,0:T(8,128)(2,1)S(1)}, bf16[32,128,128...) custom-call(s32[128]{0:T(128)S(1)} %fusion.5.index_ref, bf16[4,128,128]{2,1,0:T(8,128)(2,1)S(1)} %get-tuple-element.32.table, ...), custom_call_target="tpu_custom_call" | custom-call | flops 805306368 | bytes 14680064 | tf_op jit(solution)/shard_map/near_sums/pallas_call | solution.py:151
  15.5 1.8 %collective-permute-start.3 = (bf16[32,128,128]{2,1,0:T(8,128)(2,1)S(1)}, bf16[32,128,128]{2,1,0:T(8,128)(2,1)S(1)}, u32[]{:S(2)}, u32[]{:S(2)}) collective-permute-start(bf16[32,128,128]{2,1,0:T(8,128)(2,1)S(1)} %get-tuple-element.41), channel_id=1, source_target_pairs={{0,12},{1,13},{2,14},{3,15},{4,0},{5,1},{6,2},{7,3},{8,4},{9,5},{1... | collective-permute-start | bytes 3145736 | tf_op jit(solution)/shard_map/ppermute | solution.py:459
  17.3 5.9 %collective-permute-done.1 = bf16[32,128,128]{2,1,0:T(8,128)(2,1)S(1)} collective-permute-done((bf16[32,128,128]{2,1,0:T(8,128)(2,1)S(1)}, bf16[32,128,128]{2,1,0:T(8,128)(2,1)S(1)}, u32[]{:S(2)}, u32[]{:S(2)}) %collective-permute-start.1) | collective-permute-done | bytes 1048608 | tf_op jit(solution)/shard_map/ppermute | solution.py:459
  23.2 0.5 add_convert_fusion.refs_1_
  23.6 0.0 copy-start.3
  23.7 0.0 copy-start.4
  23.7 0.0 copy-start
  23.7 0.0 copy-start.1
  23.7 0.0 copy-start.2
  23.7 3.5 %collective-permute-start.5 = (bf16[32,128,128]{2,1,0:T(8,128)(2,1)S(1)}, bf16[32,128,128]{2,1,0:T(8,128)(2,1)S(1)}, u32[]{:S(2)}, u32[]{:S(2)}) collective-permute-start(bf16[32,128,128]{2,1,0:T(8,128)(2,1)S(1)} %add_convert_fusion.refs_1_), channel_id=1, source_target_pairs={{0,12},{1,13},{2,14},{3,15},{4,0},{5,1},{6,2},{7,3},{8,4},{9,5},{1... | collective-permute-start | bytes 3145736 | tf_op jit(solution)/shard_map/ppermute | solution.py:459
  27.2 0.0 collective-permute-done
  27.2 0.5 add_convert_fusion.1.refs_0_
  27.6 0.1 collective-permute-start.2
  27.8 7.4 %local_and_offset.1 = (f32[16,128,128]{2,1,0:T(8,128)S(1)}, bf16[8,128,128]{2,1,0:T(8,128)(2,1)S(1)}, bf16[8,128,128]{2,1,0:T(8,128)(2,1)S(1)}) custom-call(s32[128]{0:T(128)S(1)} %shift-left_or_fusion.index_ref, bf16[4,128,128]{2,1,0:T(8,128)(2,1)} %table_ref.3, bf16[16,128,128]{2,1,0:T(8,128)(2,1)S(1)} %copy-done.2, bf16[128,128,128]{2,1,0:T(8,128)(2,1)} %left_ref.3, ...), custom_call_target="tpu_custom_call" | custom-call | flops 1073741824 | bytes 12582912 | tf_op jit(solution)/shard_map/local_and_offset/pallas_call | solution.py:210
  35.2 1.1 %collective-permute-start.6 = (bf16[8,128,128]{2,1,0:T(8,128)(2,1)S(1)}, bf16[8,128,128]{2,1,0:T(8,128)(2,1)S(1)}, u32[]{:S(2)}, u32[]{:S(2)}) collective-permute-start(bf16[8,128,128]{2,1,0:T(8,128)(2,1)S(1)} %get-tuple-element.43), channel_id=1, source_target_pairs={{0,16},{16,0},{32,48},{48,32},{64,80},{80,64},{96,112},{112,96},{1... | collective-permute-start | bytes 786440 | tf_op jit(solution)/shard_map/ppermute | solution.py:467
  36.3 1.6 %collective-permute-done.4.refs_2_ = bf16[32,128,128]{2,1,0:T(8,128)(2,1)S(1)} collective-permute-done((bf16[32,128,128]{2,1,0:T(8,128)(2,1)S(1)}, bf16[32,128,128]{2,1,0:T(8,128)(2,1)S(1)}, u32[]{:S(2)}, u32[]{:S(2)}) %collective-permute-start.4) | collective-permute-done | bytes 1048608 | tf_op jit(solution)/shard_map/ppermute | solution.py:459
  37.8 7.8 %collective-permute-done.5.refs_3_ = bf16[32,128,128]{2,1,0:T(8,128)(2,1)S(1)} collective-permute-done((bf16[32,128,128]{2,1,0:T(8,128)(2,1)S(1)}, bf16[32,128,128]{2,1,0:T(8,128)(2,1)S(1)}, u32[]{:S(2)}, u32[]{:S(2)}) %collective-permute-start.5) | collective-permute-done | bytes 1048608 | tf_op jit(solution)/shard_map/ppermute | solution.py:459
  45.6 3.4 %collective-permute-done.2.refs_0_ = bf16[32,128,128]{2,1,0:T(8,128)(2,1)S(1)} collective-permute-done((bf16[32,128,128]{2,1,0:T(8,128)(2,1)S(1)}, bf16[32,128,128]{2,1,0:T(8,128)(2,1)S(1)}, u32[]{:S(2)}, u32[]{:S(2)}) %collective-permute-start.2) | collective-permute-done | bytes 1048608 | tf_op jit(solution)/shard_map/ppermute | solution.py:459
  49.1 0.7 first_totals.1
  49.8 2.5 %collective-permute-start.7 = (bf16[16,128,128]{2,1,0:T(8,128)(2,1)S(1)}, bf16[16,128,128]{2,1,0:T(8,128)(2,1)S(1)}, u32[]{:S(2)}, u32[]{:S(2)}) collective-permute-start(bf16[16,128,128]{2,1,0:T(8,128)(2,1)S(1)} %get-tuple-element.45), channel_id=1, source_target_pairs={{0,2},{1,3},{2,0},{3,1},{4,6},{5,7},{6,4},{7,5},{8,10},{9,11},{10,... | collective-permute-start | bytes 1572872 | tf_op jit(solution)/shard_map/ppermute | solution.py:459
  52.3 1.3 %collective-permute-start.8 = (bf16[16,128,128]{2,1,0:T(8,128)(2,1)S(1)}, bf16[16,128,128]{2,1,0:T(8,128)(2,1)S(1)}, u32[]{:S(2)}, u32[]{:S(2)}) collective-permute-start(bf16[16,128,128]{2,1,0:T(8,128)(2,1)S(1)} %get-tuple-element.46), channel_id=1, source_target_pairs={{0,1},{1,2},{2,3},{3,0},{4,5},{5,6},{6,7},{7,4},{8,9},{9,10},{10,1... | collective-permute-start | bytes 1572872 | tf_op jit(solution)/shard_map/ppermute | solution.py:459
  53.6 1.4 %collective-permute-start.9 = (bf16[16,128,128]{2,1,0:T(8,128)(2,1)S(1)}, bf16[16,128,128]{2,1,0:T(8,128)(2,1)S(1)}, u32[]{:S(2)}, u32[]{:S(2)}) collective-permute-start(bf16[16,128,128]{2,1,0:T(8,128)(2,1)S(1)} %get-tuple-element.47), channel_id=1, source_target_pairs={{0,3},{1,0},{2,1},{3,2},{4,7},{5,4},{6,5},{7,6},{8,11},{9,8},{10,9... | collective-permute-start | bytes 1572872 | tf_op jit(solution)/shard_map/ppermute | solution.py:459
  55.0 4.5 %collective-permute-done.7.refs_1_ = bf16[16,128,128]{2,1,0:T(8,128)(2,1)S(1)} collective-permute-done((bf16[16,128,128]{2,1,0:T(8,128)(2,1)S(1)}, bf16[16,128,128]{2,1,0:T(8,128)(2,1)S(1)}, u32[]{:S(2)}, u32[]{:S(2)}) %collective-permute-start.7) | collective-permute-done | bytes 524320 | tf_op jit(solution)/shard_map/ppermute | solution.py:459
  59.5 5.8 %collective-permute-done.8.refs_2_ = bf16[16,128,128]{2,1,0:T(8,128)(2,1)S(1)} collective-permute-done((bf16[16,128,128]{2,1,0:T(8,128)(2,1)S(1)}, bf16[16,128,128]{2,1,0:T(8,128)(2,1)S(1)}, u32[]{:S(2)}, u32[]{:S(2)}) %collective-permute-start.8) | collective-permute-done | bytes 524320 | tf_op jit(solution)/shard_map/ppermute | solution.py:459
  65.3 0.8 collective-permute-done.9.refs_3_
  66.1 2.0 %coupling_and_step.1 = (f32[16,128,128]{2,1,0:T(8,128)}, bf16[8,128,128]{2,1,0:T(8,128)(2,1)S(1)}, bf16[8,128,128]{2,1,0:T(8,128)(2,1)S(1)}) custom-call(f32[16,128,128]{2,1,0:T(8,128)S(1)} %get-tuple-element.39.refs_4_.base_ref, f32[16,128,128]{2,1,0:T(8,128)S(1)} %copy-done, bf16[16,128,128]{2,1,0:T(8,128)(2,1)S(1)} %get-tuple-element.44.refs_0_, ...), custom_call_target="tpu_custom_call" | custom-call | flops 201326592 | bytes 5767168 | tf_op jit(solution)/shard_map/coupling_and_step/pallas_call | solution.py:283
  68.1 7.1 %collective-permute-start.10 = (bf16[8,128,128]{2,1,0:T(8,128)(2,1)S(1)}, bf16[8,128,128]{2,1,0:T(8,128)(2,1)S(1)}, u32[]{:S(2)}, u32[]{:S(2)}) collective-permute-start(bf16[8,128,128]{2,1,0:T(8,128)(2,1)S(1)} %get-tuple-element.51), channel_id=1, source_target_pairs={{0,16},{16,0},{32,48},{48,32},{64,80},{80,64},{96,112},{112,96},{1... | collective-permute-start | bytes 786440 | tf_op jit(solution)/shard_map/ppermute | solution.py:467
  75.2 1.2 %collective-permute-done.10.got_ref = bf16[8,128,128]{2,1,0:T(8,128)(2,1)S(1)} collective-permute-done((bf16[8,128,128]{2,1,0:T(8,128)(2,1)S(1)}, bf16[8,128,128]{2,1,0:T(8,128)(2,1)S(1)}, u32[]{:S(2)}, u32[]{:S(2)}) %collective-permute-start.10) | collective-permute-done | bytes 262176 | tf_op jit(solution)/shard_map/ppermute | solution.py:467
  76.4 0.4 compose.1
  76.8 0.1 collective-permute-start.11
  76.9 0.3 collective-permute-start.12
  77.1 2.4 %collective-permute-start.13 = (bf16[4,128,128]{2,1,0:T(8,128)(2,1)S(1)}, bf16[4,128,128]{2,1,0:T(8,128)(2,1)S(1)}, u32[]{:S(2)}, u32[]{:S(2)}) collective-permute-start(bf16[4,128,128]{2,1,0:T(8,128)(2,1)S(1)} %get-tuple-element.55), channel_id=1, source_target_pairs={{0,96},{16,112},{32,0},{48,16},{64,32},{80,48},{96,64},{112,80},{1... | collective-permute-start | bytes 393224 | tf_op jit(solution)/shard_map/ppermute | solution.py:463
  79.5 6.2 %collective-permute-done.11.refs_1_ = bf16[4,128,128]{2,1,0:T(8,128)(2,1)S(1)} collective-permute-done((bf16[4,128,128]{2,1,0:T(8,128)(2,1)S(1)}, bf16[4,128,128]{2,1,0:T(8,128)(2,1)S(1)}, u32[]{:S(2)}, u32[]{:S(2)}) %collective-permute-start.11) | collective-permute-done | bytes 131104 | tf_op jit(solution)/shard_map/ppermute | solution.py:463
  85.8 0.0 collective-permute-done.12.refs_2_
  85.8 0.2 collective-permute-done.13.refs_3_
  85.9 0.4 run_chains.1
  86.4 0.6 collective-permute-start.14
  87.0 3.4 %collective-permute-start.15 = (bf16[2,128,128]{2,1,0:T(8,128)(2,1)S(1)}, bf16[2,128,128]{2,1,0:T(8,128)(2,1)S(1)}, u32[]{:S(2)}, u32[]{:S(2)}) collective-permute-start(bf16[2,128,128]{2,1,0:T(8,128)(2,1)S(1)} %get-tuple-element.58), channel_id=1, source_target_pairs={{0,64},{16,80},{32,96},{48,112},{64,0},{80,16},{96,32},{112,48},{1... | collective-permute-start | bytes 196616 | tf_op jit(solution)/shard_map/ppermute | solution.py:463
  90.4 0.5 collective-permute-done.14.refs_1_
  90.8 2.0 %collective-permute-done.15.refs_2_ = bf16[2,128,128]{2,1,0:T(8,128)(2,1)S(1)} collective-permute-done((bf16[2,128,128]{2,1,0:T(8,128)(2,1)S(1)}, bf16[2,128,128]{2,1,0:T(8,128)(2,1)S(1)}, u32[]{:S(2)}, u32[]{:S(2)}) %collective-permute-start.15) | collective-permute-done | bytes 65568 | tf_op jit(solution)/shard_map/ppermute | solution.py:463
  92.8 1.6 %collective-permute-done.16.refs_3_ = bf16[2,128,128]{2,1,0:T(8,128)(2,1)S(1)} collective-permute-done((bf16[2,128,128]{2,1,0:T(8,128)(2,1)S(1)}, bf16[2,128,128]{2,1,0:T(8,128)(2,1)S(1)}, u32[]{:S(2)}, u32[]{:S(2)}) %collective-permute-start.16) | collective-permute-done | bytes 65568 | tf_op jit(solution)/shard_map/ppermute | solution.py:463
  94.4 1.0 expand.1
  95.4 1.7 %collective-permute-start.17 = (bf16[8,128,128]{2,1,0:T(8,128)(2,1)S(1)}, bf16[8,128,128]{2,1,0:T(8,128)(2,1)S(1)}, u32[]{:S(2)}, u32[]{:S(2)}) collective-permute-start(bf16[8,128,128]{2,1,0:T(8,128)(2,1)S(1)} %get-tuple-element.61), channel_id=1, source_target_pairs={{0,16},{16,0},{32,48},{48,32},{64,80},{80,64},{96,112},{112,96},{1... | collective-permute-start | bytes 786440 | tf_op jit(solution)/shard_map/ppermute | solution.py:467
  97.1 1.2 %collective-permute-done.17.got_ref = bf16[8,128,128]{2,1,0:T(8,128)(2,1)S(1)} collective-permute-done((bf16[8,128,128]{2,1,0:T(8,128)(2,1)S(1)}, bf16[8,128,128]{2,1,0:T(8,128)(2,1)S(1)}, u32[]{:S(2)}, u32[]{:S(2)}) %collective-permute-start.17) | collective-permute-done | bytes 262176 | tf_op jit(solution)/shard_map/ppermute | solution.py:467
  98.2 1.0 %gather_rows.1 = f32[16,128,128]{2,1,0:T(8,128)} custom-call(f32[8,128,128]{2,1,0:T(8,128)S(1)} %get-tuple-element.60.mine_ref, bf16[8,128,128]{2,1,0:T(8,128)(2,1)S(1)} %collective-permute-done.17.got_ref), custom_call_target="tpu_custom_call" | custom-call | bytes 1835008 | tf_op jit(solution)/shard_map/gather_rows/pallas_call | solution.py:437
  (11 shorter events, 0.0 us)
Async XLA Ops:
  7.2 15.9 %collective-permute-start.1 = (bf16[32,128,128]{2,1,0:T(8,128)(2,1)S(1)}, bf16[32,128,128]{2,1,0:T(8,128)(2,1)S(1)}, u32[]{:S(2)}, u32[]{:S(2)}) collective-permute-start(bf16[32,128,128]{2,1,0:T(8,128)(2,1)S(1)} %get-tuple-element.38), channel_id=1, source_target_pairs={{0,12},{1,13},{2,14},{3,15},{4,0},{5,1},{6,2},{7,3},{8,4},{9,5},{1... | collective-permute-start | bytes 3145736 | tf_op jit(solution)/shard_map/ppermute | solution.py:459
  11.4 15.8 %collective-permute-start = (bf16[32,128,128]{2,1,0:T(8,128)(2,1)S(1)}, bf16[32,128,128]{2,1,0:T(8,128)(2,1)S(1)}, u32[]{:S(2)}, u32[]{:S(2)}) collective-permute-start(bf16[32,128,128]{2,1,0:T(8,128)(2,1)S(1)} %get-tuple-element.36), channel_id=1, source_target_pairs={{0,4},{1,5},{2,6},{3,7},{4,8},{5,9},{6,10},{7,11},{8,12},{9,13},{1... | collective-permute-start | bytes 3145736 | tf_op jit(solution)/shard_map/ppermute | solution.py:459
  15.5 20.8 %collective-permute-start.3 = (bf16[32,128,128]{2,1,0:T(8,128)(2,1)S(1)}, bf16[32,128,128]{2,1,0:T(8,128)(2,1)S(1)}, u32[]{:S(2)}, u32[]{:S(2)}) collective-permute-start(bf16[32,128,128]{2,1,0:T(8,128)(2,1)S(1)} %get-tuple-element.41), channel_id=1, source_target_pairs={{0,12},{1,13},{2,14},{3,15},{4,0},{5,1},{6,2},{7,3},{8,4},{9,5},{1... | collective-permute-start | bytes 3145736 | tf_op jit(solution)/shard_map/ppermute | solution.py:459
  17.3 20.5 %collective-permute-start.4 = (bf16[32,128,128]{2,1,0:T(8,128)(2,1)S(1)}, bf16[32,128,128]{2,1,0:T(8,128)(2,1)S(1)}, u32[]{:S(2)}, u32[]{:S(2)}) collective-permute-start(bf16[32,128,128]{2,1,0:T(8,128)(2,1)S(1)} %get-tuple-element.42), channel_id=1, source_target_pairs={{0,4},{1,5},{2,6},{3,7},{4,8},{5,9},{6,10},{7,11},{8,12},{9,13},{1... | collective-permute-start | bytes 3145736 | tf_op jit(solution)/shard_map/ppermute | solution.py:459
  23.6 4.1 %copy-start.3 = (s32[128]{0:T(128)S(1)}, s32[128]{0:T(128)}, u32[]{:S(2)}) copy-start(s32[128]{0:T(128)} %param.26) | copy-start | bytes 1540
  23.7 4.1 %copy-start.4 = (s32[128]{0:T(128)S(1)}, s32[128]{0:T(128)}, u32[]{:S(2)}) copy-start(s32[128]{0:T(128)} %param.25) | copy-start | bytes 1540
  23.7 4.1 %copy-start = (f32[16,128,128]{2,1,0:T(8,128)S(1)}, f32[16,128,128]{2,1,0:T(8,128)}, u32[]{:S(2)}) copy-start(f32[16,128,128]{2,1,0:T(8,128)} %diag_ref.3) | copy-start | bytes 3145732
  23.7 4.1 %copy-start.1 = (f32[16,128,128]{2,1,0:T(8,128)S(1)}, f32[16,128,128]{2,1,0:T(8,128)}, u32[]{:S(2)}) copy-start(f32[16,128,128]{2,1,0:T(8,128)} %seed_ref.1) | copy-start | bytes 3145732
  23.7 4.1 %copy-start.2 = (bf16[16,128,128]{2,1,0:T(8,128)(2,1)S(1)}, bf16[16,128,128]{2,1,0:T(8,128)(2,1)}, u32[]{:S(2)}) copy-start(bf16[16,128,128]{2,1,0:T(8,128)(2,1)} %coupling_ref.1) | copy-start | bytes 1572868
  23.7 21.9 %collective-permute-start.5 = (bf16[32,128,128]{2,1,0:T(8,128)(2,1)S(1)}, bf16[32,128,128]{2,1,0:T(8,128)(2,1)S(1)}, u32[]{:S(2)}, u32[]{:S(2)}) collective-permute-start(bf16[32,128,128]{2,1,0:T(8,128)(2,1)S(1)} %add_convert_fusion.refs_1_), channel_id=1, source_target_pairs={{0,12},{1,13},{2,14},{3,15},{4,0},{5,1},{6,2},{7,3},{8,4},{9,5},{1... | collective-permute-start | bytes 3145736 | tf_op jit(solution)/shard_map/ppermute | solution.py:459
  27.6 21.4 %collective-permute-start.2 = (bf16[32,128,128]{2,1,0:T(8,128)(2,1)S(1)}, bf16[32,128,128]{2,1,0:T(8,128)(2,1)S(1)}, u32[]{:S(2)}, u32[]{:S(2)}) collective-permute-start(bf16[32,128,128]{2,1,0:T(8,128)(2,1)S(1)} %add_convert_fusion.1.refs_0_), channel_id=1, source_target_pairs={{0,4},{1,5},{2,6},{3,7},{4,8},{5,9},{6,10},{7,11},{8,12},{9,13},{1... | collective-permute-start | bytes 3145736 | tf_op jit(solution)/shard_map/ppermute | solution.py:459
  35.2 2.6 %collective-permute-start.6 = (bf16[8,128,128]{2,1,0:T(8,128)(2,1)S(1)}, bf16[8,128,128]{2,1,0:T(8,128)(2,1)S(1)}, u32[]{:S(2)}, u32[]{:S(2)}) collective-permute-start(bf16[8,128,128]{2,1,0:T(8,128)(2,1)S(1)} %get-tuple-element.43), channel_id=1, source_target_pairs={{0,16},{16,0},{32,48},{48,32},{64,80},{80,64},{96,112},{112,96},{1... | collective-permute-start | bytes 786440 | tf_op jit(solution)/shard_map/ppermute | solution.py:467
  49.8 9.7 %collective-permute-start.7 = (bf16[16,128,128]{2,1,0:T(8,128)(2,1)S(1)}, bf16[16,128,128]{2,1,0:T(8,128)(2,1)S(1)}, u32[]{:S(2)}, u32[]{:S(2)}) collective-permute-start(bf16[16,128,128]{2,1,0:T(8,128)(2,1)S(1)} %get-tuple-element.45), channel_id=1, source_target_pairs={{0,2},{1,3},{2,0},{3,1},{4,6},{5,7},{6,4},{7,5},{8,10},{9,11},{10,... | collective-permute-start | bytes 1572872 | tf_op jit(solution)/shard_map/ppermute | solution.py:459
  52.3 13.0 %collective-permute-start.8 = (bf16[16,128,128]{2,1,0:T(8,128)(2,1)S(1)}, bf16[16,128,128]{2,1,0:T(8,128)(2,1)S(1)}, u32[]{:S(2)}, u32[]{:S(2)}) collective-permute-start(bf16[16,128,128]{2,1,0:T(8,128)(2,1)S(1)} %get-tuple-element.46), channel_id=1, source_target_pairs={{0,1},{1,2},{2,3},{3,0},{4,5},{5,6},{6,7},{7,4},{8,9},{9,10},{10,1... | collective-permute-start | bytes 1572872 | tf_op jit(solution)/shard_map/ppermute | solution.py:459
  53.6 12.5 %collective-permute-start.9 = (bf16[16,128,128]{2,1,0:T(8,128)(2,1)S(1)}, bf16[16,128,128]{2,1,0:T(8,128)(2,1)S(1)}, u32[]{:S(2)}, u32[]{:S(2)}) collective-permute-start(bf16[16,128,128]{2,1,0:T(8,128)(2,1)S(1)} %get-tuple-element.47), channel_id=1, source_target_pairs={{0,3},{1,0},{2,1},{3,2},{4,7},{5,4},{6,5},{7,6},{8,11},{9,8},{10,9... | collective-permute-start | bytes 1572872 | tf_op jit(solution)/shard_map/ppermute | solution.py:459
  68.1 8.3 %collective-permute-start.10 = (bf16[8,128,128]{2,1,0:T(8,128)(2,1)S(1)}, bf16[8,128,128]{2,1,0:T(8,128)(2,1)S(1)}, u32[]{:S(2)}, u32[]{:S(2)}) collective-permute-start(bf16[8,128,128]{2,1,0:T(8,128)(2,1)S(1)} %get-tuple-element.51), channel_id=1, source_target_pairs={{0,16},{16,0},{32,48},{48,32},{64,80},{80,64},{96,112},{112,96},{1... | collective-permute-start | bytes 786440 | tf_op jit(solution)/shard_map/ppermute | solution.py:467
  76.8 9.0 %collective-permute-start.11 = (bf16[4,128,128]{2,1,0:T(8,128)(2,1)S(1)}, bf16[4,128,128]{2,1,0:T(8,128)(2,1)S(1)}, u32[]{:S(2)}, u32[]{:S(2)}) collective-permute-start(bf16[4,128,128]{2,1,0:T(8,128)(2,1)S(1)} %get-tuple-element.53), channel_id=1, source_target_pairs={{0,32},{16,48},{32,64},{48,80},{64,96},{80,112},{96,0},{112,16},{1... | collective-permute-start | bytes 393224 | tf_op jit(solution)/shard_map/ppermute | solution.py:463
  76.9 8.9 %collective-permute-start.12 = (bf16[4,128,128]{2,1,0:T(8,128)(2,1)S(1)}, bf16[4,128,128]{2,1,0:T(8,128)(2,1)S(1)}, u32[]{:S(2)}, u32[]{:S(2)}) collective-permute-start(bf16[4,128,128]{2,1,0:T(8,128)(2,1)S(1)} %get-tuple-element.54), channel_id=1, source_target_pairs={{0,64},{16,80},{32,96},{48,112},{64,0},{80,16},{96,32},{112,48},{1... | collective-permute-start | bytes 393224 | tf_op jit(solution)/shard_map/ppermute | solution.py:463
  77.1 8.8 %collective-permute-start.13 = (bf16[4,128,128]{2,1,0:T(8,128)(2,1)S(1)}, bf16[4,128,128]{2,1,0:T(8,128)(2,1)S(1)}, u32[]{:S(2)}, u32[]{:S(2)}) collective-permute-start(bf16[4,128,128]{2,1,0:T(8,128)(2,1)S(1)} %get-tuple-element.55), channel_id=1, source_target_pairs={{0,96},{16,112},{32,0},{48,16},{64,32},{80,48},{96,64},{112,80},{1... | collective-permute-start | bytes 393224 | tf_op jit(solution)/shard_map/ppermute | solution.py:463
  86.4 4.5 %collective-permute-start.14 = (bf16[2,128,128]{2,1,0:T(8,128)(2,1)S(1)}, bf16[2,128,128]{2,1,0:T(8,128)(2,1)S(1)}, u32[]{:S(2)}, u32[]{:S(2)}) collective-permute-start(bf16[2,128,128]{2,1,0:T(8,128)(2,1)S(1)} %get-tuple-element.57), channel_id=1, source_target_pairs={{0,32},{16,48},{32,64},{48,80},{64,96},{80,112},{96,0},{112,16},{1... | collective-permute-start | bytes 196616 | tf_op jit(solution)/shard_map/ppermute | solution.py:463
  87.0 5.8 %collective-permute-start.15 = (bf16[2,128,128]{2,1,0:T(8,128)(2,1)S(1)}, bf16[2,128,128]{2,1,0:T(8,128)(2,1)S(1)}, u32[]{:S(2)}, u32[]{:S(2)}) collective-permute-start(bf16[2,128,128]{2,1,0:T(8,128)(2,1)S(1)} %get-tuple-element.58), channel_id=1, source_target_pairs={{0,64},{16,80},{32,96},{48,112},{64,0},{80,16},{96,32},{112,48},{1... | collective-permute-start | bytes 196616 | tf_op jit(solution)/shard_map/ppermute | solution.py:463
  90.4 4.0 %collective-permute-start.16 = (bf16[2,128,128]{2,1,0:T(8,128)(2,1)S(1)}, bf16[2,128,128]{2,1,0:T(8,128)(2,1)S(1)}, u32[]{:S(2)}, u32[]{:S(2)}) collective-permute-start(bf16[2,128,128]{2,1,0:T(8,128)(2,1)S(1)} %get-tuple-element.59), channel_id=1, source_target_pairs={{0,96},{16,112},{32,0},{48,16},{64,32},{80,48},{96,64},{112,80},{1... | collective-permute-start | bytes 196616 | tf_op jit(solution)/shard_map/ppermute | solution.py:463
  95.4 2.9 %collective-permute-start.17 = (bf16[8,128,128]{2,1,0:T(8,128)(2,1)S(1)}, bf16[8,128,128]{2,1,0:T(8,128)(2,1)S(1)}, u32[]{:S(2)}, u32[]{:S(2)}) collective-permute-start(bf16[8,128,128]{2,1,0:T(8,128)(2,1)S(1)} %get-tuple-element.61), channel_id=1, source_target_pairs={{0,16},{16,0},{32,48},{48,32},{64,80},{80,64},{96,112},{112,96},{1... | collective-permute-start | bytes 786440 | tf_op jit(solution)/shard_map/ppermute | solution.py:467

commit v6 on v5

--- a/solution.py
+++ b/solution.py
@@ -97,10 +97,13 @@
 
 
 def far_kernel(first, index_ref, table_ref, left_ref, right_ref, *refs):
-    *outs, left, right, table, listed, total, lsem, rsem, tsem = refs
+    *outs, left, right, table, index, listed, total, lsem, rsem, tsem, isem = refs
+    index_copy = pltpu.make_async_copy(index_ref, index, isem)
+    index_copy.start()
+    pairs = bulk(left_ref, right_ref, left, right, lsem, rsem)
     table_copy = pltpu.make_async_copy(table_ref, table, tsem)
     table_copy.start()
-    pairs = bulk(left_ref, right_ref, left, right, lsem, rsem)
+    index_copy.wait()
 
     def ready():
         table_copy.wait()
@@ -108,7 +111,7 @@
             for c in pair:
                 c.wait()
 
-    sum_cells(first, FAR_BIT, index_ref, listed, total, outs, ready, left, right, table)
+    sum_cells(first, FAR_BIT, index, listed, total, outs, ready, left, right, table)
 
 
 def near_kernel(first, index_ref, table, left, right, *refs):
@@ -126,13 +129,15 @@
     outs = pl.pallas_call(
         functools.partial(far_kernel, first),
         out_shape=cell_shapes(sizes) + [jax.ShapeDtypeStruct(x.shape, bf16) for x in (left, right, table)],
-        in_specs=[SMEM, HBM, HBM, HBM],
+        in_specs=[VMEM, HBM, HBM, HBM],
         out_specs=[VMEM] * (len(sizes) + 3),
         scratch_shapes=[
+            pltpu.SMEM((slots,), jnp.int32),
             pltpu.SMEM((slots + UNROLL,), jnp.int32),
             pltpu.VMEM((cells + 1, B, B), bf16),
             pltpu.SemaphoreType.DMA((CHUNKS,)),
             pltpu.SemaphoreType.DMA((CHUNKS,)),
+            pltpu.SemaphoreType.DMA,
             pltpu.SemaphoreType.DMA,
         ],
         compiler_params=pltpu.CompilerParams(vmem_limit_bytes=9 * MIB + cells * 4 * B * B),
@@ -231,69 +236,81 @@
 
 def first_totals_kernel(own, *refs):
     arrivals = (refs[:2], refs[2:4])
-    outs = refs[-SIDE:]
+    outs = refs[-2 * SIDE + 1 :]
     h = own.shape[0] // (2 * SIDE)
     for half in range(2):
         for b in range(SIDE):
             t = own[pl.ds((half * SIDE + b) * h, h)].astype(f32)
             for a in arrivals[half]:
                 t = t + a[pl.ds(b * h, h)].astype(f32)
-            outs[b][pl.ds(half * h, h)] = t.astype(bf16)
+            if b == 0:
+                outs[0][pl.ds(half * h, h)] = t.astype(bf16)
+            else:
+                outs[2 * b - 1 + half][...] = t.astype(bf16)
 
 
 def first_totals(own, arrivals, order):
     rows = own.shape[0] // SIDE
     return pl.pallas_call(
         first_totals_kernel,
-        out_shape=[jax.ShapeDtypeStruct((rows, B, B), bf16)] * SIDE,
+        out_shape=cell_shapes([rows] + [rows // 2] * (2 * SIDE - 2)),
         in_specs=[VMEM] * 5 + [ANY] * len(order),
-        out_specs=[VMEM] * SIDE,
+        out_specs=[VMEM] * (2 * SIDE - 1),
         compiler_params=pltpu.CompilerParams(vmem_limit_bytes=9 * MIB),
         cost_estimate=pl.CostEstimate(flops=0, bytes_accessed=256 * 2 * B * B, transcendentals=0),
         name="first_totals",
     )(own, *arrivals, *order)
 
 
-def coupling_kernel(base_ref, diag_ref, *refs):
-    new_ref, keep_ref, give_ref, held = refs[-4:]
+def coupling_kernel(base_ref, diag_ref, own_ref, *refs):
+    parts = (refs[:2], refs[2:4])
+    new_ref, keep_ref, give_ref, new, held, sem = refs[4:]
     rows = base_ref.shape[0]
     half = rows // 2
+    group = half // 2
     core = lax.axis_index("section") % 2
-    parts = refs[:SIDE]
-
-    def finish(r, _):
-        t = base_ref[r]
-        for p in parts:
-            t = t - p[r].astype(f32)
-        new_ref[r] = t
-        th, tl = split(t)
-        dh, dl = split(diag_ref[r])
-        held[(r + core * half) % rows] = -(mm(dh, th) + (mm(dh, tl) + mm(dl, th))).astype(bf16)
-        return 0
-
-    lax.fori_loop(0, rows, finish, 0, unroll=4)
+    copies = []
+    for g in range(rows // group):
+
+        def finish(i, _, g=g):
+            r = g * group + i
+            t = base_ref[r] - own_ref[r].astype(f32)
+            for p in parts[g * group // half]:
+                t = t - p[g * group % half + i].astype(f32)
+            new[r] = t
+            th, tl = split(t)
+            dh, dl = split(diag_ref[r])
+            held[(r + core * half) % rows] = -(mm(dh, th) + (mm(dh, tl) + mm(dl, th))).astype(bf16)
+            return 0
+
+        lax.fori_loop(0, group, finish, 0, unroll=True)
+        part = pl.ds(g * group, group)
+        copies.append(pltpu.make_async_copy(new.at[part], new_ref.at[part], sem.at[g]))
+        copies[-1].start()
     for i in range(half):
         keep_ref[i] = held[i]
         give_ref[i] = held[half + i]
-
-
-def coupling_and_step(base, diag, parts):
+    for c in copies:
+        c.wait()
+
+
+def coupling_and_step(base, diag, own, parts):
     rows = base.shape[0]
     half = rows // 2
     return pl.pallas_call(
         coupling_kernel,
-        out_shape=[
-            jax.ShapeDtypeStruct((rows, B, B), f32),
-            jax.ShapeDtypeStruct((half, B, B), bf16),
-            jax.ShapeDtypeStruct((half, B, B), bf16),
+        out_shape=[jax.ShapeDtypeStruct((rows, B, B), f32)] + cell_shapes([half, half]),
+        in_specs=[VMEM] * 7,
+        out_specs=[HBM, VMEM, VMEM],
+        scratch_shapes=[
+            pltpu.VMEM((rows, B, B), f32),
+            pltpu.VMEM((rows, B, B), bf16),
+            pltpu.SemaphoreType.DMA((4,)),
         ],
-        in_specs=[VMEM] * (2 + SIDE),
-        out_specs=[VMEM] * 3,
-        scratch_shapes=[pltpu.VMEM((rows, B, B), bf16)],
         compiler_params=pltpu.CompilerParams(vmem_limit_bytes=9 * MIB),
         cost_estimate=pl.CostEstimate(flops=rows * 6 * B**3, bytes_accessed=rows * 22 * B * B, transcendentals=0),
         name="coupling_and_step",
-    )(base, diag, *parts)
+    )(base, diag, own, *parts)
 
 
 def compose_kernel(chips, keep_ref, offset_ref, got_ref, got_offset_ref, *outs):
@@ -528,9 +545,13 @@
     got_offsets = partner(give_offsets, sections)
 
     arrivals = (joined_in[0], alone_in[1], alone_in[0], joined_in[1])
-    totals = first_totals(near[4], arrivals, [base, got_offsets])
-    parts = [totals[0]] + [moved(totals[k], 1, k, sections) for k in (2, 1, 3)]
-    updated, keep, give = coupling_and_step(base, diag_inverse, parts)
+    own, one_low, one_high, two_low, two_high, three_low, three_high = first_totals(near[4], arrivals, [base, got_offsets])
+    passed = [moved(two_low, 1, 1, sections), moved(two_high, 1, -1, sections)]
+    alone = [moved(three_low, 1, -1, sections), moved(one_high, 1, 1, sections)]
+    joined = [add(one_low, passed[0]), add(three_high, passed[1])]
+    joined = [moved(joined[0], 1, 1, sections), moved(joined[1], 1, -1, sections)]
+    parts = (joined[0], alone[0], alone[1], joined[1])
+    updated, keep, give = coupling_and_step(base, diag_inverse, own, parts)
     chips = sections // 2
     got = partner(give, sections)
     maps = compose(chips, keep, offsets, got, got_offsets)

time: 97.5 us -> 96.9 us (level); the launches traced: 99.4 us -> 96.7 us
  waiting for transfers between devices: 42.5 us -> 34.4 us
  starting transfers between devices: 31.3 us -> 38.6 us
  Pallas kernels: 22.2 us -> 20.3 us
    ppermute x9 -> x12, starting transfers between devices: 14.8 us -> 21.5 us  [moved(): return lax.ppermute(x, ('section', 'row'), pairs)]
    ppermute x9 -> x12, waiting for transfers between devices: 29.8 us -> 24.4 us  [moved(): return lax.ppermute(x, ('section', 'row'), pairs)]
    ppermute x6, waiting for transfers between devices: 10.4 us -> 7.66 us  [across(): lax.ppermute(x, 'section', [(i, (i + 2 * by) % sections) for i in range(s...]
    ppermute x6, starting transfers between devices: 6.73 us -> 9.2 us  [across(): lax.ppermute(x, 'section', [(i, (i + 2 * by) % sections) for i in range(s...]
    ppermute x3, starting transfers between devices: 9.85 us -> 7.89 us  [partner(): return lax.ppermute(x, 'section', [(i, i ^ 1) for i in range(sections)])]
    pallas_call x1, Pallas kernels: 5.22 us -> 4.21 us  [far_sums(): pl.pallas_call(functools.partial(far_kernel, first), out_shape=cell_shape...]
  transfers between devices with their start and end apart: 18 -> 21, of which waited for: 14 -> 15; matrix products, arithmetic and copies ran while one was open for 1% -> 1% of each run, Pallas kernels for 12% -> 11%
where the time goes in v6:
time: 96.9 us; the launch traced here: 96.7 us
  starting transfers between devices  38.6 us (40%)
  waiting for transfers between devices  34.4 us (36%)
  Pallas kernels  20.3 us (21%)
  other arithmetic  1.7 us (2%)
  between operations  1.66 us (2%)
    ppermute x12, waiting for transfers between devices, moved(): return lax.ppermute(x, ('section', 'row'), pairs)  24.4 us
    ppermute x12, starting transfers between devices, moved(): return lax.ppermute(x, ('section', 'row'), pairs)  21.5 us
    ppermute x6, starting transfers between devices, across(): lax.ppermute(x, 'section', [(i, (i + 2 * by) % sections) for i in range(s...  9.2 us
    ppermute x3, starting transfers between devices, partner(): return lax.ppermute(x, 'section', [(i, i ^ 1) for i in range(sections)])  7.89 us
    ppermute x6, waiting for transfers between devices, across(): lax.ppermute(x, 'section', [(i, (i + 2 * by) % sections) for i in range(s...  7.66 us
    pallas_call x1, Pallas kernels, local_and_offset(): pl.pallas_call(local_kernel, out_shape=[jax.ShapeDtypeStruct((rows, B, B)...  7.4 us
    pallas_call x1, Pallas kernels, far_sums(): pl.pallas_call(functools.partial(far_kernel, first), out_shape=cell_shape...  4.21 us
    pallas_call x1, Pallas kernels, near_sums(): pl.pallas_call(functools.partial(near_kernel, first), out_shape=cell_shap...  3.58 us
  transfers between devices with their start and end apart: 21, of which 15 were waited for; matrix products, arithmetic and copies ran while one was open for 1% of the time, Pallas kernels for 11%

profile of v6, /device:TPU:1, one launch (start us, length us, event | category | flops | bytes accessed | tf_op | source)
XLA Modules:
  0.0 96.7 jit_solution(10894919154466996018)
XLA Ops:
  1.3 0.7 fusion.5.index_ref
  2.0 4.2 %far_sums.1 = (bf16[32,128,128]{2,1,0:T(8,128)(2,1)S(1)}, bf16[32,128,128]{2,1,0:T(8,128)(2,1)S(1)}, bf16[128,128,128]{2,1,0:T(8,128)(2,1)S(1)}, bf16[128,128,12...) custom-call(s32[128]{0:T(128)S(1)} %fusion.5.index_ref, bf16[4,128,128]{2,1,0:T(8,128)(2,1)} %table_ref.3, ...), custom_call_target="tpu_custom_call" | custom-call | flops 268435456 | bytes 18874368 | tf_op jit(solution)/shard_map/far_sums/pallas_call | solution.py:129
  6.2 5.1 %collective-permute-start.1 = (bf16[32,128,128]{2,1,0:T(8,128)(2,1)S(1)}, bf16[32,128,128]{2,1,0:T(8,128)(2,1)S(1)}, u32[]{:S(2)}, u32[]{:S(2)}) collective-permute-start(bf16[32,128,128]{2,1,0:T(8,128)(2,1)S(1)} %get-tuple-element.41), channel_id=1, source_target_pairs={{0,12},{1,13},{2,14},{3,15},{4,0},{5,1},{6,2},{7,3},{8,4},{9,5},{1... | collective-permute-start | bytes 3145736 | tf_op jit(solution)/shard_map/ppermute | solution.py:476
  11.4 3.6 %near_sums.1 = (bf16[32,128,128]{2,1,0:T(8,128)(2,1)S(1)}, bf16[32,128,128]{2,1,0:T(8,128)(2,1)S(1)}, bf16[32,128,128]{2,1,0:T(8,128)(2,1)S(1)}, bf16[32,128,128...) custom-call(s32[128]{0:T(128)S(1)} %fusion.5.index_ref, bf16[4,128,128]{2,1,0:T(8,128)(2,1)S(1)} %get-tuple-element.35.table, ...), custom_call_target="tpu_custom_call" | custom-call | flops 805306368 | bytes 14680064 | tf_op jit(solution)/shard_map/near_sums/pallas_call | solution.py:156
  15.0 3.7 %collective-permute-start.3 = (bf16[32,128,128]{2,1,0:T(8,128)(2,1)S(1)}, bf16[32,128,128]{2,1,0:T(8,128)(2,1)S(1)}, u32[]{:S(2)}, u32[]{:S(2)}) collective-permute-start(bf16[32,128,128]{2,1,0:T(8,128)(2,1)S(1)} %get-tuple-element.44), channel_id=1, source_target_pairs={{0,12},{1,13},{2,14},{3,15},{4,0},{5,1},{6,2},{7,3},{8,4},{9,5},{1... | collective-permute-start | bytes 3145736 | tf_op jit(solution)/shard_map/ppermute | solution.py:476
  18.7 4.5 %collective-permute-done.1 = bf16[32,128,128]{2,1,0:T(8,128)(2,1)S(1)} collective-permute-done((bf16[32,128,128]{2,1,0:T(8,128)(2,1)S(1)}, bf16[32,128,128]{2,1,0:T(8,128)(2,1)S(1)}, u32[]{:S(2)}, u32[]{:S(2)}) %collective-permute-start.1) | collective-permute-done | bytes 1048608 | tf_op jit(solution)/shard_map/ppermute | solution.py:476
  23.1 0.4 add_convert_fusion.refs_1_
  23.5 0.0 copy-start.3
  23.6 3.5 %collective-permute-start.5 = (bf16[32,128,128]{2,1,0:T(8,128)(2,1)S(1)}, bf16[32,128,128]{2,1,0:T(8,128)(2,1)S(1)}, u32[]{:S(2)}, u32[]{:S(2)}) collective-permute-start(bf16[32,128,128]{2,1,0:T(8,128)(2,1)S(1)} %add_convert_fusion.refs_1_), channel_id=1, source_target_pairs={{0,12},{1,13},{2,14},{3,15},{4,0},{5,1},{6,2},{7,3},{8,4},{9,5},{1... | collective-permute-start | bytes 3145736 | tf_op jit(solution)/shard_map/ppermute | solution.py:476
  27.0 0.5 add_convert_fusion.1.refs_0_
  27.5 0.1 collective-permute-start.2
  27.7 7.4 %local_and_offset.1 = (f32[16,128,128]{2,1,0:T(8,128)S(1)}, bf16[8,128,128]{2,1,0:T(8,128)(2,1)S(1)}, bf16[8,128,128]{2,1,0:T(8,128)(2,1)S(1)}) custom-call(s32[128]{0:T(128)S(1)} %shift-left_or_fusion.index_ref, bf16[4,128,128]{2,1,0:T(8,128)(2,1)} %table_ref.3, bf16[16,128,128]{2,1,0:T(8,128)(2,1)S(1)} %copy-done.2, bf16[128,128,128]{2,1,0:T(8,128)(2,1)} %left_ref.3, ...), custom_call_target="tpu_custom_call" | custom-call | flops 1073741824 | bytes 12582912 | tf_op jit(solution)/shard_map/local_and_offset/pallas_call | solution.py:215
  35.1 1.0 %collective-permute-start.6 = (bf16[8,128,128]{2,1,0:T(8,128)(2,1)S(1)}, bf16[8,128,128]{2,1,0:T(8,128)(2,1)S(1)}, u32[]{:S(2)}, u32[]{:S(2)}) collective-permute-start(bf16[8,128,128]{2,1,0:T(8,128)(2,1)S(1)} %get-tuple-element.46), channel_id=1, source_target_pairs={{0,16},{16,0},{32,48},{48,32},{64,80},{80,64},{96,112},{112,96},{1... | collective-permute-start | bytes 786440 | tf_op jit(solution)/shard_map/ppermute | solution.py:484
  36.1 1.7 %collective-permute-done.4.refs_2_ = bf16[32,128,128]{2,1,0:T(8,128)(2,1)S(1)} collective-permute-done((bf16[32,128,128]{2,1,0:T(8,128)(2,1)S(1)}, bf16[32,128,128]{2,1,0:T(8,128)(2,1)S(1)}, u32[]{:S(2)}, u32[]{:S(2)}) %collective-permute-start.4) | collective-permute-done | bytes 1048608 | tf_op jit(solution)/shard_map/ppermute | solution.py:476
  37.8 7.8 %collective-permute-done.5.refs_3_ = bf16[32,128,128]{2,1,0:T(8,128)(2,1)S(1)} collective-permute-done((bf16[32,128,128]{2,1,0:T(8,128)(2,1)S(1)}, bf16[32,128,128]{2,1,0:T(8,128)(2,1)S(1)}, u32[]{:S(2)}, u32[]{:S(2)}) %collective-permute-start.5) | collective-permute-done | bytes 1048608 | tf_op jit(solution)/shard_map/ppermute | solution.py:476
  45.6 3.4 %collective-permute-done.2.refs_0_ = bf16[32,128,128]{2,1,0:T(8,128)(2,1)S(1)} collective-permute-done((bf16[32,128,128]{2,1,0:T(8,128)(2,1)S(1)}, bf16[32,128,128]{2,1,0:T(8,128)(2,1)S(1)}, u32[]{:S(2)}, u32[]{:S(2)}) %collective-permute-start.2) | collective-permute-done | bytes 1048608 | tf_op jit(solution)/shard_map/ppermute | solution.py:476
  49.0 0.7 first_totals.1
  49.7 2.7 %collective-permute-start.11 = (bf16[8,128,128]{2,1,0:T(8,128)(2,1)S(1)}, bf16[8,128,128]{2,1,0:T(8,128)(2,1)S(1)}, u32[]{:S(2)}, u32[]{:S(2)}) collective-permute-start(bf16[8,128,128]{2,1,0:T(8,128)(2,1)S(1)} %get-tuple-element.53), channel_id=1, source_target_pairs={{0,3},{1,0},{2,1},{3,2},{4,7},{5,4},{6,5},{7,6},{8,11},{9,8},{10,9... | collective-permute-start | bytes 786440 | tf_op jit(solution)/shard_map/ppermute | solution.py:476
  52.5 0.2 collective-permute-start.10
  52.7 2.5 %collective-permute-start.9 = (bf16[8,128,128]{2,1,0:T(8,128)(2,1)S(1)}, bf16[8,128,128]{2,1,0:T(8,128)(2,1)S(1)}, u32[]{:S(2)}, u32[]{:S(2)}) collective-permute-start(bf16[8,128,128]{2,1,0:T(8,128)(2,1)S(1)} %get-tuple-element.50), channel_id=1, source_target_pairs={{0,3},{1,0},{2,1},{3,2},{4,7},{5,4},{6,5},{7,6},{8,11},{9,8},{10,9... | collective-permute-start | bytes 786440 | tf_op jit(solution)/shard_map/ppermute | solution.py:476
  55.2 0.6 collective-permute-done.11
  55.8 0.1 add_convert_fusion.2
  55.9 3.5 %collective-permute-start.12 = (bf16[8,128,128]{2,1,0:T(8,128)(2,1)S(1)}, bf16[8,128,128]{2,1,0:T(8,128)(2,1)S(1)}, u32[]{:S(2)}, u32[]{:S(2)}) collective-permute-start(bf16[8,128,128]{2,1,0:T(8,128)(2,1)S(1)} %add_convert_fusion.2), channel_id=1, source_target_pairs={{0,3},{1,0},{2,1},{3,2},{4,7},{5,4},{6,5},{7,6},{8,11},{9,8},{10,9... | collective-permute-start | bytes 786440 | tf_op jit(solution)/shard_map/ppermute | solution.py:476
  59.4 0.1 add_convert_fusion.3
  59.4 0.3 collective-permute-start.8
  59.7 2.3 %collective-permute-done.10.refs_2_ = bf16[8,128,128]{2,1,0:T(8,128)(2,1)S(1)} collective-permute-done((bf16[8,128,128]{2,1,0:T(8,128)(2,1)S(1)}, bf16[8,128,128]{2,1,0:T(8,128)(2,1)S(1)}, u32[]{:S(2)}, u32[]{:S(2)}) %collective-permute-start.10) | collective-permute-done | bytes 262176 | tf_op jit(solution)/shard_map/ppermute | solution.py:476
  62.0 0.7 collective-permute-done.12.refs_3_
  62.7 3.4 %collective-permute-done.8.refs_0_ = bf16[8,128,128]{2,1,0:T(8,128)(2,1)S(1)} collective-permute-done((bf16[8,128,128]{2,1,0:T(8,128)(2,1)S(1)}, bf16[8,128,128]{2,1,0:T(8,128)(2,1)S(1)}, u32[]{:S(2)}, u32[]{:S(2)}) %collective-permute-start.8) | collective-permute-done | bytes 262176 | tf_op jit(solution)/shard_map/ppermute | solution.py:476
  66.1 1.5 %coupling_and_step.1 = (f32[16,128,128]{2,1,0:T(8,128)}, bf16[8,128,128]{2,1,0:T(8,128)(2,1)S(1)}, bf16[8,128,128]{2,1,0:T(8,128)(2,1)S(1)}) custom-call(f32[16,128,128]{2,1,0:T(8,128)S(1)} %get-tuple-element.42.refs_4_.base_ref, f32[16,128,128]{2,1,0:T(8,128)S(1)} %copy-done, bf16[16,128,128]{2,1,0:T(8,128)(2,1)S(1)} %get-tuple-element.47.own_ref, ...), custom_call_target="tpu_custom_call" | custom-call | flops 201326592 | bytes 5767168 | tf_op jit(solution)/shard_map/coupling_and_step/pallas_call | solution.py:300
  67.7 4.5 %collective-permute-start.13 = (bf16[8,128,128]{2,1,0:T(8,128)(2,1)S(1)}, bf16[8,128,128]{2,1,0:T(8,128)(2,1)S(1)}, u32[]{:S(2)}, u32[]{:S(2)}) collective-permute-start(bf16[8,128,128]{2,1,0:T(8,128)(2,1)S(1)} %get-tuple-element.57), channel_id=1, source_target_pairs={{0,16},{16,0},{32,48},{48,32},{64,80},{80,64},{96,112},{112,96},{1... | collective-permute-start | bytes 786440 | tf_op jit(solution)/shard_map/ppermute | solution.py:484
  72.1 1.2 %collective-permute-done.13.got_ref = bf16[8,128,128]{2,1,0:T(8,128)(2,1)S(1)} collective-permute-done((bf16[8,128,128]{2,1,0:T(8,128)(2,1)S(1)}, bf16[8,128,128]{2,1,0:T(8,128)(2,1)S(1)}, u32[]{:S(2)}, u32[]{:S(2)}) %collective-permute-start.13) | collective-permute-done | bytes 262176 | tf_op jit(solution)/shard_map/ppermute | solution.py:484
  73.3 0.4 compose.1
  73.7 1.4 %collective-permute-start.14 = (bf16[4,128,128]{2,1,0:T(8,128)(2,1)S(1)}, bf16[4,128,128]{2,1,0:T(8,128)(2,1)S(1)}, u32[]{:S(2)}, u32[]{:S(2)}) collective-permute-start(bf16[4,128,128]{2,1,0:T(8,128)(2,1)S(1)} %get-tuple-element.59), channel_id=1, source_target_pairs={{0,32},{16,48},{32,64},{48,80},{64,96},{80,112},{96,0},{112,16},{1... | collective-permute-start | bytes 393224 | tf_op jit(solution)/shard_map/ppermute | solution.py:480
  75.1 2.6 %collective-permute-start.15 = (bf16[4,128,128]{2,1,0:T(8,128)(2,1)S(1)}, bf16[4,128,128]{2,1,0:T(8,128)(2,1)S(1)}, u32[]{:S(2)}, u32[]{:S(2)}) collective-permute-start(bf16[4,128,128]{2,1,0:T(8,128)(2,1)S(1)} %get-tuple-element.60), channel_id=1, source_target_pairs={{0,64},{16,80},{32,96},{48,112},{64,0},{80,16},{96,32},{112,48},{1... | collective-permute-start | bytes 393224 | tf_op jit(solution)/shard_map/ppermute | solution.py:480
  77.7 1.1 %collective-permute-start.16 = (bf16[4,128,128]{2,1,0:T(8,128)(2,1)S(1)}, bf16[4,128,128]{2,1,0:T(8,128)(2,1)S(1)}, u32[]{:S(2)}, u32[]{:S(2)}) collective-permute-start(bf16[4,128,128]{2,1,0:T(8,128)(2,1)S(1)} %get-tuple-element.61), channel_id=1, source_target_pairs={{0,96},{16,112},{32,0},{48,16},{64,32},{80,48},{96,64},{112,80},{1... | collective-permute-start | bytes 393224 | tf_op jit(solution)/shard_map/ppermute | solution.py:480
  78.7 1.1 %collective-permute-done.14.refs_1_ = bf16[4,128,128]{2,1,0:T(8,128)(2,1)S(1)} collective-permute-done((bf16[4,128,128]{2,1,0:T(8,128)(2,1)S(1)}, bf16[4,128,128]{2,1,0:T(8,128)(2,1)S(1)}, u32[]{:S(2)}, u32[]{:S(2)}) %collective-permute-start.14) | collective-permute-done | bytes 131104 | tf_op jit(solution)/shard_map/ppermute | solution.py:480
  79.8 3.9 %collective-permute-done.15.refs_2_ = bf16[4,128,128]{2,1,0:T(8,128)(2,1)S(1)} collective-permute-done((bf16[4,128,128]{2,1,0:T(8,128)(2,1)S(1)}, bf16[4,128,128]{2,1,0:T(8,128)(2,1)S(1)}, u32[]{:S(2)}, u32[]{:S(2)}) %collective-permute-start.15) | collective-permute-done | bytes 131104 | tf_op jit(solution)/shard_map/ppermute | solution.py:480
  83.7 0.4 run_chains.1
  84.2 1.0 %collective-permute-start.17 = (bf16[2,128,128]{2,1,0:T(8,128)(2,1)S(1)}, bf16[2,128,128]{2,1,0:T(8,128)(2,1)S(1)}, u32[]{:S(2)}, u32[]{:S(2)}) collective-permute-start(bf16[2,128,128]{2,1,0:T(8,128)(2,1)S(1)} %get-tuple-element.63), channel_id=1, source_target_pairs={{0,32},{16,48},{32,64},{48,80},{64,96},{80,112},{96,0},{112,16},{1... | collective-permute-start | bytes 196616 | tf_op jit(solution)/shard_map/ppermute | solution.py:480
  85.2 2.2 %collective-permute-start.18 = (bf16[2,128,128]{2,1,0:T(8,128)(2,1)S(1)}, bf16[2,128,128]{2,1,0:T(8,128)(2,1)S(1)}, u32[]{:S(2)}, u32[]{:S(2)}) collective-permute-start(bf16[2,128,128]{2,1,0:T(8,128)(2,1)S(1)} %get-tuple-element.64), channel_id=1, source_target_pairs={{0,64},{16,80},{32,96},{48,112},{64,0},{80,16},{96,32},{112,48},{1... | collective-permute-start | bytes 196616 | tf_op jit(solution)/shard_map/ppermute | solution.py:480
  87.4 0.9 collective-permute-start.19
  88.3 0.2 collective-permute-done.17.refs_1_
  88.6 1.2 %collective-permute-done.18.refs_2_ = bf16[2,128,128]{2,1,0:T(8,128)(2,1)S(1)} collective-permute-done((bf16[2,128,128]{2,1,0:T(8,128)(2,1)S(1)}, bf16[2,128,128]{2,1,0:T(8,128)(2,1)S(1)}, u32[]{:S(2)}, u32[]{:S(2)}) %collective-permute-start.18) | collective-permute-done | bytes 65568 | tf_op jit(solution)/shard_map/ppermute | solution.py:480
  89.8 1.2 %collective-permute-done.19.refs_3_ = bf16[2,128,128]{2,1,0:T(8,128)(2,1)S(1)} collective-permute-done((bf16[2,128,128]{2,1,0:T(8,128)(2,1)S(1)}, bf16[2,128,128]{2,1,0:T(8,128)(2,1)S(1)}, u32[]{:S(2)}, u32[]{:S(2)}) %collective-permute-start.19) | collective-permute-done | bytes 65568 | tf_op jit(solution)/shard_map/ppermute | solution.py:480
  91.0 1.0 %expand.1 = (f32[8,128,128]{2,1,0:T(8,128)S(1)}, bf16[8,128,128]{2,1,0:T(8,128)(2,1)S(1)}) custom-call(bf16[8,128,128]{2,1,0:T(8,128)(2,1)S(1)} %get-tuple-element.55.keep_ref, bf16[8,128,128]{2,1,0:T(8,128)(2,1)S(1)} %get-tuple-element.56.offset_ref, bf16[8,128,128]{2,1,0:T(8,128)(2,1)S(1)} %collective-permute-done.13.got_ref, ...), custom_call_target="tpu_custom_call" | custom-call | flops 100663296 | bytes 2097152 | tf_op jit(solution)/shard_map/expand/pallas_call | solution.py:428
  92.0 2.4 %collective-permute-start.20 = (bf16[8,128,128]{2,1,0:T(8,128)(2,1)S(1)}, bf16[8,128,128]{2,1,0:T(8,128)(2,1)S(1)}, u32[]{:S(2)}, u32[]{:S(2)}) collective-permute-start(bf16[8,128,128]{2,1,0:T(8,128)(2,1)S(1)} %get-tuple-element.67), channel_id=1, source_target_pairs={{0,16},{16,0},{32,48},{48,32},{64,80},{80,64},{96,112},{112,96},{1... | collective-permute-start | bytes 786440 | tf_op jit(solution)/shard_map/ppermute | solution.py:484
  94.4 1.2 %collective-permute-done.20.got_ref = bf16[8,128,128]{2,1,0:T(8,128)(2,1)S(1)} collective-permute-done((bf16[8,128,128]{2,1,0:T(8,128)(2,1)S(1)}, bf16[8,128,128]{2,1,0:T(8,128)(2,1)S(1)}, u32[]{:S(2)}, u32[]{:S(2)}) %collective-permute-start.20) | collective-permute-done | bytes 262176 | tf_op jit(solution)/shard_map/ppermute | solution.py:484
  95.6 1.0 %gather_rows.1 = f32[16,128,128]{2,1,0:T(8,128)} custom-call(f32[8,128,128]{2,1,0:T(8,128)S(1)} %get-tuple-element.66.mine_ref, bf16[8,128,128]{2,1,0:T(8,128)(2,1)S(1)} %collective-permute-done.20.got_ref), custom_call_target="tpu_custom_call" | custom-call | bytes 1835008 | tf_op jit(solution)/shard_map/gather_rows/pallas_call | solution.py:454
  (19 shorter events, 0.1 us)
Async XLA Ops:
  6.2 16.9 %collective-permute-start.1 = (bf16[32,128,128]{2,1,0:T(8,128)(2,1)S(1)}, bf16[32,128,128]{2,1,0:T(8,128)(2,1)S(1)}, u32[]{:S(2)}, u32[]{:S(2)}) collective-permute-start(bf16[32,128,128]{2,1,0:T(8,128)(2,1)S(1)} %get-tuple-element.41), channel_id=1, source_target_pairs={{0,12},{1,13},{2,14},{3,15},{4,0},{5,1},{6,2},{7,3},{8,4},{9,5},{1... | collective-permute-start | bytes 3145736 | tf_op jit(solution)/shard_map/ppermute | solution.py:476
  11.4 15.7 %collective-permute-start = (bf16[32,128,128]{2,1,0:T(8,128)(2,1)S(1)}, bf16[32,128,128]{2,1,0:T(8,128)(2,1)S(1)}, u32[]{:S(2)}, u32[]{:S(2)}) collective-permute-start(bf16[32,128,128]{2,1,0:T(8,128)(2,1)S(1)} %get-tuple-element.39), channel_id=1, source_target_pairs={{0,4},{1,5},{2,6},{3,7},{4,8},{5,9},{6,10},{7,11},{8,12},{9,13},{1... | collective-permute-start | bytes 3145736 | tf_op jit(solution)/shard_map/ppermute | solution.py:476
  15.0 21.1 %collective-permute-start.3 = (bf16[32,128,128]{2,1,0:T(8,128)(2,1)S(1)}, bf16[32,128,128]{2,1,0:T(8,128)(2,1)S(1)}, u32[]{:S(2)}, u32[]{:S(2)}) collective-permute-start(bf16[32,128,128]{2,1,0:T(8,128)(2,1)S(1)} %get-tuple-element.44), channel_id=1, source_target_pairs={{0,12},{1,13},{2,14},{3,15},{4,0},{5,1},{6,2},{7,3},{8,4},{9,5},{1... | collective-permute-start | bytes 3145736 | tf_op jit(solution)/shard_map/ppermute | solution.py:476
  18.6 19.1 %collective-permute-start.4 = (bf16[32,128,128]{2,1,0:T(8,128)(2,1)S(1)}, bf16[32,128,128]{2,1,0:T(8,128)(2,1)S(1)}, u32[]{:S(2)}, u32[]{:S(2)}) collective-permute-start(bf16[32,128,128]{2,1,0:T(8,128)(2,1)S(1)} %get-tuple-element.45), channel_id=1, source_target_pairs={{0,4},{1,5},{2,6},{3,7},{4,8},{5,9},{6,10},{7,11},{8,12},{9,13},{1... | collective-permute-start | bytes 3145736 | tf_op jit(solution)/shard_map/ppermute | solution.py:476
  23.5 4.1 %copy-start.3 = (s32[128]{0:T(128)S(1)}, s32[128]{0:T(128)}, u32[]{:S(2)}) copy-start(s32[128]{0:T(128)} %param.26) | copy-start | bytes 1540
  23.5 4.1 %copy-start.4 = (s32[128]{0:T(128)S(1)}, s32[128]{0:T(128)}, u32[]{:S(2)}) copy-start(s32[128]{0:T(128)} %param.25) | copy-start | bytes 1540
  23.5 4.1 %copy-start = (f32[16,128,128]{2,1,0:T(8,128)S(1)}, f32[16,128,128]{2,1,0:T(8,128)}, u32[]{:S(2)}) copy-start(f32[16,128,128]{2,1,0:T(8,128)} %diag_ref.3) | copy-start | bytes 3145732
  23.5 4.1 %copy-start.1 = (f32[16,128,128]{2,1,0:T(8,128)S(1)}, f32[16,128,128]{2,1,0:T(8,128)}, u32[]{:S(2)}) copy-start(f32[16,128,128]{2,1,0:T(8,128)} %seed_ref.1) | copy-start | bytes 3145732
  23.6 4.1 %copy-start.2 = (bf16[16,128,128]{2,1,0:T(8,128)(2,1)S(1)}, bf16[16,128,128]{2,1,0:T(8,128)(2,1)}, u32[]{:S(2)}) copy-start(bf16[16,128,128]{2,1,0:T(8,128)(2,1)} %coupling_ref.1) | copy-start | bytes 1572868
  23.6 22.0 %collective-permute-start.5 = (bf16[32,128,128]{2,1,0:T(8,128)(2,1)S(1)}, bf16[32,128,128]{2,1,0:T(8,128)(2,1)S(1)}, u32[]{:S(2)}, u32[]{:S(2)}) collective-permute-start(bf16[32,128,128]{2,1,0:T(8,128)(2,1)S(1)} %add_convert_fusion.refs_1_), channel_id=1, source_target_pairs={{0,12},{1,13},{2,14},{3,15},{4,0},{5,1},{6,2},{7,3},{8,4},{9,5},{1... | collective-permute-start | bytes 3145736 | tf_op jit(solution)/shard_map/ppermute | solution.py:476
  27.5 21.5 %collective-permute-start.2 = (bf16[32,128,128]{2,1,0:T(8,128)(2,1)S(1)}, bf16[32,128,128]{2,1,0:T(8,128)(2,1)S(1)}, u32[]{:S(2)}, u32[]{:S(2)}) collective-permute-start(bf16[32,128,128]{2,1,0:T(8,128)(2,1)S(1)} %add_convert_fusion.1.refs_0_), channel_id=1, source_target_pairs={{0,4},{1,5},{2,6},{3,7},{4,8},{5,9},{6,10},{7,11},{8,12},{9,13},{1... | collective-permute-start | bytes 3145736 | tf_op jit(solution)/shard_map/ppermute | solution.py:476
  35.1 2.7 %collective-permute-start.6 = (bf16[8,128,128]{2,1,0:T(8,128)(2,1)S(1)}, bf16[8,128,128]{2,1,0:T(8,128)(2,1)S(1)}, u32[]{:S(2)}, u32[]{:S(2)}) collective-permute-start(bf16[8,128,128]{2,1,0:T(8,128)(2,1)S(1)} %get-tuple-element.46), channel_id=1, source_target_pairs={{0,16},{16,0},{32,48},{48,32},{64,80},{80,64},{96,112},{112,96},{1... | collective-permute-start | bytes 786440 | tf_op jit(solution)/shard_map/ppermute | solution.py:484
  49.7 6.0 %collective-permute-start.11 = (bf16[8,128,128]{2,1,0:T(8,128)(2,1)S(1)}, bf16[8,128,128]{2,1,0:T(8,128)(2,1)S(1)}, u32[]{:S(2)}, u32[]{:S(2)}) collective-permute-start(bf16[8,128,128]{2,1,0:T(8,128)(2,1)S(1)} %get-tuple-element.53), channel_id=1, source_target_pairs={{0,3},{1,0},{2,1},{3,2},{4,7},{5,4},{6,5},{7,6},{8,11},{9,8},{10,9... | collective-permute-start | bytes 786440 | tf_op jit(solution)/shard_map/ppermute | solution.py:476
  52.5 6.9 %collective-permute-start.7 = (bf16[8,128,128]{2,1,0:T(8,128)(2,1)S(1)}, bf16[8,128,128]{2,1,0:T(8,128)(2,1)S(1)}, u32[]{:S(2)}, u32[]{:S(2)}) collective-permute-start(bf16[8,128,128]{2,1,0:T(8,128)(2,1)S(1)} %get-tuple-element.49), channel_id=1, source_target_pairs={{0,1},{1,2},{2,3},{3,0},{4,5},{5,6},{6,7},{7,4},{8,9},{9,10},{10,1... | collective-permute-start | bytes 786440 | tf_op jit(solution)/shard_map/ppermute | solution.py:476
  52.5 9.5 %collective-permute-start.10 = (bf16[8,128,128]{2,1,0:T(8,128)(2,1)S(1)}, bf16[8,128,128]{2,1,0:T(8,128)(2,1)S(1)}, u32[]{:S(2)}, u32[]{:S(2)}) collective-permute-start(bf16[8,128,128]{2,1,0:T(8,128)(2,1)S(1)} %get-tuple-element.51), channel_id=1, source_target_pairs={{0,1},{1,2},{2,3},{3,0},{4,5},{5,6},{6,7},{7,4},{8,9},{9,10},{10,1... | collective-permute-start | bytes 786440 | tf_op jit(solution)/shard_map/ppermute | solution.py:476
  52.7 9.3 %collective-permute-start.9 = (bf16[8,128,128]{2,1,0:T(8,128)(2,1)S(1)}, bf16[8,128,128]{2,1,0:T(8,128)(2,1)S(1)}, u32[]{:S(2)}, u32[]{:S(2)}) collective-permute-start(bf16[8,128,128]{2,1,0:T(8,128)(2,1)S(1)} %get-tuple-element.50), channel_id=1, source_target_pairs={{0,3},{1,0},{2,1},{3,2},{4,7},{5,4},{6,5},{7,6},{8,11},{9,8},{10,9... | collective-permute-start | bytes 786440 | tf_op jit(solution)/shard_map/ppermute | solution.py:476
  55.9 6.8 %collective-permute-start.12 = (bf16[8,128,128]{2,1,0:T(8,128)(2,1)S(1)}, bf16[8,128,128]{2,1,0:T(8,128)(2,1)S(1)}, u32[]{:S(2)}, u32[]{:S(2)}) collective-permute-start(bf16[8,128,128]{2,1,0:T(8,128)(2,1)S(1)} %add_convert_fusion.2), channel_id=1, source_target_pairs={{0,3},{1,0},{2,1},{3,2},{4,7},{5,4},{6,5},{7,6},{8,11},{9,8},{10,9... | collective-permute-start | bytes 786440 | tf_op jit(solution)/shard_map/ppermute | solution.py:476
  59.4 6.7 %collective-permute-start.8 = (bf16[8,128,128]{2,1,0:T(8,128)(2,1)S(1)}, bf16[8,128,128]{2,1,0:T(8,128)(2,1)S(1)}, u32[]{:S(2)}, u32[]{:S(2)}) collective-permute-start(bf16[8,128,128]{2,1,0:T(8,128)(2,1)S(1)} %add_convert_fusion.3), channel_id=1, source_target_pairs={{0,1},{1,2},{2,3},{3,0},{4,5},{5,6},{6,7},{7,4},{8,9},{9,10},{10,1... | collective-permute-start | bytes 786440 | tf_op jit(solution)/shard_map/ppermute | solution.py:476
  67.7 5.6 %collective-permute-start.13 = (bf16[8,128,128]{2,1,0:T(8,128)(2,1)S(1)}, bf16[8,128,128]{2,1,0:T(8,128)(2,1)S(1)}, u32[]{:S(2)}, u32[]{:S(2)}) collective-permute-start(bf16[8,128,128]{2,1,0:T(8,128)(2,1)S(1)} %get-tuple-element.57), channel_id=1, source_target_pairs={{0,16},{16,0},{32,48},{48,32},{64,80},{80,64},{96,112},{112,96},{1... | collective-permute-start | bytes 786440 | tf_op jit(solution)/shard_map/ppermute | solution.py:484
  73.7 6.1 %collective-permute-start.14 = (bf16[4,128,128]{2,1,0:T(8,128)(2,1)S(1)}, bf16[4,128,128]{2,1,0:T(8,128)(2,1)S(1)}, u32[]{:S(2)}, u32[]{:S(2)}) collective-permute-start(bf16[4,128,128]{2,1,0:T(8,128)(2,1)S(1)} %get-tuple-element.59), channel_id=1, source_target_pairs={{0,32},{16,48},{32,64},{48,80},{64,96},{80,112},{96,0},{112,16},{1... | collective-permute-start | bytes 393224 | tf_op jit(solution)/shard_map/ppermute | solution.py:480
  75.1 8.7 %collective-permute-start.15 = (bf16[4,128,128]{2,1,0:T(8,128)(2,1)S(1)}, bf16[4,128,128]{2,1,0:T(8,128)(2,1)S(1)}, u32[]{:S(2)}, u32[]{:S(2)}) collective-permute-start(bf16[4,128,128]{2,1,0:T(8,128)(2,1)S(1)} %get-tuple-element.60), channel_id=1, source_target_pairs={{0,64},{16,80},{32,96},{48,112},{64,0},{80,16},{96,32},{112,48},{1... | collective-permute-start | bytes 393224 | tf_op jit(solution)/shard_map/ppermute | solution.py:480
  77.7 6.1 %collective-permute-start.16 = (bf16[4,128,128]{2,1,0:T(8,128)(2,1)S(1)}, bf16[4,128,128]{2,1,0:T(8,128)(2,1)S(1)}, u32[]{:S(2)}, u32[]{:S(2)}) collective-permute-start(bf16[4,128,128]{2,1,0:T(8,128)(2,1)S(1)} %get-tuple-element.61), channel_id=1, source_target_pairs={{0,96},{16,112},{32,0},{48,16},{64,32},{80,48},{96,64},{112,80},{1... | collective-permute-start | bytes 393224 | tf_op jit(solution)/shard_map/ppermute | solution.py:480
  84.2 4.4 %collective-permute-start.17 = (bf16[2,128,128]{2,1,0:T(8,128)(2,1)S(1)}, bf16[2,128,128]{2,1,0:T(8,128)(2,1)S(1)}, u32[]{:S(2)}, u32[]{:S(2)}) collective-permute-start(bf16[2,128,128]{2,1,0:T(8,128)(2,1)S(1)} %get-tuple-element.63), channel_id=1, source_target_pairs={{0,32},{16,48},{32,64},{48,80},{64,96},{80,112},{96,0},{112,16},{1... | collective-permute-start | bytes 196616 | tf_op jit(solution)/shard_map/ppermute | solution.py:480
  85.2 4.6 %collective-permute-start.18 = (bf16[2,128,128]{2,1,0:T(8,128)(2,1)S(1)}, bf16[2,128,128]{2,1,0:T(8,128)(2,1)S(1)}, u32[]{:S(2)}, u32[]{:S(2)}) collective-permute-start(bf16[2,128,128]{2,1,0:T(8,128)(2,1)S(1)} %get-tuple-element.64), channel_id=1, source_target_pairs={{0,64},{16,80},{32,96},{48,112},{64,0},{80,16},{96,32},{112,48},{1... | collective-permute-start | bytes 196616 | tf_op jit(solution)/shard_map/ppermute | solution.py:480
  87.4 3.6 %collective-permute-start.19 = (bf16[2,128,128]{2,1,0:T(8,128)(2,1)S(1)}, bf16[2,128,128]{2,1,0:T(8,128)(2,1)S(1)}, u32[]{:S(2)}, u32[]{:S(2)}) collective-permute-start(bf16[2,128,128]{2,1,0:T(8,128)(2,1)S(1)} %get-tuple-element.65), channel_id=1, source_target_pairs={{0,96},{16,112},{32,0},{48,16},{64,32},{80,48},{96,64},{112,80},{1... | collective-permute-start | bytes 196616 | tf_op jit(solution)/shard_map/ppermute | solution.py:480
  92.0 3.6 %collective-permute-start.20 = (bf16[8,128,128]{2,1,0:T(8,128)(2,1)S(1)}, bf16[8,128,128]{2,1,0:T(8,128)(2,1)S(1)}, u32[]{:S(2)}, u32[]{:S(2)}) collective-permute-start(bf16[8,128,128]{2,1,0:T(8,128)(2,1)S(1)} %get-tuple-element.67), channel_id=1, source_target_pairs={{0,16},{16,0},{32,48},{48,32},{64,80},{80,64},{96,112},{112,96},{1... | collective-permute-start | bytes 786440 | tf_op jit(solution)/shard_map/ppermute | solution.py:484

commit v7 on v6

--- a/solution.py
+++ b/solution.py
@@ -236,34 +236,31 @@
 
 def first_totals_kernel(own, *refs):
     arrivals = (refs[:2], refs[2:4])
-    outs = refs[-2 * SIDE + 1 :]
+    outs = refs[-SIDE:]
     h = own.shape[0] // (2 * SIDE)
     for half in range(2):
         for b in range(SIDE):
             t = own[pl.ds((half * SIDE + b) * h, h)].astype(f32)
             for a in arrivals[half]:
                 t = t + a[pl.ds(b * h, h)].astype(f32)
-            if b == 0:
-                outs[0][pl.ds(half * h, h)] = t.astype(bf16)
-            else:
-                outs[2 * b - 1 + half][...] = t.astype(bf16)
+            outs[b][pl.ds(half * h, h)] = t.astype(bf16)
 
 
 def first_totals(own, arrivals, order):
     rows = own.shape[0] // SIDE
     return pl.pallas_call(
         first_totals_kernel,
-        out_shape=cell_shapes([rows] + [rows // 2] * (2 * SIDE - 2)),
+        out_shape=[jax.ShapeDtypeStruct((rows, B, B), bf16)] * SIDE,
         in_specs=[VMEM] * 5 + [ANY] * len(order),
-        out_specs=[VMEM] * (2 * SIDE - 1),
+        out_specs=[VMEM] * SIDE,
         compiler_params=pltpu.CompilerParams(vmem_limit_bytes=9 * MIB),
         cost_estimate=pl.CostEstimate(flops=0, bytes_accessed=256 * 2 * B * B, transcendentals=0),
         name="first_totals",
     )(own, *arrivals, *order)
 
 
-def coupling_kernel(base_ref, diag_ref, own_ref, *refs):
-    parts = (refs[:2], refs[2:4])
+def coupling_kernel(base_ref, diag_ref, *refs):
+    parts = refs[:SIDE]
     new_ref, keep_ref, give_ref, new, held, sem = refs[4:]
     rows = base_ref.shape[0]
     half = rows // 2
@@ -274,9 +271,9 @@
 
         def finish(i, _, g=g):
             r = g * group + i
-            t = base_ref[r] - own_ref[r].astype(f32)
-            for p in parts[g * group // half]:
-                t = t - p[g * group % half + i].astype(f32)
+            t = base_ref[r]
+            for p in parts:
+                t = t - p[r].astype(f32)
             new[r] = t
             th, tl = split(t)
             dh, dl = split(diag_ref[r])
@@ -294,13 +291,13 @@
         c.wait()
 
 
-def coupling_and_step(base, diag, own, parts):
+def coupling_and_step(base, diag, parts):
     rows = base.shape[0]
     half = rows // 2
     return pl.pallas_call(
         coupling_kernel,
         out_shape=[jax.ShapeDtypeStruct((rows, B, B), f32)] + cell_shapes([half, half]),
-        in_specs=[VMEM] * 7,
+        in_specs=[VMEM] * (2 + SIDE),
         out_specs=[HBM, VMEM, VMEM],
         scratch_shapes=[
             pltpu.VMEM((rows, B, B), f32),
@@ -310,7 +307,7 @@
         compiler_params=pltpu.CompilerParams(vmem_limit_bytes=9 * MIB),
         cost_estimate=pl.CostEstimate(flops=rows * 6 * B**3, bytes_accessed=rows * 22 * B * B, transcendentals=0),
         name="coupling_and_step",
-    )(base, diag, own, *parts)
+    )(base, diag, *parts)
 
 
 def compose_kernel(chips, keep_ref, offset_ref, got_ref, got_offset_ref, *outs):
@@ -408,8 +405,7 @@
                 other = (got_ref[i], got_offset_ref[i])
                 (ma, oa), (mb, ob) = (mine, other) if first else (other, mine)
                 b = ob.astype(f32) + mm_nt(parts[k][j], mb)
-                high, low = split(b)
-                a = oa.astype(f32) + (mm_nt(high, ma) + mm_nt(low, ma))
+                a = oa.astype(f32) + mm_nt(b.astype(bf16), ma)
                 mine_ref[i] = a if first else b
                 other_ref[i] = (b if first else a).astype(bf16)
 
@@ -436,31 +432,56 @@
     )(keep, offsets, got, got_offsets, *parts)
 
 
-def gather_kernel(mine_ref, got_ref, out_ref, held, sem):
+def store_kernel(mine_ref, out_ref, sem):
     half = mine_ref.shape[0]
     core = lax.axis_index("section") % 2
-    own = pltpu.make_async_copy(mine_ref, out_ref.at[pl.ds(core * half, half)], sem.at[0])
-    own.start()
-    for i in range(half):
-        held[i] = got_ref[i].astype(f32)
-    rest = pltpu.make_async_copy(held, out_ref.at[pl.ds((1 - core) * half, half)], sem.at[1])
-    rest.start()
-    own.wait()
-    rest.wait()
-
-
-def gather_rows(mine, got):
+    copy = pltpu.make_async_copy(mine_ref, out_ref.at[pl.ds(core * half, half)], sem)
+    copy.start()
+    copy.wait()
+
+
+def store_rows(mine):
     half = mine.shape[0]
     return pl.pallas_call(
-        gather_kernel,
+        store_kernel,
         out_shape=jax.ShapeDtypeStruct((2 * half, B, B), f32),
-        in_specs=[VMEM, VMEM],
+        in_specs=[VMEM],
+        out_specs=HBM,
+        scratch_shapes=[pltpu.SemaphoreType.DMA],
+        compiler_params=pltpu.CompilerParams(vmem_limit_bytes=2 * MIB),
+        cost_estimate=pl.CostEstimate(flops=0, bytes_accessed=half * 8 * B * B, transcendentals=0),
+        name="store_rows",
+    )(mine)
+
+
+def add_kernel(got_ref, part_ref, out_ref, held, sem):
+    half = got_ref.shape[0]
+    group = half // 2
+    core = lax.axis_index("section") % 2
+    copies = []
+    for g in range(2):
+        for i in range(g * group, (g + 1) * group):
+            held[i] = got_ref[i].astype(f32)
+        to = out_ref.at[pl.ds((1 - core) * half + g * group, group)]
+        copies.append(pltpu.make_async_copy(held.at[pl.ds(g * group, group)], to, sem.at[g]))
+        copies[-1].start()
+    for c in copies:
+        c.wait()
+
+
+def add_rows(got, part):
+    half = got.shape[0]
+    return pl.pallas_call(
+        add_kernel,
+        out_shape=jax.ShapeDtypeStruct(part.shape, f32),
+        in_specs=[VMEM, HBM],
         out_specs=HBM,
         scratch_shapes=[pltpu.VMEM((half, B, B), f32), pltpu.SemaphoreType.DMA((2,))],
+        input_output_aliases={1: 0},
         compiler_params=pltpu.CompilerParams(vmem_limit_bytes=4 * MIB),
-        cost_estimate=pl.CostEstimate(flops=0, bytes_accessed=half * 14 * B * B, transcendentals=0),
-        name="gather_rows",
-    )(mine, got)
+        cost_estimate=pl.CostEstimate(flops=0, bytes_accessed=half * 6 * B * B, transcendentals=0),
+        name="add_rows",
+    )(got, part)
 
 
 def moved(x, stage, by, sections):
@@ -545,13 +566,9 @@
     got_offsets = partner(give_offsets, sections)
 
     arrivals = (joined_in[0], alone_in[1], alone_in[0], joined_in[1])
-    own, one_low, one_high, two_low, two_high, three_low, three_high = first_totals(near[4], arrivals, [base, got_offsets])
-    passed = [moved(two_low, 1, 1, sections), moved(two_high, 1, -1, sections)]
-    alone = [moved(three_low, 1, -1, sections), moved(one_high, 1, 1, sections)]
-    joined = [add(one_low, passed[0]), add(three_high, passed[1])]
-    joined = [moved(joined[0], 1, 1, sections), moved(joined[1], 1, -1, sections)]
-    parts = (joined[0], alone[0], alone[1], joined[1])
-    updated, keep, give = coupling_and_step(base, diag_inverse, own, parts)
+    totals = first_totals(near[4], arrivals, [base, got_offsets])
+    parts = [totals[0]] + [moved(totals[k], 1, k, sections) for k in (2, 1, 3)]
+    updated, keep, give = coupling_and_step(base, diag_inverse, parts)
     chips = sections // 2
     got = partner(give, sections)
     maps = compose(chips, keep, offsets, got, got_offsets)
@@ -559,7 +576,7 @@
     incoming = run_chains(maps)
     incoming = [incoming[0]] + [across(incoming[k], sections, k) for k in range(1, chips)]
     mine, other = expand(keep, offsets, got, got_offsets, incoming)
-    adjoint = gather_rows(mine, partner(other, sections))
+    adjoint = add_rows(partner(other, sections), store_rows(mine))
     return (updated, adjoint)
 
 

time: 96.9 us -> 95.2 us (0.982); the launches traced: 96.7 us -> 96.7 us
  starting transfers between devices: 38.6 us -> 35.7 us
  Pallas kernels: 20.3 us -> 22.9 us
    ppermute x12 -> x9, starting transfers between devices: 21.5 us -> 16.2 us  [moved(): return lax.ppermute(x, ('section', 'row'), pairs)]
    ppermute x6, starting transfers between devices: 9.2 us -> 14 us  [across(): lax.ppermute(x, 'section', [(i, (i + 2 * by) % sections) for i in range(s...]
    ppermute x12 -> x9, waiting for transfers between devices: 24.4 us -> 27.1 us  [moved(): return lax.ppermute(x, ('section', 'row'), pairs)]
    ppermute x3, starting transfers between devices: 7.89 us -> 5.56 us  [partner(): return lax.ppermute(x, 'section', [(i, i ^ 1) for i in range(sections)])]
    pallas_call x1, Pallas kernels: 3.58 us -> 5.46 us  [near_sums(): pl.pallas_call(functools.partial(near_kernel, first), out_shape=cell_shap...]
    ppermute x6, waiting for transfers between devices: 7.66 us -> 6.12 us  [across(): lax.ppermute(x, 'section', [(i, (i + 2 * by) % sections) for i in range(s...]
    pallas_call x2 -> x3, Pallas kernels: 1.74 us -> 2.37 us  [the longest x1 0.82 us: add_rows(): pl.pallas_call(add_kernel, out_shape=jax.ShapeDtypeStruct(part.shape, f32...]
  transfers between devices with their start and end apart: 21 -> 18, of which waited for: 15 -> 11; matrix products, arithmetic and copies ran while one was open for 1% -> 1% of each run, Pallas kernels for 11% -> 14%
where the time goes in v7:
time: 95.2 us; the launch traced here: 96.7 us
  starting transfers between devices  35.7 us (38%)
  waiting for transfers between devices  34.8 us (37%)
  Pallas kernels  22.9 us (24%)
  between operations  1.65 us (2%)
  other arithmetic  1.63 us (2%)
    ppermute x9, waiting for transfers between devices, moved(): return lax.ppermute(x, ('section', 'row'), pairs)  27.1 us
    ppermute x9, starting transfers between devices, moved(): return lax.ppermute(x, ('section', 'row'), pairs)  16.2 us
    ppermute x6, starting transfers between devices, across(): lax.ppermute(x, 'section', [(i, (i + 2 * by) % sections) for i in range(s...  14 us
    pallas_call x1, Pallas kernels, local_and_offset(): pl.pallas_call(local_kernel, out_shape=[jax.ShapeDtypeStruct((rows, B, B)...  7.38 us
    ppermute x6, waiting for transfers between devices, across(): lax.ppermute(x, 'section', [(i, (i + 2 * by) % sections) for i in range(s...  6.12 us
    ppermute x3, starting transfers between devices, partner(): return lax.ppermute(x, 'section', [(i, i ^ 1) for i in range(sections)])  5.56 us
    pallas_call x1, Pallas kernels, near_sums(): pl.pallas_call(functools.partial(near_kernel, first), out_shape=cell_shap...  5.46 us
    pallas_call x1, Pallas kernels, far_sums(): pl.pallas_call(functools.partial(far_kernel, first), out_shape=cell_shape...  4.68 us
  transfers between devices with their start and end apart: 18, of which 11 were waited for; matrix products, arithmetic and copies ran while one was open for 1% of the time, Pallas kernels for 14%

profile of v7, /device:TPU:1, one launch (start us, length us, event | category | flops | bytes accessed | tf_op | source)
XLA Modules:
  0.0 96.7 jit_solution(15030660734572452602)
XLA Ops:
  1.3 0.7 fusion.5.index_ref
  2.0 4.7 %far_sums.1 = (bf16[32,128,128]{2,1,0:T(8,128)(2,1)S(1)}, bf16[32,128,128]{2,1,0:T(8,128)(2,1)S(1)}, bf16[128,128,128]{2,1,0:T(8,128)(2,1)S(1)}, bf16[128,128,12...) custom-call(s32[128]{0:T(128)S(1)} %fusion.5.index_ref, bf16[4,128,128]{2,1,0:T(8,128)(2,1)} %table_ref.3, ...), custom_call_target="tpu_custom_call" | custom-call | flops 268435456 | bytes 18874368 | tf_op jit(solution)/shard_map/far_sums/pallas_call | solution.py:129
  6.7 4.6 %collective-permute-start.1 = (bf16[32,128,128]{2,1,0:T(8,128)(2,1)S(1)}, bf16[32,128,128]{2,1,0:T(8,128)(2,1)S(1)}, u32[]{:S(2)}, u32[]{:S(2)}) collective-permute-start(bf16[32,128,128]{2,1,0:T(8,128)(2,1)S(1)} %get-tuple-element.38), channel_id=1, source_target_pairs={{0,12},{1,13},{2,14},{3,15},{4,0},{5,1},{6,2},{7,3},{8,4},{9,5},{1... | collective-permute-start | bytes 3145736 | tf_op jit(solution)/shard_map/ppermute | solution.py:497
  11.4 0.0 collective-permute-start
  11.4 5.5 %near_sums.1 = (bf16[32,128,128]{2,1,0:T(8,128)(2,1)S(1)}, bf16[32,128,128]{2,1,0:T(8,128)(2,1)S(1)}, bf16[32,128,128]{2,1,0:T(8,128)(2,1)S(1)}, bf16[32,128,128...) custom-call(s32[128]{0:T(128)S(1)} %fusion.5.index_ref, bf16[4,128,128]{2,1,0:T(8,128)(2,1)S(1)} %get-tuple-element.32.table, ...), custom_call_target="tpu_custom_call" | custom-call | flops 805306368 | bytes 14680064 | tf_op jit(solution)/shard_map/near_sums/pallas_call | solution.py:156
  16.8 2.7 %collective-permute-start.3 = (bf16[32,128,128]{2,1,0:T(8,128)(2,1)S(1)}, bf16[32,128,128]{2,1,0:T(8,128)(2,1)S(1)}, u32[]{:S(2)}, u32[]{:S(2)}) collective-permute-start(bf16[32,128,128]{2,1,0:T(8,128)(2,1)S(1)} %get-tuple-element.41), channel_id=1, source_target_pairs={{0,12},{1,13},{2,14},{3,15},{4,0},{5,1},{6,2},{7,3},{8,4},{9,5},{1... | collective-permute-start | bytes 3145736 | tf_op jit(solution)/shard_map/ppermute | solution.py:497
  19.6 0.0 collective-permute-start.4
  19.6 3.5 %collective-permute-done.1 = bf16[32,128,128]{2,1,0:T(8,128)(2,1)S(1)} collective-permute-done((bf16[32,128,128]{2,1,0:T(8,128)(2,1)S(1)}, bf16[32,128,128]{2,1,0:T(8,128)(2,1)S(1)}, u32[]{:S(2)}, u32[]{:S(2)}) %collective-permute-start.1) | collective-permute-done | bytes 1048608 | tf_op jit(solution)/shard_map/ppermute | solution.py:497
  23.1 0.5 add_convert_fusion.refs_1_
  23.6 0.0 copy-start.3
  23.6 0.0 copy-start.4
  23.6 0.0 copy-start
  23.6 0.0 copy-start.1
  23.6 0.0 copy-start.2
  23.6 3.5 %collective-permute-start.5 = (bf16[32,128,128]{2,1,0:T(8,128)(2,1)S(1)}, bf16[32,128,128]{2,1,0:T(8,128)(2,1)S(1)}, u32[]{:S(2)}, u32[]{:S(2)}) collective-permute-start(bf16[32,128,128]{2,1,0:T(8,128)(2,1)S(1)} %add_convert_fusion.refs_1_), channel_id=1, source_target_pairs={{0,12},{1,13},{2,14},{3,15},{4,0},{5,1},{6,2},{7,3},{8,4},{9,5},{1... | collective-permute-start | bytes 3145736 | tf_op jit(solution)/shard_map/ppermute | solution.py:497
  27.1 0.5 add_convert_fusion.1.refs_0_
  27.6 0.1 collective-permute-start.2
  27.7 7.4 %local_and_offset.1 = (f32[16,128,128]{2,1,0:T(8,128)S(1)}, bf16[8,128,128]{2,1,0:T(8,128)(2,1)S(1)}, bf16[8,128,128]{2,1,0:T(8,128)(2,1)S(1)}) custom-call(s32[128]{0:T(128)S(1)} %shift-left_or_fusion.index_ref, bf16[4,128,128]{2,1,0:T(8,128)(2,1)} %table_ref.3, bf16[16,128,128]{2,1,0:T(8,128)(2,1)S(1)} %copy-done.2, bf16[128,128,128]{2,1,0:T(8,128)(2,1)} %left_ref.3, ...), custom_call_target="tpu_custom_call" | custom-call | flops 1073741824 | bytes 12582912 | tf_op jit(solution)/shard_map/local_and_offset/pallas_call | solution.py:215
  35.1 0.6 collective-permute-start.6
  35.7 2.0 %collective-permute-done.4.refs_2_ = bf16[32,128,128]{2,1,0:T(8,128)(2,1)S(1)} collective-permute-done((bf16[32,128,128]{2,1,0:T(8,128)(2,1)S(1)}, bf16[32,128,128]{2,1,0:T(8,128)(2,1)S(1)}, u32[]{:S(2)}, u32[]{:S(2)}) %collective-permute-start.4) | collective-permute-done | bytes 1048608 | tf_op jit(solution)/shard_map/ppermute | solution.py:497
  37.8 7.8 %collective-permute-done.5.refs_3_ = bf16[32,128,128]{2,1,0:T(8,128)(2,1)S(1)} collective-permute-done((bf16[32,128,128]{2,1,0:T(8,128)(2,1)S(1)}, bf16[32,128,128]{2,1,0:T(8,128)(2,1)S(1)}, u32[]{:S(2)}, u32[]{:S(2)}) %collective-permute-start.5) | collective-permute-done | bytes 1048608 | tf_op jit(solution)/shard_map/ppermute | solution.py:497
  45.6 3.4 %collective-permute-done.2.refs_0_ = bf16[32,128,128]{2,1,0:T(8,128)(2,1)S(1)} collective-permute-done((bf16[32,128,128]{2,1,0:T(8,128)(2,1)S(1)}, bf16[32,128,128]{2,1,0:T(8,128)(2,1)S(1)}, u32[]{:S(2)}, u32[]{:S(2)}) %collective-permute-start.2) | collective-permute-done | bytes 1048608 | tf_op jit(solution)/shard_map/ppermute | solution.py:497
  49.0 0.7 first_totals.1
  49.7 2.5 %collective-permute-start.7 = (bf16[16,128,128]{2,1,0:T(8,128)(2,1)S(1)}, bf16[16,128,128]{2,1,0:T(8,128)(2,1)S(1)}, u32[]{:S(2)}, u32[]{:S(2)}) collective-permute-start(bf16[16,128,128]{2,1,0:T(8,128)(2,1)S(1)} %get-tuple-element.45), channel_id=1, source_target_pairs={{0,2},{1,3},{2,0},{3,1},{4,6},{5,7},{6,4},{7,5},{8,10},{9,11},{10,... | collective-permute-start | bytes 1572872 | tf_op jit(solution)/shard_map/ppermute | solution.py:497
  52.3 0.3 collective-permute-start.8
  52.6 2.4 %collective-permute-start.9 = (bf16[16,128,128]{2,1,0:T(8,128)(2,1)S(1)}, bf16[16,128,128]{2,1,0:T(8,128)(2,1)S(1)}, u32[]{:S(2)}, u32[]{:S(2)}) collective-permute-start(bf16[16,128,128]{2,1,0:T(8,128)(2,1)S(1)} %get-tuple-element.47), channel_id=1, source_target_pairs={{0,3},{1,0},{2,1},{3,2},{4,7},{5,4},{6,5},{7,6},{8,11},{9,8},{10,9... | collective-permute-start | bytes 1572872 | tf_op jit(solution)/shard_map/ppermute | solution.py:497
  54.9 4.8 %collective-permute-done.7.refs_1_ = bf16[16,128,128]{2,1,0:T(8,128)(2,1)S(1)} collective-permute-done((bf16[16,128,128]{2,1,0:T(8,128)(2,1)S(1)}, bf16[16,128,128]{2,1,0:T(8,128)(2,1)S(1)}, u32[]{:S(2)}, u32[]{:S(2)}) %collective-permute-start.7) | collective-permute-done | bytes 524320 | tf_op jit(solution)/shard_map/ppermute | solution.py:497
  59.7 5.6 %collective-permute-done.8.refs_2_ = bf16[16,128,128]{2,1,0:T(8,128)(2,1)S(1)} collective-permute-done((bf16[16,128,128]{2,1,0:T(8,128)(2,1)S(1)}, bf16[16,128,128]{2,1,0:T(8,128)(2,1)S(1)}, u32[]{:S(2)}, u32[]{:S(2)}) %collective-permute-start.8) | collective-permute-done | bytes 524320 | tf_op jit(solution)/shard_map/ppermute | solution.py:497
  65.3 0.0 collective-permute-done.9.refs_3_
  65.3 1.6 %coupling_and_step.1 = (f32[16,128,128]{2,1,0:T(8,128)}, bf16[8,128,128]{2,1,0:T(8,128)(2,1)S(1)}, bf16[8,128,128]{2,1,0:T(8,128)(2,1)S(1)}) custom-call(f32[16,128,128]{2,1,0:T(8,128)S(1)} %get-tuple-element.39.refs_4_.base_ref, f32[16,128,128]{2,1,0:T(8,128)S(1)} %copy-done, bf16[16,128,128]{2,1,0:T(8,128)(2,1)S(1)} %get-tuple-element.44.refs_0_, ...), custom_call_target="tpu_custom_call" | custom-call | flops 201326592 | bytes 5767168 | tf_op jit(solution)/shard_map/coupling_and_step/pallas_call | solution.py:297
  66.9 2.9 %collective-permute-start.10 = (bf16[8,128,128]{2,1,0:T(8,128)(2,1)S(1)}, bf16[8,128,128]{2,1,0:T(8,128)(2,1)S(1)}, u32[]{:S(2)}, u32[]{:S(2)}) collective-permute-start(bf16[8,128,128]{2,1,0:T(8,128)(2,1)S(1)} %get-tuple-element.51), channel_id=1, source_target_pairs={{0,16},{16,0},{32,48},{48,32},{64,80},{80,64},{96,112},{112,96},{1... | collective-permute-start | bytes 786440 | tf_op jit(solution)/shard_map/ppermute | solution.py:505
  69.8 1.2 %collective-permute-done.10.got_ref = bf16[8,128,128]{2,1,0:T(8,128)(2,1)S(1)} collective-permute-done((bf16[8,128,128]{2,1,0:T(8,128)(2,1)S(1)}, bf16[8,128,128]{2,1,0:T(8,128)(2,1)S(1)}, u32[]{:S(2)}, u32[]{:S(2)}) %collective-permute-start.10) | collective-permute-done | bytes 262176 | tf_op jit(solution)/shard_map/ppermute | solution.py:505
  70.9 0.4 compose.1
  71.3 6.0 %collective-permute-start.11 = (bf16[4,128,128]{2,1,0:T(8,128)(2,1)S(1)}, bf16[4,128,128]{2,1,0:T(8,128)(2,1)S(1)}, u32[]{:S(2)}, u32[]{:S(2)}) collective-permute-start(bf16[4,128,128]{2,1,0:T(8,128)(2,1)S(1)} %get-tuple-element.53), channel_id=1, source_target_pairs={{0,32},{16,48},{32,64},{48,80},{64,96},{80,112},{96,0},{112,16},{1... | collective-permute-start | bytes 393224 | tf_op jit(solution)/shard_map/ppermute | solution.py:501
  77.3 0.0 collective-permute-start.12
  77.3 2.5 %collective-permute-start.13 = (bf16[4,128,128]{2,1,0:T(8,128)(2,1)S(1)}, bf16[4,128,128]{2,1,0:T(8,128)(2,1)S(1)}, u32[]{:S(2)}, u32[]{:S(2)}) collective-permute-start(bf16[4,128,128]{2,1,0:T(8,128)(2,1)S(1)} %get-tuple-element.55), channel_id=1, source_target_pairs={{0,96},{16,112},{32,0},{48,16},{64,32},{80,48},{96,64},{112,80},{1... | collective-permute-start | bytes 393224 | tf_op jit(solution)/shard_map/ppermute | solution.py:501
  79.8 3.2 %collective-permute-done.12.refs_2_ = bf16[4,128,128]{2,1,0:T(8,128)(2,1)S(1)} collective-permute-done((bf16[4,128,128]{2,1,0:T(8,128)(2,1)S(1)}, bf16[4,128,128]{2,1,0:T(8,128)(2,1)S(1)}, u32[]{:S(2)}, u32[]{:S(2)}) %collective-permute-start.12) | collective-permute-done | bytes 131104 | tf_op jit(solution)/shard_map/ppermute | solution.py:501
  83.0 0.6 collective-permute-done.13.refs_3_
  83.6 0.4 run_chains.1
  84.0 2.8 %collective-permute-start.14 = (bf16[2,128,128]{2,1,0:T(8,128)(2,1)S(1)}, bf16[2,128,128]{2,1,0:T(8,128)(2,1)S(1)}, u32[]{:S(2)}, u32[]{:S(2)}) collective-permute-start(bf16[2,128,128]{2,1,0:T(8,128)(2,1)S(1)} %get-tuple-element.57), channel_id=1, source_target_pairs={{0,32},{16,48},{32,64},{48,80},{64,96},{80,112},{96,0},{112,16},{1... | collective-permute-start | bytes 196616 | tf_op jit(solution)/shard_map/ppermute | solution.py:501
  86.8 0.9 collective-permute-start.15
  87.7 1.8 %collective-permute-start.16 = (bf16[2,128,128]{2,1,0:T(8,128)(2,1)S(1)}, bf16[2,128,128]{2,1,0:T(8,128)(2,1)S(1)}, u32[]{:S(2)}, u32[]{:S(2)}) collective-permute-start(bf16[2,128,128]{2,1,0:T(8,128)(2,1)S(1)} %get-tuple-element.59), channel_id=1, source_target_pairs={{0,96},{16,112},{32,0},{48,16},{64,32},{80,48},{96,64},{112,80},{1... | collective-permute-start | bytes 196616 | tf_op jit(solution)/shard_map/ppermute | solution.py:501
  89.5 2.3 %collective-permute-done.15.refs_2_ = bf16[2,128,128]{2,1,0:T(8,128)(2,1)S(1)} collective-permute-done((bf16[2,128,128]{2,1,0:T(8,128)(2,1)S(1)}, bf16[2,128,128]{2,1,0:T(8,128)(2,1)S(1)}, u32[]{:S(2)}, u32[]{:S(2)}) %collective-permute-start.15) | collective-permute-done | bytes 65568 | tf_op jit(solution)/shard_map/ppermute | solution.py:501
  91.9 0.5 expand.1
  92.4 2.1 %collective-permute-start.17 = (bf16[8,128,128]{2,1,0:T(8,128)(2,1)S(1)}, bf16[8,128,128]{2,1,0:T(8,128)(2,1)S(1)}, u32[]{:S(2)}, u32[]{:S(2)}) collective-permute-start(bf16[8,128,128]{2,1,0:T(8,128)(2,1)S(1)} %get-tuple-element.60), channel_id=1, source_target_pairs={{0,16},{16,0},{32,48},{48,32},{64,80},{80,64},{96,112},{112,96},{1... | collective-permute-start | bytes 786440 | tf_op jit(solution)/shard_map/ppermute | solution.py:505
  94.5 0.8 store_rows.1.part_ref
  95.3 0.4 collective-permute-done.17.got_ref
  95.7 0.8 add_rows.1
  (12 shorter events, 0.0 us)
Async XLA Ops:
  6.7 16.4 %collective-permute-start.1 = (bf16[32,128,128]{2,1,0:T(8,128)(2,1)S(1)}, bf16[32,128,128]{2,1,0:T(8,128)(2,1)S(1)}, u32[]{:S(2)}, u32[]{:S(2)}) collective-permute-start(bf16[32,128,128]{2,1,0:T(8,128)(2,1)S(1)} %get-tuple-element.38), channel_id=1, source_target_pairs={{0,12},{1,13},{2,14},{3,15},{4,0},{5,1},{6,2},{7,3},{8,4},{9,5},{1... | collective-permute-start | bytes 3145736 | tf_op jit(solution)/shard_map/ppermute | solution.py:497
  11.4 15.8 %collective-permute-start = (bf16[32,128,128]{2,1,0:T(8,128)(2,1)S(1)}, bf16[32,128,128]{2,1,0:T(8,128)(2,1)S(1)}, u32[]{:S(2)}, u32[]{:S(2)}) collective-permute-start(bf16[32,128,128]{2,1,0:T(8,128)(2,1)S(1)} %get-tuple-element.36), channel_id=1, source_target_pairs={{0,4},{1,5},{2,6},{3,7},{4,8},{5,9},{6,10},{7,11},{8,12},{9,13},{1... | collective-permute-start | bytes 3145736 | tf_op jit(solution)/shard_map/ppermute | solution.py:497
  16.8 18.9 %collective-permute-start.3 = (bf16[32,128,128]{2,1,0:T(8,128)(2,1)S(1)}, bf16[32,128,128]{2,1,0:T(8,128)(2,1)S(1)}, u32[]{:S(2)}, u32[]{:S(2)}) collective-permute-start(bf16[32,128,128]{2,1,0:T(8,128)(2,1)S(1)} %get-tuple-element.41), channel_id=1, source_target_pairs={{0,12},{1,13},{2,14},{3,15},{4,0},{5,1},{6,2},{7,3},{8,4},{9,5},{1... | collective-permute-start | bytes 3145736 | tf_op jit(solution)/shard_map/ppermute | solution.py:497
  19.6 18.2 %collective-permute-start.4 = (bf16[32,128,128]{2,1,0:T(8,128)(2,1)S(1)}, bf16[32,128,128]{2,1,0:T(8,128)(2,1)S(1)}, u32[]{:S(2)}, u32[]{:S(2)}) collective-permute-start(bf16[32,128,128]{2,1,0:T(8,128)(2,1)S(1)} %get-tuple-element.42), channel_id=1, source_target_pairs={{0,4},{1,5},{2,6},{3,7},{4,8},{5,9},{6,10},{7,11},{8,12},{9,13},{1... | collective-permute-start | bytes 3145736 | tf_op jit(solution)/shard_map/ppermute | solution.py:497
  23.6 4.1 %copy-start.3 = (s32[128]{0:T(128)S(1)}, s32[128]{0:T(128)}, u32[]{:S(2)}) copy-start(s32[128]{0:T(128)} %param.26) | copy-start | bytes 1540
  23.6 4.1 %copy-start.4 = (s32[128]{0:T(128)S(1)}, s32[128]{0:T(128)}, u32[]{:S(2)}) copy-start(s32[128]{0:T(128)} %param.25) | copy-start | bytes 1540
  23.6 4.1 %copy-start = (f32[16,128,128]{2,1,0:T(8,128)S(1)}, f32[16,128,128]{2,1,0:T(8,128)}, u32[]{:S(2)}) copy-start(f32[16,128,128]{2,1,0:T(8,128)} %diag_ref.3) | copy-start | bytes 3145732
  23.6 4.1 %copy-start.1 = (f32[16,128,128]{2,1,0:T(8,128)S(1)}, f32[16,128,128]{2,1,0:T(8,128)}, u32[]{:S(2)}) copy-start(f32[16,128,128]{2,1,0:T(8,128)} %seed_ref.1) | copy-start | bytes 3145732
  23.6 4.1 %copy-start.2 = (bf16[16,128,128]{2,1,0:T(8,128)(2,1)S(1)}, bf16[16,128,128]{2,1,0:T(8,128)(2,1)}, u32[]{:S(2)}) copy-start(bf16[16,128,128]{2,1,0:T(8,128)(2,1)} %coupling_ref.1) | copy-start | bytes 1572868
  23.6 21.9 %collective-permute-start.5 = (bf16[32,128,128]{2,1,0:T(8,128)(2,1)S(1)}, bf16[32,128,128]{2,1,0:T(8,128)(2,1)S(1)}, u32[]{:S(2)}, u32[]{:S(2)}) collective-permute-start(bf16[32,128,128]{2,1,0:T(8,128)(2,1)S(1)} %add_convert_fusion.refs_1_), channel_id=1, source_target_pairs={{0,12},{1,13},{2,14},{3,15},{4,0},{5,1},{6,2},{7,3},{8,4},{9,5},{1... | collective-permute-start | bytes 3145736 | tf_op jit(solution)/shard_map/ppermute | solution.py:497
  27.6 21.4 %collective-permute-start.2 = (bf16[32,128,128]{2,1,0:T(8,128)(2,1)S(1)}, bf16[32,128,128]{2,1,0:T(8,128)(2,1)S(1)}, u32[]{:S(2)}, u32[]{:S(2)}) collective-permute-start(bf16[32,128,128]{2,1,0:T(8,128)(2,1)S(1)} %add_convert_fusion.1.refs_0_), channel_id=1, source_target_pairs={{0,4},{1,5},{2,6},{3,7},{4,8},{5,9},{6,10},{7,11},{8,12},{9,13},{1... | collective-permute-start | bytes 3145736 | tf_op jit(solution)/shard_map/ppermute | solution.py:497
  35.1 2.6 %collective-permute-start.6 = (bf16[8,128,128]{2,1,0:T(8,128)(2,1)S(1)}, bf16[8,128,128]{2,1,0:T(8,128)(2,1)S(1)}, u32[]{:S(2)}, u32[]{:S(2)}) collective-permute-start(bf16[8,128,128]{2,1,0:T(8,128)(2,1)S(1)} %get-tuple-element.43), channel_id=1, source_target_pairs={{0,16},{16,0},{32,48},{48,32},{64,80},{80,64},{96,112},{112,96},{1... | collective-permute-start | bytes 786440 | tf_op jit(solution)/shard_map/ppermute | solution.py:505
  49.7 10.0 %collective-permute-start.7 = (bf16[16,128,128]{2,1,0:T(8,128)(2,1)S(1)}, bf16[16,128,128]{2,1,0:T(8,128)(2,1)S(1)}, u32[]{:S(2)}, u32[]{:S(2)}) collective-permute-start(bf16[16,128,128]{2,1,0:T(8,128)(2,1)S(1)} %get-tuple-element.45), channel_id=1, source_target_pairs={{0,2},{1,3},{2,0},{3,1},{4,6},{5,7},{6,4},{7,5},{8,10},{9,11},{10,... | collective-permute-start | bytes 1572872 | tf_op jit(solution)/shard_map/ppermute | solution.py:497
  52.3 13.0 %collective-permute-start.8 = (bf16[16,128,128]{2,1,0:T(8,128)(2,1)S(1)}, bf16[16,128,128]{2,1,0:T(8,128)(2,1)S(1)}, u32[]{:S(2)}, u32[]{:S(2)}) collective-permute-start(bf16[16,128,128]{2,1,0:T(8,128)(2,1)S(1)} %get-tuple-element.46), channel_id=1, source_target_pairs={{0,1},{1,2},{2,3},{3,0},{4,5},{5,6},{6,7},{7,4},{8,9},{9,10},{10,1... | collective-permute-start | bytes 1572872 | tf_op jit(solution)/shard_map/ppermute | solution.py:497
  52.6 12.7 %collective-permute-start.9 = (bf16[16,128,128]{2,1,0:T(8,128)(2,1)S(1)}, bf16[16,128,128]{2,1,0:T(8,128)(2,1)S(1)}, u32[]{:S(2)}, u32[]{:S(2)}) collective-permute-start(bf16[16,128,128]{2,1,0:T(8,128)(2,1)S(1)} %get-tuple-element.47), channel_id=1, source_target_pairs={{0,3},{1,0},{2,1},{3,2},{4,7},{5,4},{6,5},{7,6},{8,11},{9,8},{10,9... | collective-permute-start | bytes 1572872 | tf_op jit(solution)/shard_map/ppermute | solution.py:497
  66.9 4.0 %collective-permute-start.10 = (bf16[8,128,128]{2,1,0:T(8,128)(2,1)S(1)}, bf16[8,128,128]{2,1,0:T(8,128)(2,1)S(1)}, u32[]{:S(2)}, u32[]{:S(2)}) collective-permute-start(bf16[8,128,128]{2,1,0:T(8,128)(2,1)S(1)} %get-tuple-element.51), channel_id=1, source_target_pairs={{0,16},{16,0},{32,48},{48,32},{64,80},{80,64},{96,112},{112,96},{1... | collective-permute-start | bytes 786440 | tf_op jit(solution)/shard_map/ppermute | solution.py:505
  71.3 8.5 %collective-permute-start.11 = (bf16[4,128,128]{2,1,0:T(8,128)(2,1)S(1)}, bf16[4,128,128]{2,1,0:T(8,128)(2,1)S(1)}, u32[]{:S(2)}, u32[]{:S(2)}) collective-permute-start(bf16[4,128,128]{2,1,0:T(8,128)(2,1)S(1)} %get-tuple-element.53), channel_id=1, source_target_pairs={{0,32},{16,48},{32,64},{48,80},{64,96},{80,112},{96,0},{112,16},{1... | collective-permute-start | bytes 393224 | tf_op jit(solution)/shard_map/ppermute | solution.py:501
  77.3 5.7 %collective-permute-start.12 = (bf16[4,128,128]{2,1,0:T(8,128)(2,1)S(1)}, bf16[4,128,128]{2,1,0:T(8,128)(2,1)S(1)}, u32[]{:S(2)}, u32[]{:S(2)}) collective-permute-start(bf16[4,128,128]{2,1,0:T(8,128)(2,1)S(1)} %get-tuple-element.54), channel_id=1, source_target_pairs={{0,64},{16,80},{32,96},{48,112},{64,0},{80,16},{96,32},{112,48},{1... | collective-permute-start | bytes 393224 | tf_op jit(solution)/shard_map/ppermute | solution.py:501
  77.3 6.3 %collective-permute-start.13 = (bf16[4,128,128]{2,1,0:T(8,128)(2,1)S(1)}, bf16[4,128,128]{2,1,0:T(8,128)(2,1)S(1)}, u32[]{:S(2)}, u32[]{:S(2)}) collective-permute-start(bf16[4,128,128]{2,1,0:T(8,128)(2,1)S(1)} %get-tuple-element.55), channel_id=1, source_target_pairs={{0,96},{16,112},{32,0},{48,16},{64,32},{80,48},{96,64},{112,80},{1... | collective-permute-start | bytes 393224 | tf_op jit(solution)/shard_map/ppermute | solution.py:501
  84.0 5.5 %collective-permute-start.14 = (bf16[2,128,128]{2,1,0:T(8,128)(2,1)S(1)}, bf16[2,128,128]{2,1,0:T(8,128)(2,1)S(1)}, u32[]{:S(2)}, u32[]{:S(2)}) collective-permute-start(bf16[2,128,128]{2,1,0:T(8,128)(2,1)S(1)} %get-tuple-element.57), channel_id=1, source_target_pairs={{0,32},{16,48},{32,64},{48,80},{64,96},{80,112},{96,0},{112,16},{1... | collective-permute-start | bytes 196616 | tf_op jit(solution)/shard_map/ppermute | solution.py:501
  86.8 5.1 %collective-permute-start.15 = (bf16[2,128,128]{2,1,0:T(8,128)(2,1)S(1)}, bf16[2,128,128]{2,1,0:T(8,128)(2,1)S(1)}, u32[]{:S(2)}, u32[]{:S(2)}) collective-permute-start(bf16[2,128,128]{2,1,0:T(8,128)(2,1)S(1)} %get-tuple-element.58), channel_id=1, source_target_pairs={{0,64},{16,80},{32,96},{48,112},{64,0},{80,16},{96,32},{112,48},{1... | collective-permute-start | bytes 196616 | tf_op jit(solution)/shard_map/ppermute | solution.py:501
  87.7 4.1 %collective-permute-start.16 = (bf16[2,128,128]{2,1,0:T(8,128)(2,1)S(1)}, bf16[2,128,128]{2,1,0:T(8,128)(2,1)S(1)}, u32[]{:S(2)}, u32[]{:S(2)}) collective-permute-start(bf16[2,128,128]{2,1,0:T(8,128)(2,1)S(1)} %get-tuple-element.59), channel_id=1, source_target_pairs={{0,96},{16,112},{32,0},{48,16},{64,32},{80,48},{96,64},{112,80},{1... | collective-permute-start | bytes 196616 | tf_op jit(solution)/shard_map/ppermute | solution.py:501
  92.4 3.3 %collective-permute-start.17 = (bf16[8,128,128]{2,1,0:T(8,128)(2,1)S(1)}, bf16[8,128,128]{2,1,0:T(8,128)(2,1)S(1)}, u32[]{:S(2)}, u32[]{:S(2)}) collective-permute-start(bf16[8,128,128]{2,1,0:T(8,128)(2,1)S(1)} %get-tuple-element.60), channel_id=1, source_target_pairs={{0,16},{16,0},{32,48},{48,32},{64,80},{80,64},{96,112},{112,96},{1... | collective-permute-start | bytes 786440 | tf_op jit(solution)/shard_map/ppermute | solution.py:505
